TPU v7x, 32 devices: a whole 2x2x4 slice. The times are simulated.
32 devices in a mesh: tile: 2 (over y), pts: 4 (over z), head: 4 (over x, core).
Axes of the slice: x: 2, y: 2, z: 4, core: 2. Of those that a mesh axis runs over, the one named last changes fastest.
Arguments:
- z_feat: bfloat16 [24544, 512], P(('tile', 'pts')), parts along dimension 0, may hold values from -12 to 12
- shard_count: int32 [8], P(('tile', 'pts')), parts along dimension 0, may hold values from 1028 to 3068, as said below
- hilbert_rank: int32 [24544], P(('tile', 'pts')), parts along dimension 0, may hold values from 0 to 8191, as said below
- z_slot: int32 [16384], P(('tile', 'pts')), parts along dimension 0, may hold values from 0 to 12271, as said below
- ln1_gain: float32 [512], replicated, may hold values from 0.25 to 1.75
- ln1_bias: float32 [512], replicated, may hold values from -1.5 to 1.5
- w_qkv: bfloat16 [3, 512, 512], P(None, None, 'head'), may hold values from -16 to 16
- w_out: bfloat16 [512, 512], P(None, 'head'), may hold values from -0.25 to 0.25
- b_out: float32 [512], P('head'), may hold values from -2.5 to 2.5
- ln2_gain: float32 [512], replicated, may hold values from 0.25 to 1.75
- ln2_bias: float32 [512], replicated, may hold values from -1.5 to 1.5
- w_up: bfloat16 [512, 2048], P(None, 'head'), may hold values from -0.25 to 0.25
- b_up: float32 [2048], P('head'), may hold values from -2.5 to 2.5
- w_down: bfloat16 [2048, 512], P('head'), may hold values from -0.125 to 0.125
- b_down: float32 [512], P('head'), may hold values from -2.5 to 2.5
Outputs:
- z_out: bfloat16 [24544, 512], P(('tile', 'pts'), 'head'), parts along dimension 0
There are 2 independent parts, one for each index of `tile`. A program takes and returns all parts, laid end to end along the dimension named above; an argument that names none is the same for every part. Nothing has to cross between parts.
Inputs may be any that keep to these rules, and one draw needn't show every extreme that they name: `shard_count`: the number of points of z-order shard s, held in the first that many of its 3068 slots; the counts sum to 8192; some shard holds 3068 points. `hilbert_rank`: on occupied slots, a one to one map onto the 8192 Hilbert positions; empty slots hold 0; of the points of one z-order shard at most 1022 lie among the 2048 Hilbert positions of one index of pts, and some shard and index reach 1022. `z_slot`: the inverse of hilbert_rank: for Hilbert position h, the occupied slot whose hilbert_rank is h.
All inputs are finite; a program needn't handle non-finite values.
Results may differ from a plain program's by a relative error of at most 0.013.
Values may be sent and summed in bfloat16 or wider, within the bound.
No kernel may reach another device: no remote copies, remote signals or barrier semaphores. Data moves between devices by JAX's collectives and lax.ppermute only.
A program may use at most 64 MiB of HBM per device.

v0:
```python
import functools
import math

import jax
import jax.numpy as jnp
from jax import lax
from jax.experimental import pallas as pl
from jax.experimental.pallas import tpu as pltpu
from jax.sharding import PartitionSpec as P

PATCH = 1024
HEAD_DIM = 16
LANES = 128
ROW_STEP = 64
TILE = 512
DIRECT = 8
F32 = jnp.float32
BF = jnp.bfloat16
I32 = jnp.int32
SMEM = pl.BlockSpec(memory_space=pltpu.SMEM)
VMEM = pl.BlockSpec(memory_space=pltpu.VMEM)
ANY = pl.BlockSpec(memory_space=pl.ANY)


def dot(lhs, rhs, dims=(1, 0)):
    return lax.dot_general(
        lhs, rhs, (((dims[0],), (dims[1],)), ((), ())), preferred_element_type=F32
    )


def round_up(value, unit):
    return (value + unit - 1) // unit * unit


def grant(mib):
    return pltpu.CompilerParams(vmem_limit_bytes=mib * 2 ** 20)


def convert_rows(source, source_at, target, target_at, rows):
    step = math.gcd(rows, 128)

    def one(i, carry):
        at = pl.multiple_of(i * step, step)
        target[pl.ds(target_at + at, step), :] = source[pl.ds(source_at + at, step), :].astype(
            target.dtype
        )
        return carry

    lax.fori_loop(0, rows // step, one, 0)


def pack_kernel(
    shards, cap, rows_here, columns_at, held, rank, z_feat, *refs
):
    sends = refs[:shards]
    place_out = refs[shards]
    place, place_smem, ranks_full, narrow, wide, packed, sems = refs[shards + 1 :]
    here, member, count = lax.axis_index("pts"), lax.axis_index("head"), held[0]
    slots = place.shape[1]
    zone_rows, width = narrow.shape
    if columns_at:
        column = pl.multiple_of(member * width, width)
        source = z_feat.at[:, pl.ds(column, width)]
    else:
        source = z_feat
    feature_copy = pltpu.make_async_copy(source, narrow, sems.at[0])
    feature_copy.start()

    grid_rows = shards * rows_here // LANES
    block = rows_here // LANES
    ranks_full[:, :zone_rows] = rank[...]
    ranks = ranks_full[...]
    occupied = lax.broadcasted_iota(I32, (1, slots), 1) < count
    major = jnp.where(occupied, ranks // LANES, -1)
    minor = ranks % LANES
    hot_major = (lax.broadcasted_iota(I32, (grid_rows, slots), 0) == major).astype(BF)
    hot_minor = (lax.broadcasted_iota(I32, (LANES, slots), 0) == minor).astype(BF)
    members = dot(hot_minor, hot_major, (1, 1)).astype(BF)
    minor_r = lax.broadcasted_iota(I32, (LANES, LANES), 0)
    minor_c = lax.broadcasted_iota(I32, (LANES, LANES), 1)
    below = (minor_c < minor_r).astype(BF)
    major_r = lax.broadcasted_iota(I32, (grid_rows, grid_rows), 0)
    major_c = lax.broadcasted_iota(I32, (grid_rows, grid_rows), 1)
    earlier = ((major_r < major_c) & (major_r // block == major_c // block)).astype(BF)
    row_wise = dot(members, earlier)
    counts = dot(below, members) + dot(jnp.ones((LANES, LANES), BF), row_wise.astype(BF))
    high = jnp.floor(counts * (1.0 / 32.0))
    low = counts - high * 32.0
    spread = dot(high.astype(BF), hot_major) * 32.0 + dot(low.astype(BF), hot_major)
    found = jnp.sum(jnp.where(hot_minor > 0, spread, 0.0), axis=0, keepdims=True)
    target = ranks // rows_here
    place[...] = jnp.where(occupied, target * cap + found.astype(I32), shards * cap)
    to_smem = pltpu.make_async_copy(place, place_smem, sems.at[1])
    to_smem.start()
    to_out = pltpu.make_async_copy(place, place_out, sems.at[2])
    to_out.start()
    feature_copy.wait()
    whole_rows = zone_rows // LANES * LANES
    convert_rows(narrow, 0, wide, 0, whole_rows)
    if whole_rows < zone_rows:
        wide[pl.ds(whole_rows, zone_rows - whole_rows), :] = narrow[
            pl.ds(whole_rows, zone_rows - whole_rows), :
        ].astype(F32)
    to_smem.wait()

    def place_rows(i, carry):
        base = pl.multiple_of(i * ROW_STEP, ROW_STEP)
        for k in range(ROW_STEP):
            packed[pl.ds(place_smem[0, base + k], 1), :] = wide[pl.ds(base + k, 1), :]
        return carry

    lax.fori_loop(0, (count + ROW_STEP - 1) // ROW_STEP, place_rows, 0)
    for k in range(shards):
        at = pl.multiple_of(lax.rem(here + k, shards) * cap, cap)
        convert_rows(packed, at, sends[k], 0, cap)
    to_out.wait()


def pack(held, rank, z_feat, columns_at, width, shards, cap, rows_here):
    zone_rows = z_feat.shape[0]
    slots = round_up(zone_rows, LANES)
    return pl.pallas_call(
        functools.partial(pack_kernel, shards, cap, rows_here, columns_at),
        out_shape=[jax.ShapeDtypeStruct((cap, width), BF)] * shards
        + [jax.ShapeDtypeStruct((1, slots), I32)],
        in_specs=[SMEM, VMEM, ANY],
        out_specs=[VMEM] * shards + [ANY],
        scratch_shapes=[
            pltpu.VMEM((1, slots), I32),
            pltpu.SMEM((1, slots), I32),
            pltpu.VMEM((1, slots), I32),
            pltpu.VMEM((zone_rows, width), BF),
            pltpu.VMEM((slots, width), F32),
            pltpu.VMEM((shards * cap + 8, width), F32),
            pltpu.SemaphoreType.DMA((3,)),
        ],
        name="pack",
    )(held, rank, z_feat)


def move_segment(source, source_at, target, target_at, length):
    def one(i, carry):
        for k in range(4):
            target[pl.ds(target_at + i * 32 + k * 8, 8), :] = source[
                pl.ds(source_at + i * 32 + k * 8, 8), :
            ]
        return carry

    lax.fori_loop(0, (length + 31) // 32, one, 0)


def segment_starts(pieces, patches, shards, cap):
    packed_at, patch_at = {}, {}
    for s in range(shards):
        at = s * cap
        for p in range(patches):
            packed_at[p, s] = at
            at = at + pieces[p, s]
    for p in range(patches):
        at = p * PATCH
        for s in range(shards):
            patch_at[p, s] = at
            at = at + pieces[p, s]
    return packed_at, patch_at


def compact_kernel(shards, patches, group, cap, pieces, *refs):
    blocks = refs[:shards]
    outs = refs[shards : shards + patches]
    wide, patch_rows = refs[shards + patches :]
    here, member = lax.axis_index("pts"), lax.axis_index("head")
    for k in range(shards):
        at = pl.multiple_of(lax.rem(here - k + shards, shards) * cap, cap)
        convert_rows(blocks[k], 0, wide, at, cap)
    packed_at, patch_at = segment_starts(pieces, patches, shards, cap)
    for p in range(patches):
        for s in range(shards):
            move_segment(wide, packed_at[p, s], patch_rows, patch_at[p, s], pieces[p, s])
    own_group = member // group
    for k in range(patches):
        at = pl.multiple_of(lax.rem(own_group + k, patches) * PATCH, PATCH)
        convert_rows(patch_rows, at, outs[k], 0, PATCH)


def compact(pieces, blocks, patches, group):
    shards = len(blocks)
    cap, width = blocks[0].shape
    return pl.pallas_call(
        functools.partial(compact_kernel, shards, patches, group, cap),
        out_shape=[jax.ShapeDtypeStruct((PATCH, width), BF)] * patches,
        in_specs=[SMEM] + [VMEM] * shards,
        out_specs=[VMEM] * patches,
        scratch_shapes=[
            pltpu.VMEM((shards * cap + 64, width), F32),
            pltpu.VMEM((patches * PATCH + 64, width), F32),
        ],
        compiler_params=grant(12),
        name="compact",
    )(pieces, *blocks)


def spread_kernel(shards, patches, members, cap, pieces, *refs):
    blocks = refs[:members]
    sends = refs[members : members + shards]
    patch_rows, wide = refs[members + shards :]
    here, member = lax.axis_index("pts"), lax.axis_index("head")
    part_rows = blocks[0].shape[0]
    for k in range(members):
        at = pl.multiple_of(lax.rem(member - k + members, members) * part_rows, part_rows)
        convert_rows(blocks[k], 0, patch_rows, at, part_rows)
    packed_at, patch_at = segment_starts(pieces, patches, shards, cap)
    for s in range(shards):
        for p in range(patches):
            move_segment(patch_rows, patch_at[p, s], wide, packed_at[p, s], pieces[p, s])
    for k in range(shards):
        at = pl.multiple_of(lax.rem(here + k, shards) * cap, cap)
        convert_rows(wide, at, sends[k], 0, cap)


def spread(pieces, blocks, patches, shards, cap):
    members = len(blocks)
    _, width = blocks[0].shape
    return pl.pallas_call(
        functools.partial(spread_kernel, shards, patches, members, cap),
        out_shape=[jax.ShapeDtypeStruct((cap, width), BF)] * shards,
        in_specs=[SMEM] + [VMEM] * members,
        out_specs=[VMEM] * shards,
        scratch_shapes=[
            pltpu.VMEM((patches * PATCH + 64, width), F32),
            pltpu.VMEM((shards * cap + 64, width), F32),
        ],
        compiler_params=grant(12),
        name="spread",
    )(pieces, *blocks)


def unpack_kernel(shards, cap, held, place, *refs):
    blocks = refs[:shards]
    out = refs[shards]
    wide, picked = refs[shards + 1 :]
    here, count = lax.axis_index("pts"), held[0]
    zone_rows, width = out.shape
    for k in range(shards):
        at = pl.multiple_of(lax.rem(here - k + shards, shards) * cap, cap)
        convert_rows(blocks[k], 0, wide, at, cap)

    def pick_rows(i, carry):
        base = pl.multiple_of(i * ROW_STEP, ROW_STEP)
        for k in range(ROW_STEP):
            picked[pl.ds(base + k, 1), :] = wide[pl.ds(place[0, base + k], 1), :]
        return carry

    lax.fori_loop(0, (count + ROW_STEP - 1) // ROW_STEP, pick_rows, 0)

    def masked(at, rows):
        slot = at + lax.broadcasted_iota(I32, (rows, width), 0)
        out[pl.ds(at, rows), :] = jnp.where(slot < count, picked[pl.ds(at, rows), :], 0.0).astype(
            BF
        )

    def one(i, carry):
        masked(pl.multiple_of(i * LANES, LANES), LANES)
        return carry

    whole_rows = zone_rows // LANES * LANES
    lax.fori_loop(0, whole_rows // LANES, one, 0)
    if whole_rows < zone_rows:
        masked(whole_rows, zone_rows - whole_rows)


def unpack(held, place, blocks, zone_rows):
    shards = len(blocks)
    cap, width = blocks[0].shape
    slots = place.shape[1]
    return pl.pallas_call(
        functools.partial(unpack_kernel, shards, cap),
        out_shape=jax.ShapeDtypeStruct((zone_rows, width), BF),
        in_specs=[SMEM, SMEM] + [VMEM] * shards,
        out_specs=VMEM,
        scratch_shapes=[
            pltpu.VMEM((shards * cap + 8, width), F32),
            pltpu.VMEM((slots, width), F32),
        ],
        compiler_params=grant(14),
        name="unpack",
    )(held, place, *blocks)


def row_stats(parts, width):
    total = jnp.sum(sum(parts[1:], parts[0]), axis=1, keepdims=True)
    squares = jnp.sum(
        sum((x * x for x in parts[1:]), parts[0] * parts[0]), axis=1, keepdims=True
    )
    mean = total / width
    var = squares / width - mean * mean
    return mean, lax.rsqrt(var + 1e-05)


def block_places(blocks, patches, group):
    if blocks == patches * group:
        return arrival_order(patches, group)
    return list(range(blocks))


def place_of(places, index):
    found = places[0]
    for k in range(1, len(places)):
        found = jnp.where(index == k, places[k], found)
    return found


def attend_kernel(blocks, patches, group, tile, params, *refs):
    feats = refs[:blocks]
    weights = refs[blocks : 2 * blocks]
    out, kept = refs[2 * blocks : 2 * blocks + 2]
    normed, keys, values, query, even, odd = refs[2 * blocks + 2 :]
    rows = feats[0].shape[0]
    width = blocks * LANES
    queries = query.shape[1]
    places = block_places(blocks, patches, group)
    part = lax.rem(lax.axis_index("head"), group)
    first = pl.multiple_of(part * queries, queries)

    def norm(i, carry):
        at = pl.ds(pl.multiple_of(i * 128, 128), 128)
        parts = [feats[b][at, :].astype(F32) for b in range(blocks)]
        mean, scale = row_stats(parts, width)
        for b in range(blocks):
            cols = pl.ds(pl.multiple_of(places[b] * LANES, LANES), LANES)
            normed[at, cols] = (
                (parts[b] - mean) * scale * params[0:1, cols] + params[1:2, cols]
            ).astype(BF)
        return carry

    lax.fori_loop(0, rows // 128, norm, 0, unroll=2)
    for b in range(blocks):
        kept[places[b]] = feats[b][pl.ds(first, queries), :]
    lane = lax.broadcasted_iota(I32, (1, LANES), 1)
    score_scale = HEAD_DIM ** (-0.5) * math.log2(math.e)
    pair_of = 2 if blocks % 2 == 0 else 1
    for b in range(0, blocks, pair_of):
        both = range(b, b + pair_of)
        q_weight, k_weight, v_weight = (
            jnp.concatenate([weights[c][t] for c in both], axis=1) for t in range(3)
        )
        for i in range(rows // 256):
            at = pl.ds(i * 256, 256)
            found = dot(normed[at, :], k_weight).astype(BF)
            turned = dot(v_weight, normed[at, :], (0, 1)).astype(BF)
            for n, c in enumerate(both):
                keys[c, at, :] = found[:, n * LANES : (n + 1) * LANES]
                values[c, :, i * 256 : (i + 1) * 256] = turned[n * LANES : (n + 1) * LANES]
        for i in range(queries // 256):
            at = pl.ds(pl.multiple_of(first + i * 256, 256), 256)
            found = (dot(normed[at, :], q_weight) * score_scale).astype(BF)
            for n, c in enumerate(both):
                query[c, pl.ds(i * 256, 256), :] = found[:, n * LANES : (n + 1) * LANES]
    per_block = LANES // HEAD_DIM
    heads = blocks * per_block

    def select(head):
        b, j = head // per_block, head % per_block
        return jnp.where(lane // HEAD_DIM == j, query[b], jnp.zeros((), BF))

    def step(head, scores, top, coming, next_scores):
        b, j = head // per_block, head % per_block
        at = pl.ds(pl.multiple_of(j * HEAD_DIM, HEAD_DIM), HEAD_DIM)
        own = select(coming)
        next_keys = coming // per_block
        summed, next_top = None, None
        for i in range(rows // tile):
            part = pl.ds(i * tile, tile)
            found = dot(keys[next_keys, part, :], own, (1, 1))
            next_scores[part, :] = found
            most = jnp.max(found, axis=0, keepdims=True)
            next_top = most if i == 0 else jnp.maximum(next_top, most)
            if top is not None:
                raised = jnp.exp2(scores[part, :] - top).astype(BF)
                lhs = jnp.concatenate(
                    [values[b, at, i * tile : (i + 1) * tile], jnp.ones((HEAD_DIM, tile), BF)],
                    axis=0,
                )
                more = dot(lhs, raised)
                summed = more if i == 0 else summed + more
        if top is not None:
            out[place_of(places, b), at, :] = (summed[:HEAD_DIM] / summed[HEAD_DIM:]).astype(BF)
        return next_top

    def pair(i, top):
        once = jnp.minimum(i, 0) + 1
        next_top = lax.fori_loop(
            0, once, lambda _, most: step(2 * i, even, top, 2 * i + 1, odd), top
        )
        following = jnp.minimum(2 * i + 2, heads - 1)
        return lax.fori_loop(
            0, once, lambda _, most: step(2 * i + 1, odd, next_top, following, even), next_top
        )

    lax.fori_loop(0, heads // 2, pair, step(0, None, None, 0, even))


def attend(feats, weights, params, patches, group):
    blocks = len(feats)
    rows = feats[0].shape[0]
    queries = rows // group
    width = weights[0].shape[1]
    tile = TILE
    flops = 4 * queries * rows * LANES * blocks * (LANES // HEAD_DIM)
    return pl.pallas_call(
        functools.partial(attend_kernel, blocks, patches, group, tile),
        out_shape=[
            jax.ShapeDtypeStruct((blocks, LANES, queries), BF),
            jax.ShapeDtypeStruct((blocks, queries, LANES), BF),
        ],
        in_specs=[VMEM] * (1 + 2 * blocks),
        out_specs=[VMEM, VMEM],
        scratch_shapes=[
            pltpu.VMEM((rows, width), BF),
            pltpu.VMEM((blocks, rows, LANES), BF),
            pltpu.VMEM((blocks, LANES, rows), BF),
            pltpu.VMEM((blocks, queries, LANES), BF),
            pltpu.VMEM((rows, queries), F32),
            pltpu.VMEM((rows, queries), F32),
        ],
        cost_estimate=pl.CostEstimate(
            flops=flops, bytes_accessed=4 * rows * width, transcendentals=0
        ),
        compiler_params=grant(24),
        name="attend",
    )(params, *feats, *weights)


def mlp_kernel(blocks, members, patches, sends, chunk, params, mixed, kept, *refs):
    projs = refs[:blocks]
    ups = refs[blocks : blocks + members]
    downs = refs[blocks + members : blocks + 2 * members]
    vectors = refs[blocks + 2 * members : blocks + 3 * members]
    results = refs[blocks + 3 * members : blocks + 3 * members + sends]
    proj, vector, final = refs[blocks + 3 * members + sends :]
    rows = kept.shape[1]
    width = blocks * LANES
    share = width // members
    group = members // patches
    spots = arrival_order(patches, group)
    places = block_places(blocks, patches, group)
    for k in range(blocks):
        proj[:, pl.ds(pl.multiple_of(places[k] * LANES, LANES), LANES)] = projs[k][...]
    for k in range(members):
        vector[spots[k]] = vectors[k][...]
    out_bias = jnp.concatenate([vector[k, :, :share] for k in range(members)], axis=1)
    down_bias = jnp.concatenate([vector[k, :, share : 2 * share] for k in range(members)], axis=1)
    root_half = 0.5 ** 0.5

    def one(i, carry):
        at = pl.ds(pl.multiple_of(i * chunk, chunk), chunk)
        attended = jnp.concatenate([mixed[b, :, at] for b in range(blocks)], axis=0)
        features = jnp.concatenate([kept[b, at, :] for b in range(blocks)], axis=1)
        residual = (features.astype(F32) + dot(attended, proj[...], (0, 0)) + out_bias).astype(BF)
        wide = residual.astype(F32)
        mean, scale = row_stats([wide], width)
        normed = ((wide - mean) * scale * params[2:3, :] + params[3:4, :]).astype(BF)
        total = wide + down_bias
        for k in range(members):
            spot = spots[k]
            before = dot(normed, ups[k][...]) + vector[spot, :, 2 * share :]
            hidden = (0.5 * before * (1.0 + lax.erf(before * root_half))).astype(BF)
            total = total + dot(hidden, downs[k][...])
        for b in range(blocks):
            final[b, at, :] = total[:, b * LANES : (b + 1) * LANES].astype(BF)
        return carry

    lax.fori_loop(0, rows // chunk, one, 0)
    if sends > 1:
        me = lax.axis_index("head")
        for k in range(sends):
            results[k][...] = final[lax.rem(me + k, sends)]
    else:
        results[0][...] = final[...]


def mlp(patches, params, mixed, kept, projs, ups, downs, vectors):
    blocks, rows, _ = kept.shape
    members = len(ups)
    width = blocks * LANES
    hidden_here = ups[0].shape[1]
    sends = members if members == blocks else 1
    shape = (rows, LANES) if sends > 1 else (blocks, rows, LANES)
    chunk = min(256, rows)
    return pl.pallas_call(
        functools.partial(mlp_kernel, blocks, members, patches, sends, chunk),
        out_shape=[jax.ShapeDtypeStruct(shape, BF)] * sends,
        in_specs=[VMEM, VMEM, VMEM] + [VMEM] * (blocks + 3 * members),
        out_specs=[VMEM] * sends,
        scratch_shapes=[
            pltpu.VMEM((width, width), BF),
            pltpu.VMEM((members, 1, vectors[0].shape[1]), F32),
            pltpu.VMEM((blocks, rows, LANES), BF),
        ],
        cost_estimate=pl.CostEstimate(
            flops=4 * rows * width * hidden_here * members,
            bytes_accessed=4 * width * hidden_here * members,
            transcendentals=0,
        ),
        compiler_params=grant(22),
        name="mlp",
    )(params, mixed, kept, *projs, *ups, *downs, *vectors)


def shift(array, axis, size, step):
    return lax.ppermute(array, axis, [(i, (i + step) % size) for i in range(size)])


def exchange(blocks, axis, size):
    if size <= DIRECT:
        return [blocks[0]] + [shift(blocks[k], axis, size, k) for k in range(1, size)]
    me = lax.axis_index(axis)
    steps = jnp.arange(size, dtype=I32)
    stacked = jnp.stack(blocks)[(steps - me) % size]
    got = lax.all_to_all(stacked, axis, 0, 0, tiled=True)[(me - steps) % size]
    return [got[k] for k in range(size)]


def arrival_order(groups, group):
    member = lax.axis_index("head")
    return [
        lax.rem(member // group - k + groups, groups) * group
        + lax.rem(lax.rem(member, group) - j + group, group)
        for k in range(groups)
        for j in range(group)
    ]


def group_shift(array, groups, group, step):
    size = groups * group
    pairs = [(i, (i // group + step) % groups * group + i % group) for i in range(size)]
    return lax.ppermute(array, "head", pairs)


def member_shift(array, groups, group, step):
    size = groups * group
    pairs = [(i, i // group * group + (i % group + step) % group) for i in range(size)]
    return lax.ppermute(array, "head", pairs)


def gather_members(sources, groups, group):
    found = []
    for k in range(groups):
        moved = sources[k]
        if k > 0:
            moved = group_shift(moved, groups, group, k)
        for j in range(group):
            found.append(moved if j == 0 else member_shift(moved, groups, group, j))
    return found


def body(
    z_feat,
    shard_count,
    hilbert_rank,
    z_slot,
    ln1_gain,
    ln1_bias,
    w_qkv,
    w_out,
    b_out,
    ln2_gain,
    ln2_bias,
    w_up,
    b_up,
    w_down,
    b_down,
):
    shards = lax.axis_size("pts")
    members = lax.axis_size("head")
    rows_here = z_slot.shape[0]
    zone_rows, full_width = z_feat.shape
    width = w_out.shape[1]
    patches = rows_here // PATCH
    group = members // patches
    blocks = full_width // LANES
    skew_step = rows_here // (2 * shards * (shards - 1))
    cap = round_up(rows_here // shards + 2 * skew_step * (shards - 1), 16)
    member = lax.axis_index("head")

    def natural(found):
        spots = jnp.stack(arrival_order(patches, group)).astype(I32)
        stacked = jnp.stack(found)
        back = jnp.zeros((members,), I32).at[spots].set(jnp.arange(members, dtype=I32))
        stacked = jnp.take(stacked, back, axis=0)
        joined = jnp.concatenate([stacked[i] for i in range(members)], axis=-1)
        return [joined[..., b * LANES : (b + 1) * LANES] for b in range(blocks)]

    def everywhere(array):
        return gather_members([array] * patches, patches, group)

    qkv_found = everywhere(w_qkv)
    out_found = everywhere(w_out)
    up_found = everywhere(w_up)
    down_found = everywhere(w_down)
    vector = jnp.concatenate([b_out, b_down, b_up])[None, :]
    vectors = [vector]
    for step in range(1, members):
        k, j = step // group, step % group
        pairs = [
            (i, (i // group + k) % patches * group + (i % group + j) % group)
            for i in range(members)
        ]
        vectors.append(lax.ppermute(vector, "head", pairs))

    rank = hilbert_rank[None, :]
    if width % LANES == 0:
        z_source = z_feat
    else:
        z_source = lax.dynamic_slice_in_dim(z_feat, member * width, width, 1)
    *sends, place = pack(
        shard_count, rank, z_source, width % LANES == 0, width, shards, cap, rows_here
    )
    source = (z_slot // zone_rows).reshape(patches, PATCH, 1)
    pieces = jnp.sum((source == jnp.arange(shards, dtype=I32)).astype(I32), axis=1)
    params = jnp.stack([ln1_gain, ln1_bias, ln2_gain, ln2_bias])
    pieces, params = lax.optimization_barrier((pieces, params))
    arrived = exchange(sends, "pts", shards)
    patch_blocks = compact(pieces, arrived, patches, group)
    feats = gather_members(patch_blocks, patches, group)

    if width == LANES:
        qkv_blocks, out_blocks = qkv_found, out_found
    else:
        feats = natural(feats)
        qkv_blocks, out_blocks = natural(qkv_found), natural(out_found)

    mixed, kept = attend(feats, qkv_blocks, params, patches, group)
    results = mlp(
        patches,
        params,
        mixed,
        kept,
        out_blocks,
        up_found,
        down_found,
        vectors,
    )
    if width != LANES:
        joined = jnp.concatenate([results[0][b] for b in range(blocks)], axis=1)
        results = [
            lax.dynamic_slice_in_dim(joined, (member + k) % members * width, width, 1)
            for k in range(members)
        ]
    parts = [results[0]] + [shift(results[k], "head", members, k) for k in range(1, members)]
    outgoing = spread(pieces, parts, patches, shards, cap)
    returned = exchange(outgoing, "pts", shards)
    return unpack(shard_count, place, returned, zone_rows)


def solution(mesh):
    placed = (
        P(("tile", "pts"), None),
        P(("tile", "pts")),
        P(("tile", "pts")),
        P(("tile", "pts")),
        P(),
        P(),
        P(None, None, "head"),
        P(None, "head"),
        P("head"),
        P(),
        P(),
        P(None, "head"),
        P("head"),
        P("head", None),
        P("head"),
    )

    return jax.shard_map(
        body, mesh=mesh, in_specs=placed, out_specs=P(("tile", "pts"), "head"), check_vma=False
    )
```

profile of v0, /device:TPU:13, one launch (start us, length us, event | category | flops | bytes accessed | tf_op | source)
XLA Modules:
  0.0 137.5 jit_solution(3013294818733241098)
XLA Ops:
  0.9 6.9 %pack.1 = (bf16[1024,128]{1,0:T(8,128)(2,1)}, bf16[1024,128]{1,0:T(8,128)(2,1)}, bf16[1024,128]{1,0:T(8,128)(2,1)}, bf16[1024,128]{1,0:T(8,128)(2,1)}, s32[1,3072]{1,0:T(1,128)}) custom-call(s32[1]{0:T(128)S(6)} %copy.16.held, s32[1,3068]{1,0:T(1,128)} %bitcast.5, bf16[3068,512]{1,0:T(8,128)(2,1)} %z_feat.1), custom_call_target="tpu_custom_call" | custom-call | tf_op jit(solution)/shard_map/pack/pallas_call | solution.py:122
  8.0 1.6 %collective-permute-start.1 = (bf16[1024,128]{1,0:T(8,128)(2,1)}, bf16[1024,128]{1,0:T(8,128)(2,1)S(1)}, u32[]{:S(2)}, u32[]{:S(2)}) collective-permute-start(bf16[1024,128]{1,0:T(8,128)(2,1)} %get-tuple-element.29), channel_id=1, source_target_pairs={{0,8},{4,12},{8,0},{12,4},{1,9},{5,13},{9,1},{13,5},{2,10},{6,14},... | collective-permute-start | bytes 786440 | tf_op jit(solution)/shard_map/ppermute | solution.py:510
  9.6 1.3 collective-permute-start.18
  10.9 1.2 collective-permute-start.19
  13.0 0.7 collective-permute-done.19.refs_14_
  13.6 0.9 collective-permute-start.6
  14.6 0.7 collective-permute-done.refs_1_
  15.3 2.7 %collective-permute-start.9 = (bf16[512,128]{1,0:T(8,128)(2,1)S(1)}, bf16[512,128]{1,0:T(8,128)(2,1)S(1)}, u32[]{:S(2)}, u32[]{:S(2)}) collective-permute-start(bf16[512,128]{1,0:T(8,128)(2,1)S(1)} %copy-done.5), channel_id=1, source_target_pairs={{0,1},{1,0},{2,3},{3,2},{4,5},{5,4},{6,7},{7,6},{8,9},{9,8},{10,11... | collective-permute-start | bytes 393224 | tf_op jit(solution)/shard_map/ppermute | solution.py:542
  17.9 12.2 %collective-permute-done.1.refs_2_ = bf16[1024,128]{1,0:T(8,128)(2,1)S(1)} collective-permute-done((bf16[1024,128]{1,0:T(8,128)(2,1)}, bf16[1024,128]{1,0:T(8,128)(2,1)S(1)}, u32[]{:S(2)}, u32[]{:S(2)}) %collective-permute-start.1) | collective-permute-done | bytes 262176 | tf_op jit(solution)/shard_map/ppermute | solution.py:510
  30.2 1.2 collective-permute-start.10
  31.5 1.9 %collective-permute-done.2.refs_3_ = bf16[1024,128]{1,0:T(8,128)(2,1)S(1)} collective-permute-done((bf16[1024,128]{1,0:T(8,128)(2,1)}, bf16[1024,128]{1,0:T(8,128)(2,1)S(1)}, u32[]{:S(2)}, u32[]{:S(2)}) %collective-permute-start.2) | collective-permute-done | bytes 262176 | tf_op jit(solution)/shard_map/ppermute | solution.py:510
  33.4 1.6 %collective-permute-start.20 = (f32[1,768]{1,0:T(1,128)S(1)}, f32[1,768]{1,0:T(1,128)S(1)}, u32[]{:S(2)}, u32[]{:S(2)}) collective-permute-start(f32[1,768]{1,0:T(1,128)S(1)} %broadcast_in_dim.8.refs_12_), channel_id=1, source_target_pairs={{0,3},{1,2},{2,1},{3,0},{4,7},{5,6},{6,5},{7,4},{8,11},{9,10},{10,... | collective-permute-start | bytes 9224 | tf_op jit(solution)/shard_map/ppermute | solution.py:608
  35.1 0.9 copy-done
  36.0 1.4 %compact.1 = (bf16[1024,128]{1,0:T(8,128)(2,1)S(1)}, bf16[1024,128]{1,0:T(8,128)(2,1)S(1)}) custom-call(s32[2,4]{1,0:T(2,128)S(1)} %convert_reduce_fusion.pieces, bf16[1024,128]{1,0:T(8,128)(2,1)S(1)} %copy-done, bf16[1024,128]{1,0:T(8,128)(2,1)S(1)} %collective-permute-done.refs_1_, bf16[1024,128]{1,0:T(8,128)(2,1)S(1)} %collective-permute-done.1.refs_2_, ...), custom_call_target="tpu_custom_call" | custom-call | tf_op jit(solution)/shard_map/compact/pallas_call | solution.py:188
  37.8 1.2 collective-permute-start.16
  39.2 1.2 collective-permute-start.8
  40.6 27.3 %collective-permute-done.4.refs_2_ = bf16[1024,128]{1,0:T(8,128)(2,1)S(1)} collective-permute-done((bf16[1024,128]{1,0:T(8,128)(2,1)S(1)}, bf16[1024,128]{1,0:T(8,128)(2,1)S(1)}, u32[]{:S(2)}, u32[]{:S(2)}) %collective-permute-start.4) | collective-permute-done | bytes 262176 | tf_op jit(solution)/shard_map/ppermute | solution.py:536
  67.8 0.9 collective-permute-start.5
  69.3 0.6 collective-permute-done.5.refs_3_
  70.4 23.1 %attend.1 = (bf16[4,128,512]{2,1,0:T(8,128)(2,1)S(1)}, bf16[4,512,128]{2,1,0:T(8,128)(2,1)S(1)}) custom-call(f32[4,512]{1,0:T(4,128)S(1)} %pad_maximum_fusion.params, bf16[1024,128]{1,0:T(8,128)(2,1)S(1)} %get-tuple-element.31.refs_0_, bf16[1024,128]{1,0:T(8,128)(2,1)S(1)} %collective-permute-done.3.refs_1_, ...), custom_call_target="tpu_custom_call" | custom-call | flops 8589934592 | bytes 2097152 | tf_op jit(solution)/shard_map/attend/pallas_call | solution.py:409
  93.6 4.4 %mlp.1 = (bf16[512,128]{1,0:T(8,128)(2,1)S(1)}, bf16[512,128]{1,0:T(8,128)(2,1)S(1)}, bf16[512,128]{1,0:T(8,128)(2,1)S(1)}, bf16[512,128]{1,0:T(8,128)(2,1)S(1)}) custom-call(f32[4,512]{1,0:T(4,128)S(1)} %pad_maximum_fusion.params, bf16[4,128,512]{2,1,0:T(8,128)(2,1)S(1)} %get-tuple-element.33.mixed, bf16[4,512,128]{2,1,0:T(8,128)(2,1)S(1)} %get-tuple-element.34.kept, ...), custom_call_target="tpu_custom_call" | custom-call | flops 2147483648 | bytes 4194304 | tf_op jit(solution)/shard_map/mlp/pallas_call | solution.py:489
  98.6 1.2 collective-permute-start.22
  99.8 1.3 collective-permute-done.21.refs_1_
  101.2 4.5 %collective-permute-done.22.refs_2_ = bf16[512,128]{1,0:T(8,128)(2,1)S(1)} collective-permute-done((bf16[512,128]{1,0:T(8,128)(2,1)S(1)}, bf16[512,128]{1,0:T(8,128)(2,1)S(1)}, u32[]{:S(2)}, u32[]{:S(2)}) %collective-permute-start.22) | collective-permute-done | bytes 131104 | tf_op jit(solution)/shard_map/ppermute | solution.py:510
  105.7 0.7 collective-permute-done.23.refs_3_
  106.4 1.4 %spread.1 = (bf16[1024,128]{1,0:T(8,128)(2,1)S(1)}, bf16[1024,128]{1,0:T(8,128)(2,1)S(1)}, bf16[1024,128]{1,0:T(8,128)(2,1)S(1)}, bf16[1024,128]{1,0:T(8,128)(2,1)S(1)}) custom-call(s32[2,4]{1,0:T(2,128)S(1)} %convert_reduce_fusion.pieces, bf16[512,128]{1,0:T(8,128)(2,1)S(1)} %get-tuple-element.35.refs_0_, ...), custom_call_target="tpu_custom_call" | custom-call | tf_op jit(solution)/shard_map/spread/pallas_call | solution.py:223
  107.9 1.8 %collective-permute-start.25 = (bf16[1024,128]{1,0:T(8,128)(2,1)S(1)}, bf16[1024,128]{1,0:T(8,128)(2,1)S(1)}, u32[]{:S(2)}, u32[]{:S(2)}) collective-permute-start(bf16[1024,128]{1,0:T(8,128)(2,1)S(1)} %get-tuple-element.41), channel_id=1, source_target_pairs={{0,8},{4,12},{8,0},{12,4},{1,9},{5,13},{9,1},{13,5},{2,10},{6,14},... | collective-permute-start | bytes 786440 | tf_op jit(solution)/shard_map/ppermute | solution.py:510
  109.7 1.4 %collective-permute-start.26 = (bf16[1024,128]{1,0:T(8,128)(2,1)S(1)}, bf16[1024,128]{1,0:T(8,128)(2,1)S(1)}, u32[]{:S(2)}, u32[]{:S(2)}) collective-permute-start(bf16[1024,128]{1,0:T(8,128)(2,1)S(1)} %get-tuple-element.42), channel_id=1, source_target_pairs={{0,12},{4,0},{8,4},{12,8},{1,13},{5,1},{9,5},{13,9},{2,14},{6,2},{... | collective-permute-start | bytes 786440 | tf_op jit(solution)/shard_map/ppermute | solution.py:510
  111.1 5.1 %collective-permute-done.24.refs_1_ = bf16[1024,128]{1,0:T(8,128)(2,1)S(1)} collective-permute-done((bf16[1024,128]{1,0:T(8,128)(2,1)S(1)}, bf16[1024,128]{1,0:T(8,128)(2,1)S(1)}, u32[]{:S(2)}, u32[]{:S(2)}) %collective-permute-start.24) | collective-permute-done | bytes 262176 | tf_op jit(solution)/shard_map/ppermute | solution.py:510
  116.2 13.6 %collective-permute-done.25.refs_2_ = bf16[1024,128]{1,0:T(8,128)(2,1)S(1)} collective-permute-done((bf16[1024,128]{1,0:T(8,128)(2,1)S(1)}, bf16[1024,128]{1,0:T(8,128)(2,1)S(1)}, u32[]{:S(2)}, u32[]{:S(2)}) %collective-permute-start.25) | collective-permute-done | bytes 262176 | tf_op jit(solution)/shard_map/ppermute | solution.py:510
  129.7 2.8 %collective-permute-done.26.refs_3_ = bf16[1024,128]{1,0:T(8,128)(2,1)S(1)} collective-permute-done((bf16[1024,128]{1,0:T(8,128)(2,1)S(1)}, bf16[1024,128]{1,0:T(8,128)(2,1)S(1)}, u32[]{:S(2)}, u32[]{:S(2)}) %collective-permute-start.26) | collective-permute-done | bytes 262176 | tf_op jit(solution)/shard_map/ppermute | solution.py:510
  132.6 4.9 %unpack.1 = bf16[3068,128]{1,0:T(8,128)(2,1)} custom-call(s32[1]{0:T(128)S(6)} %copy.16.held, s32[1,3072]{1,0:T(1,128)S(1)} %copy-done.1, bf16[1024,128]{1,0:T(8,128)(2,1)S(1)} %get-tuple-element.39.refs_0_, bf16[1024,128]{1,0:T(8,128)(2,1)S(1)} %collective-permute-done.24.refs_1_, bf16[1024,128]{1,0:T(8,128)(2,1)S(1)} %collective-permute-done.25.refs_2_, ...), custom_call_target="tpu_custom_call" | custom-call | tf_op jit(solution)/shard_map/unpack/pallas_call | solution.py:275
  (62 shorter events, 3.6 us)
Async XLA Ops:
  0.0 35.0 %copy-start.8 = (f32[512]{0:T(512)S(1)}, f32[512]{0:T(512)}, u32[]{:S(2)}) copy-start(f32[512]{0:T(512)} %param.25) | copy-start | bytes 6148
  0.0 35.0 %copy-start.9 = (f32[512]{0:T(512)S(1)}, f32[512]{0:T(512)}, u32[]{:S(2)}) copy-start(f32[512]{0:T(512)} %param.24) | copy-start | bytes 6148
  0.1 37.4 %copy-start.2 = (bf16[512,512]{1,0:T(8,128)(2,1)S(1)}, bf16[512,512]{1,0:T(8,128)(2,1)}, u32[]{:S(2)}) copy-start(bf16[512,512]{1,0:T(8,128)(2,1)} %refs_4_.3) | copy-start | bytes 1572868
  0.1 37.7 %copy-start.3 = (bf16[512,512]{1,0:T(8,128)(2,1)S(1)}, bf16[512,512]{1,0:T(8,128)(2,1)}, u32[]{:S(2)}) copy-start(bf16[512,512]{1,0:T(8,128)(2,1)} %refs_8_.1) | copy-start | bytes 1572868
  7.8 7.5 %collective-permute-start = (bf16[1024,128]{1,0:T(8,128)(2,1)}, bf16[1024,128]{1,0:T(8,128)(2,1)S(1)}, u32[]{:S(2)}, u32[]{:S(2)}) collective-permute-start(bf16[1024,128]{1,0:T(8,128)(2,1)} %get-tuple-element.28), channel_id=1, source_target_pairs={{0,4},{4,8},{8,12},{12,0},{1,5},{5,9},{9,13},{13,1},{2,6},{6,10},{... | collective-permute-start | bytes 786440 | tf_op jit(solution)/shard_map/ppermute | solution.py:510
  8.0 22.2 %collective-permute-start.1 = (bf16[1024,128]{1,0:T(8,128)(2,1)}, bf16[1024,128]{1,0:T(8,128)(2,1)S(1)}, u32[]{:S(2)}, u32[]{:S(2)}) collective-permute-start(bf16[1024,128]{1,0:T(8,128)(2,1)} %get-tuple-element.29), channel_id=1, source_target_pairs={{0,8},{4,12},{8,0},{12,4},{1,9},{5,13},{9,1},{13,5},{2,10},{6,14},... | collective-permute-start | bytes 786440 | tf_op jit(solution)/shard_map/ppermute | solution.py:510
  9.6 2.9 %collective-permute-start.18 = (f32[1,768]{1,0:T(1,128)S(1)}, f32[1,768]{1,0:T(1,128)S(1)}, u32[]{:S(2)}, u32[]{:S(2)}) collective-permute-start(f32[1,768]{1,0:T(1,128)S(1)} %broadcast_in_dim.8.refs_12_), channel_id=1, source_target_pairs={{0,1},{1,0},{2,3},{3,2},{4,5},{5,4},{6,7},{7,6},{8,9},{9,8},{10,11... | collective-permute-start | bytes 9224 | tf_op jit(solution)/shard_map/ppermute | solution.py:608
  10.9 2.7 %collective-permute-start.19 = (f32[1,768]{1,0:T(1,128)S(1)}, f32[1,768]{1,0:T(1,128)S(1)}, u32[]{:S(2)}, u32[]{:S(2)}) collective-permute-start(f32[1,768]{1,0:T(1,128)S(1)} %broadcast_in_dim.8.refs_12_), channel_id=1, source_target_pairs={{0,2},{1,3},{2,0},{3,1},{4,6},{5,7},{6,4},{7,5},{8,10},{9,11},{10,... | collective-permute-start | bytes 9224 | tf_op jit(solution)/shard_map/ppermute | solution.py:608
  12.1 21.3 %collective-permute-start.2 = (bf16[1024,128]{1,0:T(8,128)(2,1)}, bf16[1024,128]{1,0:T(8,128)(2,1)S(1)}, u32[]{:S(2)}, u32[]{:S(2)}) collective-permute-start(bf16[1024,128]{1,0:T(8,128)(2,1)} %get-tuple-element.30), channel_id=1, source_target_pairs={{0,12},{4,0},{8,4},{12,8},{1,13},{5,1},{9,5},{13,9},{2,14},{6,2},{... | collective-permute-start | bytes 786440 | tf_op jit(solution)/shard_map/ppermute | solution.py:510
  12.5 26.8 %collective-permute-start.7 = (bf16[3,512,128]{2,1,0:T(8,128)(2,1)S(1)}, bf16[3,512,128]{2,1,0:T(8,128)(2,1)S(1)}, u32[]{:S(2)}, u32[]{:S(2)}) collective-permute-start(bf16[3,512,128]{2,1,0:T(8,128)(2,1)S(1)} %copy-done.4), channel_id=1, source_target_pairs={{0,2},{1,3},{2,0},{3,1},{4,6},{5,7},{6,4},{7,5},{8,10},{9,11},{10,... | collective-permute-start | bytes 1179656 | tf_op jit(solution)/shard_map/ppermute | solution.py:536
  13.6 26.8 %collective-permute-start.6 = (bf16[3,512,128]{2,1,0:T(8,128)(2,1)S(1)}, bf16[3,512,128]{2,1,0:T(8,128)(2,1)S(1)}, u32[]{:S(2)}, u32[]{:S(2)}) collective-permute-start(bf16[3,512,128]{2,1,0:T(8,128)(2,1)S(1)} %copy-done.4), channel_id=1, source_target_pairs={{0,1},{1,0},{2,3},{3,2},{4,5},{5,4},{6,7},{7,6},{8,9},{9,8},{10,11... | collective-permute-start | bytes 1179656 | tf_op jit(solution)/shard_map/ppermute | solution.py:542
  15.3 22.5 %collective-permute-start.9 = (bf16[512,128]{1,0:T(8,128)(2,1)S(1)}, bf16[512,128]{1,0:T(8,128)(2,1)S(1)}, u32[]{:S(2)}, u32[]{:S(2)}) collective-permute-start(bf16[512,128]{1,0:T(8,128)(2,1)S(1)} %copy-done.5), channel_id=1, source_target_pairs={{0,1},{1,0},{2,3},{3,2},{4,5},{5,4},{6,7},{7,6},{8,9},{9,8},{10,11... | collective-permute-start | bytes 393224 | tf_op jit(solution)/shard_map/ppermute | solution.py:542
  30.2 8.8 %collective-permute-start.10 = (bf16[512,128]{1,0:T(8,128)(2,1)S(1)}, bf16[512,128]{1,0:T(8,128)(2,1)S(1)}, u32[]{:S(2)}, u32[]{:S(2)}) collective-permute-start(bf16[512,128]{1,0:T(8,128)(2,1)S(1)} %copy-done.5), channel_id=1, source_target_pairs={{0,2},{1,3},{2,0},{3,1},{4,6},{5,7},{6,4},{7,5},{8,10},{9,11},{10,... | collective-permute-start | bytes 393224 | tf_op jit(solution)/shard_map/ppermute | solution.py:536
  33.4 4.1 %collective-permute-start.20 = (f32[1,768]{1,0:T(1,128)S(1)}, f32[1,768]{1,0:T(1,128)S(1)}, u32[]{:S(2)}, u32[]{:S(2)}) collective-permute-start(f32[1,768]{1,0:T(1,128)S(1)} %broadcast_in_dim.8.refs_12_), channel_id=1, source_target_pairs={{0,3},{1,2},{2,1},{3,0},{4,7},{5,6},{6,5},{7,4},{8,11},{9,10},{10,... | collective-permute-start | bytes 9224 | tf_op jit(solution)/shard_map/ppermute | solution.py:608
  37.5 31.3 %collective-permute-start.13 = (bf16[512,512]{1,0:T(8,128)(2,1)S(1)}, bf16[512,512]{1,0:T(8,128)(2,1)S(1)}, u32[]{:S(2)}, u32[]{:S(2)}) collective-permute-start(bf16[512,512]{1,0:T(8,128)(2,1)S(1)} %copy-done.2), channel_id=1, source_target_pairs={{0,2},{1,3},{2,0},{3,1},{4,6},{5,7},{6,4},{7,5},{8,10},{9,11},{10,... | collective-permute-start | bytes 1572872 | tf_op jit(solution)/shard_map/ppermute | solution.py:536
  37.8 31.5 %collective-permute-start.16 = (bf16[512,512]{1,0:T(8,128)(2,1)S(1)}, bf16[512,512]{1,0:T(8,128)(2,1)S(1)}, u32[]{:S(2)}, u32[]{:S(2)}) collective-permute-start(bf16[512,512]{1,0:T(8,128)(2,1)S(1)} %copy-done.3), channel_id=1, source_target_pairs={{0,2},{1,3},{2,0},{3,1},{4,6},{5,7},{6,4},{7,5},{8,10},{9,11},{10,... | collective-permute-start | bytes 1572872 | tf_op jit(solution)/shard_map/ppermute | solution.py:536
  39.0 28.8 %collective-permute-start.4 = (bf16[1024,128]{1,0:T(8,128)(2,1)S(1)}, bf16[1024,128]{1,0:T(8,128)(2,1)S(1)}, u32[]{:S(2)}, u32[]{:S(2)}) collective-permute-start(bf16[1024,128]{1,0:T(8,128)(2,1)S(1)} %get-tuple-element.32), channel_id=1, source_target_pairs={{0,2},{1,3},{2,0},{3,1},{4,6},{5,7},{6,4},{7,5},{8,10},{9,11},{10,... | collective-permute-start | bytes 786440 | tf_op jit(solution)/shard_map/ppermute | solution.py:536
  39.2 31.0 %collective-permute-start.8 = (bf16[3,512,128]{2,1,0:T(8,128)(2,1)S(1)}, bf16[3,512,128]{2,1,0:T(8,128)(2,1)S(1)}, u32[]{:S(2)}, u32[]{:S(2)}) collective-permute-start(bf16[3,512,128]{2,1,0:T(8,128)(2,1)S(1)} %collective-permute-done.7.refs_6_), channel_id=1, source_target_pairs={{0,1},{1,0},{2,3},{3,2},{4,5},{5,4},{6,7},{7,6},{8,9},{9,8},{10,11... | collective-permute-start | bytes 1179656 | tf_op jit(solution)/shard_map/ppermute | solution.py:542
  40.5 28.2 %collective-permute-start.3 = (bf16[1024,128]{1,0:T(8,128)(2,1)S(1)}, bf16[1024,128]{1,0:T(8,128)(2,1)S(1)}, u32[]{:S(2)}, u32[]{:S(2)}) collective-permute-start(bf16[1024,128]{1,0:T(8,128)(2,1)S(1)} %get-tuple-element.31.refs_0_), channel_id=1, source_target_pairs={{0,1},{1,0},{2,3},{3,2},{4,5},{5,4},{6,7},{7,6},{8,9},{9,8},{10,11... | collective-permute-start | bytes 786440 | tf_op jit(solution)/shard_map/ppermute | solution.py:542
  67.8 2.0 %collective-permute-start.5 = (bf16[1024,128]{1,0:T(8,128)(2,1)S(1)}, bf16[1024,128]{1,0:T(8,128)(2,1)S(1)}, u32[]{:S(2)}, u32[]{:S(2)}) collective-permute-start(bf16[1024,128]{1,0:T(8,128)(2,1)S(1)} %collective-permute-done.4.refs_2_), channel_id=1, source_target_pairs={{0,1},{1,0},{2,3},{3,2},{4,5},{5,4},{6,7},{7,6},{8,9},{9,8},{10,11... | collective-permute-start | bytes 786440 | tf_op jit(solution)/shard_map/ppermute | solution.py:542
  68.7 24.8 %collective-permute-start.12 = (bf16[512,512]{1,0:T(8,128)(2,1)S(1)}, bf16[512,512]{1,0:T(8,128)(2,1)S(1)}, u32[]{:S(2)}, u32[]{:S(2)}) collective-permute-start(bf16[512,512]{1,0:T(8,128)(2,1)S(1)} %copy-done.2), channel_id=1, source_target_pairs={{0,1},{1,0},{2,3},{3,2},{4,5},{5,4},{6,7},{7,6},{8,9},{9,8},{10,11... | collective-permute-start | bytes 1572872 | tf_op jit(solution)/shard_map/ppermute | solution.py:542
  68.7 24.8 %collective-permute-start.15 = (bf16[512,512]{1,0:T(8,128)(2,1)S(1)}, bf16[512,512]{1,0:T(8,128)(2,1)S(1)}, u32[]{:S(2)}, u32[]{:S(2)}) collective-permute-start(bf16[512,512]{1,0:T(8,128)(2,1)S(1)} %copy-done.3), channel_id=1, source_target_pairs={{0,1},{1,0},{2,3},{3,2},{4,5},{5,4},{6,7},{7,6},{8,9},{9,8},{10,11... | collective-permute-start | bytes 1572872 | tf_op jit(solution)/shard_map/ppermute | solution.py:542
  69.2 24.3 %collective-permute-start.11 = (bf16[512,128]{1,0:T(8,128)(2,1)S(1)}, bf16[512,128]{1,0:T(8,128)(2,1)S(1)}, u32[]{:S(2)}, u32[]{:S(2)}) collective-permute-start(bf16[512,128]{1,0:T(8,128)(2,1)S(1)} %collective-permute-done.10.refs_2_), channel_id=1, source_target_pairs={{0,1},{1,0},{2,3},{3,2},{4,5},{5,4},{6,7},{7,6},{8,9},{9,8},{10,11... | collective-permute-start | bytes 393224 | tf_op jit(solution)/shard_map/ppermute | solution.py:542
  69.9 23.7 %collective-permute-start.14 = (bf16[512,512]{1,0:T(8,128)(2,1)S(1)}, bf16[512,512]{1,0:T(8,128)(2,1)S(1)}, u32[]{:S(2)}, u32[]{:S(2)}) collective-permute-start(bf16[512,512]{1,0:T(8,128)(2,1)S(1)} %collective-permute-done.13.refs_6_), channel_id=1, source_target_pairs={{0,1},{1,0},{2,3},{3,2},{4,5},{5,4},{6,7},{7,6},{8,9},{9,8},{10,11... | collective-permute-start | bytes 1572872 | tf_op jit(solution)/shard_map/ppermute | solution.py:542
  70.3 23.3 %collective-permute-start.17 = (bf16[512,512]{1,0:T(8,128)(2,1)S(1)}, bf16[512,512]{1,0:T(8,128)(2,1)S(1)}, u32[]{:S(2)}, u32[]{:S(2)}) collective-permute-start(bf16[512,512]{1,0:T(8,128)(2,1)S(1)} %collective-permute-done.16.refs_10_), channel_id=1, source_target_pairs={{0,1},{1,0},{2,3},{3,2},{4,5},{5,4},{6,7},{7,6},{8,9},{9,8},{10,11... | collective-permute-start | bytes 1572872 | tf_op jit(solution)/shard_map/ppermute | solution.py:542
  93.6 39.0 %copy-start.1 = (s32[1,3072]{1,0:T(1,128)S(1)}, s32[1,3072]{1,0:T(1,128)}, u32[]{:S(2)}) copy-start(s32[1,3072]{1,0:T(1,128)} %get-tuple-element.24.place) | copy-start | bytes 36868
  98.1 3.1 %collective-permute-start.21 = (bf16[512,128]{1,0:T(8,128)(2,1)S(1)}, bf16[512,128]{1,0:T(8,128)(2,1)S(1)}, u32[]{:S(2)}, u32[]{:S(2)}) collective-permute-start(bf16[512,128]{1,0:T(8,128)(2,1)S(1)} %get-tuple-element.36), channel_id=1, source_target_pairs={{0,1},{1,2},{2,3},{3,0},{4,5},{5,6},{6,7},{7,4},{8,9},{9,10},{10,1... | collective-permute-start | bytes 393224 | tf_op jit(solution)/shard_map/ppermute | solution.py:510
  98.6 7.1 %collective-permute-start.22 = (bf16[512,128]{1,0:T(8,128)(2,1)S(1)}, bf16[512,128]{1,0:T(8,128)(2,1)S(1)}, u32[]{:S(2)}, u32[]{:S(2)}) collective-permute-start(bf16[512,128]{1,0:T(8,128)(2,1)S(1)} %get-tuple-element.37), channel_id=1, source_target_pairs={{0,2},{1,3},{2,0},{3,1},{4,6},{5,7},{6,4},{7,5},{8,10},{9,11},{10,... | collective-permute-start | bytes 393224 | tf_op jit(solution)/shard_map/ppermute | solution.py:510
  99.8 6.6 %collective-permute-start.23 = (bf16[512,128]{1,0:T(8,128)(2,1)S(1)}, bf16[512,128]{1,0:T(8,128)(2,1)S(1)}, u32[]{:S(2)}, u32[]{:S(2)}) collective-permute-start(bf16[512,128]{1,0:T(8,128)(2,1)S(1)} %get-tuple-element.38), channel_id=1, source_target_pairs={{0,3},{1,0},{2,1},{3,2},{4,7},{5,4},{6,5},{7,6},{8,11},{9,8},{10,9... | collective-permute-start | bytes 393224 | tf_op jit(solution)/shard_map/ppermute | solution.py:510
  107.8 8.4 %collective-permute-start.24 = (bf16[1024,128]{1,0:T(8,128)(2,1)S(1)}, bf16[1024,128]{1,0:T(8,128)(2,1)S(1)}, u32[]{:S(2)}, u32[]{:S(2)}) collective-permute-start(bf16[1024,128]{1,0:T(8,128)(2,1)S(1)} %get-tuple-element.40), channel_id=1, source_target_pairs={{0,4},{4,8},{8,12},{12,0},{1,5},{5,9},{9,13},{13,1},{2,6},{6,10},{... | collective-permute-start | bytes 786440 | tf_op jit(solution)/shard_map/ppermute | solution.py:510
  107.9 21.9 %collective-permute-start.25 = (bf16[1024,128]{1,0:T(8,128)(2,1)S(1)}, bf16[1024,128]{1,0:T(8,128)(2,1)S(1)}, u32[]{:S(2)}, u32[]{:S(2)}) collective-permute-start(bf16[1024,128]{1,0:T(8,128)(2,1)S(1)} %get-tuple-element.41), channel_id=1, source_target_pairs={{0,8},{4,12},{8,0},{12,4},{1,9},{5,13},{9,1},{13,5},{2,10},{6,14},... | collective-permute-start | bytes 786440 | tf_op jit(solution)/shard_map/ppermute | solution.py:510
  109.7 22.8 %collective-permute-start.26 = (bf16[1024,128]{1,0:T(8,128)(2,1)S(1)}, bf16[1024,128]{1,0:T(8,128)(2,1)S(1)}, u32[]{:S(2)}, u32[]{:S(2)}) collective-permute-start(bf16[1024,128]{1,0:T(8,128)(2,1)S(1)} %get-tuple-element.42), channel_id=1, source_target_pairs={{0,12},{4,0},{8,4},{12,8},{1,13},{5,1},{9,5},{13,9},{2,14},{6,2},{... | collective-permute-start | bytes 786440 | tf_op jit(solution)/shard_map/ppermute | solution.py:510
  (9 other events, 140.2 us)
where the time goes:
time: 138 us; the launch traced here: 137 us
  waiting for transfers between devices  71.4 us (52%)
  Pallas kernels  42.2 us (31%)
  starting transfers between devices  21.6 us (16%)
    ppermute x9, waiting for transfers between devices, shift(): lax.ppermute(array, axis, [(i, (i + step) % size) for i in range(size)])  42.8 us
    ppermute x5, waiting for transfers between devices, group_shift(): return lax.ppermute(array, 'head', pairs)  27.3 us
    pallas_call x1, Pallas kernels, attend(): pl.pallas_call(functools.partial(attend_kernel, blocks, patches, group, t...  23.1 us
    ppermute x9, starting transfers between devices, shift(): lax.ppermute(array, axis, [(i, (i + step) % size) for i in range(size)])  7.21 us
    pallas_call x1, Pallas kernels, pack(): pl.pallas_call(functools.partial(pack_kernel, shards, cap, rows_here, col...  6.94 us
    ppermute x10, starting transfers between devices, member_shift(): return lax.ppermute(array, 'head', pairs)  6.86 us
    pallas_call x1, Pallas kernels, unpack(): pl.pallas_call(functools.partial(unpack_kernel, shards, cap), out_shape=j...  4.89 us
    pallas_call x1, Pallas kernels, mlp(): pl.pallas_call(functools.partial(mlp_kernel, blocks, members, patches, se...  4.44 us
  transfers between devices with their start and end apart: 27, of which 12 were waited for; matrix products, arithmetic and copies ran while one was open for 0% of the time, Pallas kernels for 18%

commit v1 on v0

--- a/solution.py
+++ b/solution.py
@@ -26,6 +26,12 @@
     return lax.dot_general(
         lhs, rhs, (((dims[0],), (dims[1],)), ((), ())), preferred_element_type=F32
     )
+
+
+def exact_dot(values, choice):
+    high = jnp.floor(values * (1.0 / LANES))
+    low = values - high * LANES
+    return dot(high.astype(BF), choice) * LANES + dot(low.astype(BF), choice)
 
 
 def round_up(value, unit):
@@ -79,17 +85,32 @@
     minor_r = lax.broadcasted_iota(I32, (LANES, LANES), 0)
     minor_c = lax.broadcasted_iota(I32, (LANES, LANES), 1)
     below = (minor_c < minor_r).astype(BF)
+    ones = jnp.ones((LANES, LANES), BF)
     major_r = lax.broadcasted_iota(I32, (grid_rows, grid_rows), 0)
     major_c = lax.broadcasted_iota(I32, (grid_rows, grid_rows), 1)
-    earlier = ((major_r < major_c) & (major_r // block == major_c // block)).astype(BF)
-    row_wise = dot(members, earlier)
-    counts = dot(below, members) + dot(jnp.ones((LANES, LANES), BF), row_wise.astype(BF))
-    high = jnp.floor(counts * (1.0 / 32.0))
-    low = counts - high * 32.0
-    spread = dot(high.astype(BF), hot_major) * 32.0 + dot(low.astype(BF), hot_major)
-    found = jnp.sum(jnp.where(hot_minor > 0, spread, 0.0), axis=0, keepdims=True)
-    target = ranks // rows_here
-    place[...] = jnp.where(occupied, target * cap + found.astype(I32), shards * cap)
+    group = PATCH // LANES
+    same_group = major_r // group == major_c // group
+    earlier_row = (same_group & (major_r < major_c)).astype(BF)
+    earlier_group = (
+        (major_r // block == major_c // block)
+        & (major_r // group < major_c // group)
+        & (major_r % group == 0)
+    ).astype(BF)
+    before = dot(below, members) + dot(ones, dot(members, earlier_row).astype(BF))
+    total = dot(ones, dot(members, same_group.astype(BF)).astype(BF))
+    first_half = jnp.floor(total * 0.5)
+    second_half = total - first_half
+    first_base = exact_dot(first_half, earlier_group)
+    second_base = exact_dot(second_half, earlier_group)
+    target = lax.broadcasted_iota(I32, (LANES, grid_rows), 1) // block * cap
+    spot = target.astype(F32) + jnp.where(
+        before < first_half,
+        first_base + before,
+        second_base + before - first_half + cap // 2,
+    )
+    spread_out = exact_dot(spot, hot_major)
+    found = jnp.sum(jnp.where(hot_minor > 0, spread_out, 0.0), axis=0, keepdims=True)
+    place[...] = jnp.where(occupied, found.astype(I32), shards * cap)
     to_smem = pltpu.make_async_copy(place, place_smem, sems.at[1])
     to_smem.start()
     to_out = pltpu.make_async_copy(place, place_out, sems.at[2])
@@ -149,19 +170,24 @@
     lax.fori_loop(0, (length + 31) // 32, one, 0)
 
 
-def segment_starts(pieces, patches, shards, cap):
-    packed_at, patch_at = {}, {}
+def segment_table(pieces, patches, shards, cap):
+    packed_at, patch_at, lengths = {}, {}, {}
     for s in range(shards):
-        at = s * cap
+        ends = [s * cap, s * cap + cap // 2]
         for p in range(patches):
-            packed_at[p, s] = at
-            at = at + pieces[p, s]
+            count = pieces[p, s]
+            lengths[0, p, s] = lax.shift_right_logical(count, 1)
+            lengths[1, p, s] = count - lengths[0, p, s]
+            for half in range(2):
+                packed_at[half, p, s] = ends[half]
+                ends[half] = ends[half] + lengths[half, p, s]
     for p in range(patches):
         at = p * PATCH
-        for s in range(shards):
-            patch_at[p, s] = at
-            at = at + pieces[p, s]
-    return packed_at, patch_at
+        for half in range(2):
+            for s in range(shards):
+                patch_at[half, p, s] = at
+                at = at + lengths[half, p, s]
+    return packed_at, patch_at, lengths
 
 
 def compact_kernel(shards, patches, group, cap, pieces, *refs):
@@ -172,10 +198,12 @@
     for k in range(shards):
         at = pl.multiple_of(lax.rem(here - k + shards, shards) * cap, cap)
         convert_rows(blocks[k], 0, wide, at, cap)
-    packed_at, patch_at = segment_starts(pieces, patches, shards, cap)
+    packed_at, patch_at, lengths = segment_table(pieces, patches, shards, cap)
     for p in range(patches):
-        for s in range(shards):
-            move_segment(wide, packed_at[p, s], patch_rows, patch_at[p, s], pieces[p, s])
+        for half in range(2):
+            for s in range(shards):
+                key = half, p, s
+                move_segment(wide, packed_at[key], patch_rows, patch_at[key], lengths[key])
     own_group = member // group
     for k in range(patches):
         at = pl.multiple_of(lax.rem(own_group + k, patches) * PATCH, PATCH)
@@ -199,35 +227,47 @@
     )(pieces, *blocks)
 
 
-def spread_kernel(shards, patches, members, cap, pieces, *refs):
-    blocks = refs[:members]
-    sends = refs[members : members + shards]
-    patch_rows, wide = refs[members + shards :]
+def spread_kernel(shards, patches, members, cap, half, pieces, *refs):
+    given = members * (half + 1)
+    blocks = refs[:given]
+    sends = refs[given : given + shards]
+    patch_rows, wide = refs[given + shards :]
     here, member = lax.axis_index("pts"), lax.axis_index("head")
+    group = members // patches
     part_rows = blocks[0].shape[0]
-    for k in range(members):
-        at = pl.multiple_of(lax.rem(member - k + members, members) * part_rows, part_rows)
-        convert_rows(blocks[k], 0, patch_rows, at, part_rows)
-    packed_at, patch_at = segment_starts(pieces, patches, shards, cap)
+    for phase in range(half + 1):
+        for k in range(members):
+            source = lax.rem(member - k + members, members)
+            at = source // group * PATCH + phase * (PATCH // 2)
+            at = pl.multiple_of(at + lax.rem(source, group) * part_rows, part_rows)
+            convert_rows(blocks[phase * members + k], 0, patch_rows, at, part_rows)
+    packed_at, patch_at, lengths = segment_table(pieces, patches, shards, cap)
+    size = cap // 2
     for s in range(shards):
         for p in range(patches):
-            move_segment(patch_rows, patch_at[p, s], wide, packed_at[p, s], pieces[p, s])
+            key = half, p, s
+            move_segment(
+                patch_rows,
+                patch_at[key],
+                wide,
+                packed_at[key] - s * cap - half * size + s * size,
+                lengths[key],
+            )
     for k in range(shards):
-        at = pl.multiple_of(lax.rem(here + k, shards) * cap, cap)
-        convert_rows(wide, at, sends[k], 0, cap)
-
-
-def spread(pieces, blocks, patches, shards, cap):
-    members = len(blocks)
-    _, width = blocks[0].shape
+        at = pl.multiple_of(lax.rem(here + k, shards) * size, size)
+        convert_rows(wide, at, sends[k], 0, size)
+
+
+def spread(pieces, blocks, patches, members, shards, cap, half):
+    width = blocks[0].shape[1]
     return pl.pallas_call(
-        functools.partial(spread_kernel, shards, patches, members, cap),
-        out_shape=[jax.ShapeDtypeStruct((cap, width), BF)] * shards,
-        in_specs=[SMEM] + [VMEM] * members,
+        functools.partial(spread_kernel, shards, patches, members, cap, half),
+        out_shape=[jax.ShapeDtypeStruct((cap // 2, width), BF)] * shards,
+        in_specs=[SMEM] + [VMEM] * len(blocks),
         out_specs=[VMEM] * shards,
         scratch_shapes=[
             pltpu.VMEM((patches * PATCH + 64, width), F32),
-            pltpu.VMEM((shards * cap + 64, width), F32),
+            pltpu.VMEM((shards * cap // 2 + 64, width), F32),
         ],
         compiler_params=grant(12),
         name="spread",
@@ -235,14 +275,16 @@
 
 
 def unpack_kernel(shards, cap, held, place, *refs):
-    blocks = refs[:shards]
-    out = refs[shards]
-    wide, picked = refs[shards + 1 :]
+    blocks = refs[: 2 * shards]
+    out = refs[2 * shards]
+    wide, picked = refs[2 * shards + 1 :]
     here, count = lax.axis_index("pts"), held[0]
     zone_rows, width = out.shape
-    for k in range(shards):
-        at = pl.multiple_of(lax.rem(here - k + shards, shards) * cap, cap)
-        convert_rows(blocks[k], 0, wide, at, cap)
+    size = cap // 2
+    for half in range(2):
+        for k in range(shards):
+            at = lax.rem(here - k + shards, shards) * cap + half * size
+            convert_rows(blocks[half * shards + k], 0, wide, pl.multiple_of(at, size), size)
 
     def pick_rows(i, carry):
         base = pl.multiple_of(i * ROW_STEP, ROW_STEP)
@@ -269,13 +311,14 @@
 
 
 def unpack(held, place, blocks, zone_rows):
-    shards = len(blocks)
-    cap, width = blocks[0].shape
+    shards = len(blocks) // 2
+    size, width = blocks[0].shape
+    cap = 2 * size
     slots = place.shape[1]
     return pl.pallas_call(
         functools.partial(unpack_kernel, shards, cap),
         out_shape=jax.ShapeDtypeStruct((zone_rows, width), BF),
-        in_specs=[SMEM, SMEM] + [VMEM] * shards,
+        in_specs=[SMEM, SMEM] + [VMEM] * (2 * shards),
         out_specs=VMEM,
         scratch_shapes=[
             pltpu.VMEM((shards * cap + 8, width), F32),
@@ -302,24 +345,15 @@
     return list(range(blocks))
 
 
-def place_of(places, index):
-    found = places[0]
-    for k in range(1, len(places)):
-        found = jnp.where(index == k, places[k], found)
-    return found
-
-
-def attend_kernel(blocks, patches, group, tile, params, *refs):
+def project_kernel(blocks, patches, group, params, *refs):
     feats = refs[:blocks]
     weights = refs[blocks : 2 * blocks]
-    out, kept = refs[2 * blocks : 2 * blocks + 2]
-    normed, keys, values, query, even, odd = refs[2 * blocks + 2 :]
+    keys, values, query, kept, normed = refs[2 * blocks :]
     rows = feats[0].shape[0]
     width = blocks * LANES
-    queries = query.shape[1]
+    queries = query.shape[1] // 2
     places = block_places(blocks, patches, group)
     part = lax.rem(lax.axis_index("head"), group)
-    first = pl.multiple_of(part * queries, queries)
 
     def norm(i, carry):
         at = pl.ds(pl.multiple_of(i * 128, 128), 128)
@@ -333,9 +367,14 @@
         return carry
 
     lax.fori_loop(0, rows // 128, norm, 0, unroll=2)
+    starts = [
+        pl.multiple_of(part * queries + half * (rows // 2), queries) for half in range(2)
+    ]
     for b in range(blocks):
-        kept[places[b]] = feats[b][pl.ds(first, queries), :]
-    lane = lax.broadcasted_iota(I32, (1, LANES), 1)
+        for half in range(2):
+            kept[places[b], pl.ds(half * queries, queries), :] = feats[b][
+                pl.ds(starts[half], queries), :
+            ]
     score_scale = HEAD_DIM ** (-0.5) * math.log2(math.e)
     pair_of = 2 if blocks % 2 == 0 else 1
     for b in range(0, blocks, pair_of):
@@ -350,24 +389,62 @@
             for n, c in enumerate(both):
                 keys[c, at, :] = found[:, n * LANES : (n + 1) * LANES]
                 values[c, :, i * 256 : (i + 1) * 256] = turned[n * LANES : (n + 1) * LANES]
-        for i in range(queries // 256):
-            at = pl.ds(pl.multiple_of(first + i * 256, 256), 256)
+        for half in range(2):
+            at = pl.ds(starts[half], queries)
             found = (dot(normed[at, :], q_weight) * score_scale).astype(BF)
             for n, c in enumerate(both):
-                query[c, pl.ds(i * 256, 256), :] = found[:, n * LANES : (n + 1) * LANES]
-    per_block = LANES // HEAD_DIM
-    heads = blocks * per_block
-
-    def select(head):
-        b, j = head // per_block, head % per_block
-        return jnp.where(lane // HEAD_DIM == j, query[b], jnp.zeros((), BF))
-
-    def step(head, scores, top, coming, next_scores):
-        b, j = head // per_block, head % per_block
-        at = pl.ds(pl.multiple_of(j * HEAD_DIM, HEAD_DIM), HEAD_DIM)
+                query[c, pl.ds(half * queries, queries), :] = found[
+                    :, n * LANES : (n + 1) * LANES
+                ]
+
+
+def project(feats, weights, params, patches, group):
+    blocks = len(feats)
+    rows = feats[0].shape[0]
+    width = weights[0].shape[1]
+    own = jax.ShapeDtypeStruct((blocks, rows // group, LANES), BF)
+    return pl.pallas_call(
+        functools.partial(project_kernel, blocks, patches, group),
+        out_shape=[
+            jax.ShapeDtypeStruct((blocks, rows, LANES), BF),
+            jax.ShapeDtypeStruct((blocks, LANES, rows), BF),
+            own,
+            own,
+        ],
+        in_specs=[VMEM] * (1 + 2 * blocks),
+        out_specs=[VMEM] * 4,
+        scratch_shapes=[pltpu.VMEM((rows, width), BF)],
+        compiler_params=grant(14),
+        cost_estimate=pl.CostEstimate(
+            flops=6 * rows * width * width, bytes_accessed=8 * rows * width, transcendentals=0
+        ),
+        name="project",
+    )(params, *feats, *weights)
+
+
+def attend_kernel(low, high, half, tile, keys, values, query, out, even, odd):
+    rows = keys.shape[1]
+    queries = query.shape[1] // 2
+    lane = lax.broadcasted_iota(I32, (1, LANES), 1)
+    per_block = LANES // HEAD_DIM // 2
+    steps = (high - low) * per_block
+
+    def select(index):
+        b, j = low + index // per_block, index % per_block
+        own = query[b, pl.ds(half * queries, queries), :]
+        zero = jnp.zeros((), BF)
+        return jnp.concatenate(
+            [jnp.where(lane // HEAD_DIM == 2 * j + n, own, zero) for n in range(2)], axis=0
+        )
+
+    def step(index, scores, top, coming, next_scores):
+        b, j = index // per_block, index % per_block
+        at = [
+            pl.ds(pl.multiple_of((2 * j + n) * HEAD_DIM, HEAD_DIM), HEAD_DIM) for n in range(2)
+        ]
         own = select(coming)
-        next_keys = coming // per_block
-        summed, next_top = None, None
+        next_keys = low + coming // per_block
+        summed, next_top = [None, None], None
         for i in range(rows // tile):
             part = pl.ds(i * tile, tile)
             found = dot(keys[next_keys, part, :], own, (1, 1))
@@ -376,14 +453,19 @@
             next_top = most if i == 0 else jnp.maximum(next_top, most)
             if top is not None:
                 raised = jnp.exp2(scores[part, :] - top).astype(BF)
-                lhs = jnp.concatenate(
-                    [values[b, at, i * tile : (i + 1) * tile], jnp.ones((HEAD_DIM, tile), BF)],
-                    axis=0,
-                )
-                more = dot(lhs, raised)
-                summed = more if i == 0 else summed + more
+                for n in range(2):
+                    lhs = jnp.concatenate(
+                        [
+                            values[low + b, at[n], i * tile : (i + 1) * tile],
+                            jnp.ones((HEAD_DIM, tile), BF),
+                        ],
+                        axis=0,
+                    )
+                    more = dot(lhs, raised[:, n * queries : (n + 1) * queries])
+                    summed[n] = more if i == 0 else summed[n] + more
         if top is not None:
-            out[place_of(places, b), at, :] = (summed[:HEAD_DIM] / summed[HEAD_DIM:]).astype(BF)
+            for n in range(2):
+                out[b, at[n], :] = (summed[n][:HEAD_DIM] / summed[n][HEAD_DIM:]).astype(BF)
         return next_top
 
     def pair(i, top):
@@ -391,60 +473,53 @@
         next_top = lax.fori_loop(
             0, once, lambda _, most: step(2 * i, even, top, 2 * i + 1, odd), top
         )
-        following = jnp.minimum(2 * i + 2, heads - 1)
+        following = jnp.minimum(2 * i + 2, steps - 1)
         return lax.fori_loop(
             0, once, lambda _, most: step(2 * i + 1, odd, next_top, following, even), next_top
         )
 
-    lax.fori_loop(0, heads // 2, pair, step(0, None, None, 0, even))
-
-
-def attend(feats, weights, params, patches, group):
-    blocks = len(feats)
-    rows = feats[0].shape[0]
-    queries = rows // group
-    width = weights[0].shape[1]
-    tile = TILE
-    flops = 4 * queries * rows * LANES * blocks * (LANES // HEAD_DIM)
+    lax.fori_loop(0, steps // 2, pair, step(0, None, None, 0, even))
+
+
+def attend(keys, values, query, low, high, half):
+    rows = keys.shape[1]
+    queries = query.shape[1] // 2
     return pl.pallas_call(
-        functools.partial(attend_kernel, blocks, patches, group, tile),
-        out_shape=[
-            jax.ShapeDtypeStruct((blocks, LANES, queries), BF),
-            jax.ShapeDtypeStruct((blocks, queries, LANES), BF),
-        ],
-        in_specs=[VMEM] * (1 + 2 * blocks),
-        out_specs=[VMEM, VMEM],
-        scratch_shapes=[
-            pltpu.VMEM((rows, width), BF),
-            pltpu.VMEM((blocks, rows, LANES), BF),
-            pltpu.VMEM((blocks, LANES, rows), BF),
-            pltpu.VMEM((blocks, queries, LANES), BF),
-            pltpu.VMEM((rows, queries), F32),
-            pltpu.VMEM((rows, queries), F32),
-        ],
+        functools.partial(attend_kernel, low, high, half, min(TILE, rows)),
+        out_shape=jax.ShapeDtypeStruct((high - low, LANES, queries), BF),
+        in_specs=[VMEM] * 3,
+        out_specs=VMEM,
+        scratch_shapes=[pltpu.VMEM((rows, 2 * queries), F32)] * 2,
+        compiler_params=grant(14),
         cost_estimate=pl.CostEstimate(
-            flops=flops, bytes_accessed=4 * rows * width, transcendentals=0
+            flops=4 * queries * rows * LANES * (high - low) * (LANES // HEAD_DIM),
+            bytes_accessed=4 * rows * LANES * (high - low),
+            transcendentals=0,
         ),
-        compiler_params=grant(24),
         name="attend",
-    )(params, *feats, *weights)
-
-
-def mlp_kernel(blocks, members, patches, sends, chunk, params, mixed, kept, *refs):
+    )(keys, values, query)
+
+
+def mlp_kernel(blocks, members, patches, sends, chunk, half, pieces_of, params, kept, *refs):
+    mixed = refs[:pieces_of]
+    refs = refs[pieces_of:]
     projs = refs[:blocks]
     ups = refs[blocks : blocks + members]
     downs = refs[blocks + members : blocks + 2 * members]
     vectors = refs[blocks + 2 * members : blocks + 3 * members]
     results = refs[blocks + 3 * members : blocks + 3 * members + sends]
     proj, vector, final = refs[blocks + 3 * members + sends :]
-    rows = kept.shape[1]
+    rows = kept.shape[1] // 2
     width = blocks * LANES
     share = width // members
     group = members // patches
     spots = arrival_order(patches, group)
     places = block_places(blocks, patches, group)
     for k in range(blocks):
-        proj[:, pl.ds(pl.multiple_of(places[k] * LANES, LANES), LANES)] = projs[k][...]
+        cols = pl.ds(pl.multiple_of(places[k] * LANES, LANES), LANES)
+        for r in range(blocks):
+            from_rows = pl.ds(pl.multiple_of(places[r] * LANES, LANES), LANES)
+            proj[r * LANES : (r + 1) * LANES, cols] = projs[k][from_rows, :]
     for k in range(members):
         vector[spots[k]] = vectors[k][...]
     out_bias = jnp.concatenate([vector[k, :, :share] for k in range(members)], axis=1)
@@ -453,8 +528,11 @@
 
     def one(i, carry):
         at = pl.ds(pl.multiple_of(i * chunk, chunk), chunk)
-        attended = jnp.concatenate([mixed[b, :, at] for b in range(blocks)], axis=0)
-        features = jnp.concatenate([kept[b, at, :] for b in range(blocks)], axis=1)
+        attended = jnp.concatenate(
+            [m[b, :, at] for m in mixed for b in range(m.shape[0])], axis=0
+        )
+        own = pl.ds(pl.multiple_of(half * rows + i * chunk, chunk), chunk)
+        features = jnp.concatenate([kept[b, own, :] for b in range(blocks)], axis=1)
         residual = (features.astype(F32) + dot(attended, proj[...], (0, 0)) + out_bias).astype(BF)
         wide = residual.astype(F32)
         mean, scale = row_stats([wide], width)
@@ -478,8 +556,8 @@
         results[0][...] = final[...]
 
 
-def mlp(patches, params, mixed, kept, projs, ups, downs, vectors):
-    blocks, rows, _ = kept.shape
+def mlp(patches, half, params, mixed, kept, projs, ups, downs, vectors):
+    blocks, rows = kept.shape[0], kept.shape[1] // 2
     members = len(ups)
     width = blocks * LANES
     hidden_here = ups[0].shape[1]
@@ -487,9 +565,11 @@
     shape = (rows, LANES) if sends > 1 else (blocks, rows, LANES)
     chunk = min(256, rows)
     return pl.pallas_call(
-        functools.partial(mlp_kernel, blocks, members, patches, sends, chunk),
+        functools.partial(
+            mlp_kernel, blocks, members, patches, sends, chunk, half, len(mixed)
+        ),
         out_shape=[jax.ShapeDtypeStruct(shape, BF)] * sends,
-        in_specs=[VMEM, VMEM, VMEM] + [VMEM] * (blocks + 3 * members),
+        in_specs=[VMEM] * (2 + len(mixed) + blocks + 3 * members),
         out_specs=[VMEM] * sends,
         scratch_shapes=[
             pltpu.VMEM((width, width), BF),
@@ -503,7 +583,7 @@
         ),
         compiler_params=grant(22),
         name="mlp",
-    )(params, mixed, kept, *projs, *ups, *downs, *vectors)
+    )(params, kept, *mixed, *projs, *ups, *downs, *vectors)
 
 
 def shift(array, axis, size, step):
@@ -579,7 +659,7 @@
     group = members // patches
     blocks = full_width // LANES
     skew_step = rows_here // (2 * shards * (shards - 1))
-    cap = round_up(rows_here // shards + 2 * skew_step * (shards - 1), 16)
+    cap = round_up(rows_here // shards + 2 * skew_step * (shards - 1), 32)
     member = lax.axis_index("head")
 
     def natural(found):
@@ -629,26 +709,30 @@
         feats = natural(feats)
         qkv_blocks, out_blocks = natural(qkv_found), natural(out_found)
 
-    mixed, kept = attend(feats, qkv_blocks, params, patches, group)
-    results = mlp(
-        patches,
-        params,
-        mixed,
-        kept,
-        out_blocks,
-        up_found,
-        down_found,
-        vectors,
-    )
-    if width != LANES:
-        joined = jnp.concatenate([results[0][b] for b in range(blocks)], axis=1)
-        results = [
-            lax.dynamic_slice_in_dim(joined, (member + k) % members * width, width, 1)
-            for k in range(members)
-        ]
-    parts = [results[0]] + [shift(results[k], "head", members, k) for k in range(1, members)]
-    outgoing = spread(pieces, parts, patches, shards, cap)
+    keys, values, query, kept = project(feats, qkv_blocks, params, patches, group)
+
+    def columns_back(half, mixed):
+        results = mlp(
+            patches, half, params, mixed, kept, out_blocks, up_found, down_found, vectors
+        )
+        if width != LANES:
+            joined = jnp.concatenate([results[0][b] for b in range(blocks)], axis=1)
+            results = [
+                lax.dynamic_slice_in_dim(joined, (member + k) % members * width, width, 1)
+                for k in range(members)
+            ]
+        return [results[0]] + [shift(results[k], "head", members, k) for k in range(1, members)]
+
+    mixed = attend(keys, values, query, 0, blocks, 0)
+    parts = columns_back(0, [mixed])
+    middle = blocks // 2
+    mixed_low = attend(keys, values, query, 0, middle, 1)
+    outgoing = spread(pieces, parts, patches, members, shards, cap, 0)
     returned = exchange(outgoing, "pts", shards)
+    mixed_high = attend(keys, values, query, middle, blocks, 1)
+    parts = parts + columns_back(1, [mixed_low, mixed_high])
+    outgoing = spread(pieces, parts, patches, members, shards, cap, 1)
+    returned = returned + exchange(outgoing, "pts", shards)
     return unpack(shard_count, place, returned, zone_rows)
 
 

time: 138 us -> 136 us (0.986)
  the two profiles are of different devices: /device:TPU:13 before, /device:TPU:0 now
where the time goes in v1:
time: 136 us
  waiting for transfers between devices  57 us (42%)
  Pallas kernels  44.7 us (33%)
  starting transfers between devices  31.9 us (23%)
    ppermute x15, waiting for transfers between devices, shift(): lax.ppermute(array, axis, [(i, (i + step) % size) for i in range(size)])  34.3 us
    ppermute x15, starting transfers between devices, shift(): lax.ppermute(array, axis, [(i, (i + step) % size) for i in range(size)])  22 us
    pallas_call x3, Pallas kernels, attend(): pl.pallas_call(functools.partial(attend_kernel, low, high, half, min(TILE...  21.7 us
    ppermute x3, waiting for transfers between devices, body(): vectors.append(lax.ppermute(vector, 'head', pairs))  15 us
    pallas_call x1, Pallas kernels, pack(): pl.pallas_call(functools.partial(pack_kernel, shards, cap, rows_here, col...  7.21 us
    ppermute x5, waiting for transfers between devices, group_shift(): return lax.ppermute(array, 'head', pairs)  6.85 us
    ppermute x5, starting transfers between devices, group_shift(): return lax.ppermute(array, 'head', pairs)  5.73 us
    pallas_call x1, Pallas kernels, unpack(): pl.pallas_call(functools.partial(unpack_kernel, shards, cap), out_shape=j...  4.89 us
  transfers between devices with their start and end apart: 33, of which 10 were waited for; matrix products, arithmetic and copies ran while one was open for 0% of the time, Pallas kernels for 27%

profile of v1, /device:TPU:0, one launch (start us, length us, event | category | flops | bytes accessed | tf_op | source)
XLA Modules:
  0.0 135.7 jit_solution(6900300181557985849)
XLA Ops:
  0.1 3.0 %collective-permute-start.7 = (bf16[3,512,128]{2,1,0:T(8,128)(2,1)}, bf16[3,512,128]{2,1,0:T(8,128)(2,1)S(1)}, u32[]{:S(2)}, u32[]{:S(2)}) collective-permute-start(bf16[3,512,128]{2,1,0:T(8,128)(2,1)} %refs_4_.1), channel_id=1, source_target_pairs={{0,2},{1,3},{2,0},{3,1},{4,6},{5,7},{6,4},{7,5},{8,10},{9,11},{10,... | collective-permute-start | bytes 1179656 | tf_op jit(solution)/shard_map/ppermute | solution.py:616
  3.8 7.2 %pack.1 = (bf16[1024,128]{1,0:T(8,128)(2,1)}, bf16[1024,128]{1,0:T(8,128)(2,1)}, bf16[1024,128]{1,0:T(8,128)(2,1)}, bf16[1024,128]{1,0:T(8,128)(2,1)}, s32[1,3072]{1,0:T(1,128)}) custom-call(s32[1]{0:T(128)S(6)} %copy.16.held, s32[1,3068]{1,0:T(1,128)} %bitcast.5, bf16[3068,512]{1,0:T(8,128)(2,1)} %z_feat.1), custom_call_target="tpu_custom_call" | custom-call | tf_op jit(solution)/shard_map/pack/pallas_call | solution.py:143
  11.0 1.1 collective-permute-start
  12.1 1.4 %collective-permute-start.1 = (bf16[1024,128]{1,0:T(8,128)(2,1)}, bf16[1024,128]{1,0:T(8,128)(2,1)S(1)}, u32[]{:S(2)}, u32[]{:S(2)}) collective-permute-start(bf16[1024,128]{1,0:T(8,128)(2,1)} %get-tuple-element.39), channel_id=1, source_target_pairs={{0,8},{4,12},{8,0},{12,4},{1,9},{5,13},{9,1},{13,5},{2,10},{6,14},... | collective-permute-start | bytes 786440 | tf_op jit(solution)/shard_map/ppermute | solution.py:590
  13.5 1.9 %collective-permute-start.2 = (bf16[1024,128]{1,0:T(8,128)(2,1)}, bf16[1024,128]{1,0:T(8,128)(2,1)S(1)}, u32[]{:S(2)}, u32[]{:S(2)}) collective-permute-start(bf16[1024,128]{1,0:T(8,128)(2,1)} %get-tuple-element.40), channel_id=1, source_target_pairs={{0,12},{4,0},{8,4},{12,8},{1,13},{5,1},{9,5},{13,9},{2,14},{6,2},{... | collective-permute-start | bytes 786440 | tf_op jit(solution)/shard_map/ppermute | solution.py:590
  15.7 6.7 %collective-permute-done.refs_1_ = bf16[1024,128]{1,0:T(8,128)(2,1)S(1)} collective-permute-done((bf16[1024,128]{1,0:T(8,128)(2,1)}, bf16[1024,128]{1,0:T(8,128)(2,1)S(1)}, u32[]{:S(2)}, u32[]{:S(2)}) %collective-permute-start) | collective-permute-done | bytes 262176 | tf_op jit(solution)/shard_map/ppermute | solution.py:590
  22.4 10.8 %collective-permute-done.1.refs_2_ = bf16[1024,128]{1,0:T(8,128)(2,1)S(1)} collective-permute-done((bf16[1024,128]{1,0:T(8,128)(2,1)}, bf16[1024,128]{1,0:T(8,128)(2,1)S(1)}, u32[]{:S(2)}, u32[]{:S(2)}) %collective-permute-start.1) | collective-permute-done | bytes 262176 | tf_op jit(solution)/shard_map/ppermute | solution.py:590
  34.1 1.5 %compact.1 = (bf16[1024,128]{1,0:T(8,128)(2,1)S(1)}, bf16[1024,128]{1,0:T(8,128)(2,1)S(1)}) custom-call(s32[2,4]{1,0:T(2,128)S(1)} %convert_reduce_fusion.pieces, bf16[1024,128]{1,0:T(8,128)(2,1)S(1)} %copy-done.3, bf16[1024,128]{1,0:T(8,128)(2,1)S(1)} %collective-permute-done.refs_1_, bf16[1024,128]{1,0:T(8,128)(2,1)S(1)} %collective-permute-done.1.refs_2_, ...), custom_call_target="tpu_custom_call" | custom-call | tf_op jit(solution)/shard_map/compact/pallas_call | solution.py:216
  35.8 2.0 %collective-permute-start.13 = (bf16[512,512]{1,0:T(8,128)(2,1)S(1)}, bf16[512,512]{1,0:T(8,128)(2,1)S(1)}, u32[]{:S(2)}, u32[]{:S(2)}) collective-permute-start(bf16[512,512]{1,0:T(8,128)(2,1)S(1)} %copy-done), channel_id=1, source_target_pairs={{0,2},{1,3},{2,0},{3,1},{4,6},{5,7},{6,4},{7,5},{8,10},{9,11},{10,... | collective-permute-start | bytes 1572872 | tf_op jit(solution)/shard_map/ppermute | solution.py:616
  38.1 6.8 %collective-permute-done.4.refs_2_ = bf16[1024,128]{1,0:T(8,128)(2,1)S(1)} collective-permute-done((bf16[1024,128]{1,0:T(8,128)(2,1)S(1)}, bf16[1024,128]{1,0:T(8,128)(2,1)S(1)}, u32[]{:S(2)}, u32[]{:S(2)}) %collective-permute-start.4) | collective-permute-done | bytes 262176 | tf_op jit(solution)/shard_map/ppermute | solution.py:616
  46.5 1.4 %collective-permute-start.20 = (f32[1,768]{1,0:T(1,128)S(1)}, f32[1,768]{1,0:T(1,128)S(1)}, u32[]{:S(2)}, u32[]{:S(2)}) collective-permute-start(f32[1,768]{1,0:T(1,128)S(1)} %broadcast_in_dim.8.refs_13_.refs_14_), channel_id=1, source_target_pairs={{0,3},{1,2},{2,1},{3,0},{4,7},{5,6},{6,5},{7,4},{8,11},{9,10},{10,... | collective-permute-start | bytes 9224 | tf_op jit(solution)/shard_map/ppermute | solution.py:688
  47.9 2.5 %project.1 = (bf16[4,1024,128]{2,1,0:T(8,128)(2,1)S(1)}, bf16[4,128,1024]{2,1,0:T(8,128)(2,1)S(1)}, bf16[4,512,128]{2,1,0:T(8,128)(2,1)S(1)}, bf16[4,512,128]{2,1,0:T(8,128)(2,1)S(1)}) custom-call(f32[4,512]{1,0:T(4,128)S(1)} %pad_maximum_fusion.params, bf16[1024,128]{1,0:T(8,128)(2,1)S(1)} %get-tuple-element.41.refs_0_, ...), custom_call_target="tpu_custom_call" | custom-call | flops 1610612736 | bytes 4194304 | tf_op jit(solution)/shard_map/project/pallas_call | solution.py:406
  51.2 14.9 %collective-permute-done.19.refs_15_.refs_16_ = f32[1,768]{1,0:T(1,128)S(1)} collective-permute-done((f32[1,768]{1,0:T(1,128)S(1)}, f32[1,768]{1,0:T(1,128)S(1)}, u32[]{:S(2)}, u32[]{:S(2)}) %collective-permute-start.19) | collective-permute-done | bytes 3104 | tf_op jit(solution)/shard_map/ppermute | solution.py:688
  67.1 10.6 %attend.3.refs_0_ = bf16[4,128,256]{2,1,0:T(8,128)(2,1)S(1)} custom-call(bf16[4,1024,128]{2,1,0:T(8,128)(2,1)S(1)} %get-tuple-element.44.keys, bf16[4,128,1024]{2,1,0:T(8,128)(2,1)S(1)} %get-tuple-element.45.values, bf16[4,512,128]{2,1,0:T(8,128)(2,1)S(1)} %get-tuple-element.46.query), custom_call_target="tpu_custom_call" | custom-call | flops 4294967296 | bytes 2097152 | tf_op jit(solution)/shard_map/attend/pallas_call | solution.py:487
  78.0 5.5 %attend.5.refs_1_ = bf16[2,128,256]{2,1,0:T(8,128)(2,1)S(1)} custom-call(bf16[4,1024,128]{2,1,0:T(8,128)(2,1)S(1)} %get-tuple-element.44.keys, bf16[4,128,1024]{2,1,0:T(8,128)(2,1)S(1)} %get-tuple-element.45.values, bf16[4,512,128]{2,1,0:T(8,128)(2,1)S(1)} %get-tuple-element.46.query), custom_call_target="tpu_custom_call" | custom-call | flops 2147483648 | bytes 1048576 | tf_op jit(solution)/shard_map/attend/pallas_call | solution.py:487
  83.9 5.5 %attend.4.refs_0_ = bf16[2,128,256]{2,1,0:T(8,128)(2,1)S(1)} custom-call(bf16[4,1024,128]{2,1,0:T(8,128)(2,1)S(1)} %get-tuple-element.44.keys, bf16[4,128,1024]{2,1,0:T(8,128)(2,1)S(1)} %get-tuple-element.45.values, bf16[4,512,128]{2,1,0:T(8,128)(2,1)S(1)} %get-tuple-element.46.query), custom_call_target="tpu_custom_call" | custom-call | flops 2147483648 | bytes 1048576 | tf_op jit(solution)/shard_map/attend/pallas_call | solution.py:487
  89.5 2.4 %mlp.3 = (bf16[256,128]{1,0:T(8,128)(2,1)S(1)}, bf16[256,128]{1,0:T(8,128)(2,1)S(1)}, bf16[256,128]{1,0:T(8,128)(2,1)S(1)}, bf16[256,128]{1,0:T(8,128)(2,1)S(1)}) custom-call(f32[4,512]{1,0:T(4,128)S(1)} %pad_maximum_fusion.params, bf16[4,512,128]{2,1,0:T(8,128)(2,1)S(1)} %get-tuple-element.43.kept, bf16[2,128,256]{2,1,0:T(8,128)(2,1)S(1)} %attend.4.refs_0_, ...), custom_call_target="tpu_custom_call" | custom-call | flops 1073741824 | bytes 4194304 | tf_op jit(solution)/shard_map/mlp/pallas_call | solution.py:567
  92.1 1.6 %collective-permute-start.28 = (bf16[256,128]{1,0:T(8,128)(2,1)S(1)}, bf16[256,128]{1,0:T(8,128)(2,1)S(1)}, u32[]{:S(2)}, u32[]{:S(2)}) collective-permute-start(bf16[256,128]{1,0:T(8,128)(2,1)S(1)} %get-tuple-element.57), channel_id=1, source_target_pairs={{0,2},{1,3},{2,0},{3,1},{4,6},{5,7},{6,4},{7,5},{8,10},{9,11},{10,... | collective-permute-start | bytes 196616 | tf_op jit(solution)/shard_map/ppermute | solution.py:590
  93.7 1.3 collective-permute-start.29
  95.0 2.3 %mlp.2 = (bf16[256,128]{1,0:T(8,128)(2,1)S(1)}, bf16[256,128]{1,0:T(8,128)(2,1)S(1)}, bf16[256,128]{1,0:T(8,128)(2,1)S(1)}, bf16[256,128]{1,0:T(8,128)(2,1)S(1)}) custom-call(f32[4,512]{1,0:T(4,128)S(1)} %pad_maximum_fusion.params, bf16[4,512,128]{2,1,0:T(8,128)(2,1)S(1)} %get-tuple-element.43.kept, bf16[4,128,256]{2,1,0:T(8,128)(2,1)S(1)} %attend.3.refs_0_, ...), custom_call_target="tpu_custom_call" | custom-call | flops 1073741824 | bytes 4194304 | tf_op jit(solution)/shard_map/mlp/pallas_call | solution.py:567
  97.9 1.4 %collective-permute-start.23 = (bf16[256,128]{1,0:T(8,128)(2,1)S(1)}, bf16[256,128]{1,0:T(8,128)(2,1)S(1)}, u32[]{:S(2)}, u32[]{:S(2)}) collective-permute-start(bf16[256,128]{1,0:T(8,128)(2,1)S(1)} %get-tuple-element.50), channel_id=1, source_target_pairs={{0,3},{1,0},{2,1},{3,2},{4,7},{5,4},{6,5},{7,6},{8,11},{9,8},{10,9... | collective-permute-start | bytes 196616 | tf_op jit(solution)/shard_map/ppermute | solution.py:590
  99.3 1.8 %collective-permute-done.21.refs_1_ = bf16[256,128]{1,0:T(8,128)(2,1)S(1)} collective-permute-done((bf16[256,128]{1,0:T(8,128)(2,1)S(1)}, bf16[256,128]{1,0:T(8,128)(2,1)S(1)}, u32[]{:S(2)}, u32[]{:S(2)}) %collective-permute-start.21) | collective-permute-done | bytes 65568 | tf_op jit(solution)/shard_map/ppermute | solution.py:590
  101.1 1.3 collective-permute-done.22.refs_2_
  102.5 1.1 spread.3
  103.6 6.2 %collective-permute-start.30 = (bf16[512,128]{1,0:T(8,128)(2,1)S(1)}, bf16[512,128]{1,0:T(8,128)(2,1)S(1)}, u32[]{:S(2)}, u32[]{:S(2)}) collective-permute-start(bf16[512,128]{1,0:T(8,128)(2,1)S(1)} %get-tuple-element.60), channel_id=1, source_target_pairs={{0,4},{4,8},{8,12},{12,0},{1,5},{5,9},{9,13},{13,1},{2,6},{6,10},{... | collective-permute-start | bytes 393224 | tf_op jit(solution)/shard_map/ppermute | solution.py:590
  110.3 2.0 %collective-permute-start.32 = (bf16[512,128]{1,0:T(8,128)(2,1)S(1)}, bf16[512,128]{1,0:T(8,128)(2,1)S(1)}, u32[]{:S(2)}, u32[]{:S(2)}) collective-permute-start(bf16[512,128]{1,0:T(8,128)(2,1)S(1)} %get-tuple-element.62), channel_id=1, source_target_pairs={{0,12},{4,0},{8,4},{12,8},{1,13},{5,1},{9,5},{13,9},{2,14},{6,2},{... | collective-permute-start | bytes 393224 | tf_op jit(solution)/shard_map/ppermute | solution.py:590
  113.4 2.5 %collective-permute-start.25 = (bf16[512,128]{1,0:T(8,128)(2,1)S(1)}, bf16[512,128]{1,0:T(8,128)(2,1)S(1)}, u32[]{:S(2)}, u32[]{:S(2)}) collective-permute-start(bf16[512,128]{1,0:T(8,128)(2,1)S(1)} %get-tuple-element.53), channel_id=1, source_target_pairs={{0,8},{4,12},{8,0},{12,4},{1,9},{5,13},{9,1},{13,5},{2,10},{6,14},... | collective-permute-start | bytes 393224 | tf_op jit(solution)/shard_map/ppermute | solution.py:590
  115.9 1.3 collective-permute-start.26
  117.2 2.6 %collective-permute-done.31.refs_6_ = bf16[512,128]{1,0:T(8,128)(2,1)S(1)} collective-permute-done((bf16[512,128]{1,0:T(8,128)(2,1)S(1)}, bf16[512,128]{1,0:T(8,128)(2,1)S(1)}, u32[]{:S(2)}, u32[]{:S(2)}) %collective-permute-start.31) | collective-permute-done | bytes 131104 | tf_op jit(solution)/shard_map/ppermute | solution.py:590
  119.8 2.8 %collective-permute-done.24.refs_1_ = bf16[512,128]{1,0:T(8,128)(2,1)S(1)} collective-permute-done((bf16[512,128]{1,0:T(8,128)(2,1)S(1)}, bf16[512,128]{1,0:T(8,128)(2,1)S(1)}, u32[]{:S(2)}, u32[]{:S(2)}) %collective-permute-start.24) | collective-permute-done | bytes 131104 | tf_op jit(solution)/shard_map/ppermute | solution.py:590
  122.6 8.2 %collective-permute-done.25.refs_2_ = bf16[512,128]{1,0:T(8,128)(2,1)S(1)} collective-permute-done((bf16[512,128]{1,0:T(8,128)(2,1)S(1)}, bf16[512,128]{1,0:T(8,128)(2,1)S(1)}, u32[]{:S(2)}, u32[]{:S(2)}) %collective-permute-start.25) | collective-permute-done | bytes 131104 | tf_op jit(solution)/shard_map/ppermute | solution.py:590
  130.8 4.9 %unpack.1 = bf16[3068,128]{1,0:T(8,128)(2,1)} custom-call(s32[1]{0:T(128)S(6)} %copy.16.held, s32[1,3072]{1,0:T(1,128)S(1)} %copy-done.4, bf16[512,128]{1,0:T(8,128)(2,1)S(1)} %get-tuple-element.51.refs_0_, bf16[512,128]{1,0:T(8,128)(2,1)S(1)} %collective-permute-done.24.refs_1_, bf16[512,128]{1,0:T(8,128)(2,1)S(1)} %collective-permute-done.25.refs_2_, ...), custom_call_target="tpu_custom_call" | custom-call | tf_op jit(solution)/shard_map/unpack/pallas_call | solution.py:318
  (79 shorter events, 7.8 us)
Async XLA Ops:
  0.1 35.7 %collective-permute-start.7 = (bf16[3,512,128]{2,1,0:T(8,128)(2,1)}, bf16[3,512,128]{2,1,0:T(8,128)(2,1)S(1)}, u32[]{:S(2)}, u32[]{:S(2)}) collective-permute-start(bf16[3,512,128]{2,1,0:T(8,128)(2,1)} %refs_4_.1), channel_id=1, source_target_pairs={{0,2},{1,3},{2,0},{3,1},{4,6},{5,7},{6,4},{7,5},{8,10},{9,11},{10,... | collective-permute-start | bytes 1179656 | tf_op jit(solution)/shard_map/ppermute | solution.py:616
  3.1 34.8 %collective-permute-start.6 = (bf16[3,512,128]{2,1,0:T(8,128)(2,1)}, bf16[3,512,128]{2,1,0:T(8,128)(2,1)S(1)}, u32[]{:S(2)}, u32[]{:S(2)}) collective-permute-start(bf16[3,512,128]{2,1,0:T(8,128)(2,1)} %refs_4_.1), channel_id=1, source_target_pairs={{0,1},{1,0},{2,3},{3,2},{4,5},{5,4},{6,7},{7,6},{8,9},{9,8},{10,11... | collective-permute-start | bytes 1179656 | tf_op jit(solution)/shard_map/ppermute | solution.py:622
  11.0 11.4 %collective-permute-start = (bf16[1024,128]{1,0:T(8,128)(2,1)}, bf16[1024,128]{1,0:T(8,128)(2,1)S(1)}, u32[]{:S(2)}, u32[]{:S(2)}) collective-permute-start(bf16[1024,128]{1,0:T(8,128)(2,1)} %get-tuple-element.38), channel_id=1, source_target_pairs={{0,4},{4,8},{8,12},{12,0},{1,5},{5,9},{9,13},{13,1},{2,6},{6,10},{... | collective-permute-start | bytes 786440 | tf_op jit(solution)/shard_map/ppermute | solution.py:590
  12.1 21.1 %collective-permute-start.1 = (bf16[1024,128]{1,0:T(8,128)(2,1)}, bf16[1024,128]{1,0:T(8,128)(2,1)S(1)}, u32[]{:S(2)}, u32[]{:S(2)}) collective-permute-start(bf16[1024,128]{1,0:T(8,128)(2,1)} %get-tuple-element.39), channel_id=1, source_target_pairs={{0,8},{4,12},{8,0},{12,4},{1,9},{5,13},{9,1},{13,5},{2,10},{6,14},... | collective-permute-start | bytes 786440 | tf_op jit(solution)/shard_map/ppermute | solution.py:590
  13.5 19.6 %collective-permute-start.2 = (bf16[1024,128]{1,0:T(8,128)(2,1)}, bf16[1024,128]{1,0:T(8,128)(2,1)S(1)}, u32[]{:S(2)}, u32[]{:S(2)}) collective-permute-start(bf16[1024,128]{1,0:T(8,128)(2,1)} %get-tuple-element.40), channel_id=1, source_target_pairs={{0,12},{4,0},{8,4},{12,8},{1,13},{5,1},{9,5},{13,9},{2,14},{6,2},{... | collective-permute-start | bytes 786440 | tf_op jit(solution)/shard_map/ppermute | solution.py:590
  35.7 9.2 %collective-permute-start.4 = (bf16[1024,128]{1,0:T(8,128)(2,1)S(1)}, bf16[1024,128]{1,0:T(8,128)(2,1)S(1)}, u32[]{:S(2)}, u32[]{:S(2)}) collective-permute-start(bf16[1024,128]{1,0:T(8,128)(2,1)S(1)} %get-tuple-element.42), channel_id=1, source_target_pairs={{0,2},{1,3},{2,0},{3,1},{4,6},{5,7},{6,4},{7,5},{8,10},{9,11},{10,... | collective-permute-start | bytes 786440 | tf_op jit(solution)/shard_map/ppermute | solution.py:616
  35.8 10.7 %collective-permute-start.8 = (bf16[3,512,128]{2,1,0:T(8,128)(2,1)S(1)}, bf16[3,512,128]{2,1,0:T(8,128)(2,1)S(1)}, u32[]{:S(2)}, u32[]{:S(2)}) collective-permute-start(bf16[3,512,128]{2,1,0:T(8,128)(2,1)S(1)} %collective-permute-done.7.refs_6_), channel_id=1, source_target_pairs={{0,1},{1,0},{2,3},{3,2},{4,5},{5,4},{6,7},{7,6},{8,9},{9,8},{10,11... | collective-permute-start | bytes 1179656 | tf_op jit(solution)/shard_map/ppermute | solution.py:622
  35.8 30.8 %collective-permute-start.13 = (bf16[512,512]{1,0:T(8,128)(2,1)S(1)}, bf16[512,512]{1,0:T(8,128)(2,1)S(1)}, u32[]{:S(2)}, u32[]{:S(2)}) collective-permute-start(bf16[512,512]{1,0:T(8,128)(2,1)S(1)} %copy-done), channel_id=1, source_target_pairs={{0,2},{1,3},{2,0},{3,1},{4,6},{5,7},{6,4},{7,5},{8,10},{9,11},{10,... | collective-permute-start | bytes 1572872 | tf_op jit(solution)/shard_map/ppermute | solution.py:616
  37.8 28.9 %collective-permute-start.16 = (bf16[512,512]{1,0:T(8,128)(2,1)S(1)}, bf16[512,512]{1,0:T(8,128)(2,1)S(1)}, u32[]{:S(2)}, u32[]{:S(2)}) collective-permute-start(bf16[512,512]{1,0:T(8,128)(2,1)S(1)} %copy-done.1), channel_id=1, source_target_pairs={{0,2},{1,3},{2,0},{3,1},{4,6},{5,7},{6,4},{7,5},{8,10},{9,11},{10,... | collective-permute-start | bytes 1572872 | tf_op jit(solution)/shard_map/ppermute | solution.py:616
  37.9 7.0 %collective-permute-start.3 = (bf16[1024,128]{1,0:T(8,128)(2,1)S(1)}, bf16[1024,128]{1,0:T(8,128)(2,1)S(1)}, u32[]{:S(2)}, u32[]{:S(2)}) collective-permute-start(bf16[1024,128]{1,0:T(8,128)(2,1)S(1)} %get-tuple-element.41.refs_0_), channel_id=1, source_target_pairs={{0,1},{1,0},{2,3},{3,2},{4,5},{5,4},{6,7},{7,6},{8,9},{9,8},{10,11... | collective-permute-start | bytes 786440 | tf_op jit(solution)/shard_map/ppermute | solution.py:622
  45.0 5.5 %collective-permute-start.18 = (f32[1,768]{1,0:T(1,128)S(1)}, f32[1,768]{1,0:T(1,128)S(1)}, u32[]{:S(2)}, u32[]{:S(2)}) collective-permute-start(f32[1,768]{1,0:T(1,128)S(1)} %broadcast_in_dim.8.refs_13_.refs_14_), channel_id=1, source_target_pairs={{0,1},{1,0},{2,3},{3,2},{4,5},{5,4},{6,7},{7,6},{8,9},{9,8},{10,11... | collective-permute-start | bytes 9224 | tf_op jit(solution)/shard_map/ppermute | solution.py:688
  46.4 19.7 %collective-permute-start.19 = (f32[1,768]{1,0:T(1,128)S(1)}, f32[1,768]{1,0:T(1,128)S(1)}, u32[]{:S(2)}, u32[]{:S(2)}) collective-permute-start(f32[1,768]{1,0:T(1,128)S(1)} %broadcast_in_dim.8.refs_13_.refs_14_), channel_id=1, source_target_pairs={{0,2},{1,3},{2,0},{3,1},{4,6},{5,7},{6,4},{7,5},{8,10},{9,11},{10,... | collective-permute-start | bytes 9224 | tf_op jit(solution)/shard_map/ppermute | solution.py:688
  46.5 19.6 %collective-permute-start.20 = (f32[1,768]{1,0:T(1,128)S(1)}, f32[1,768]{1,0:T(1,128)S(1)}, u32[]{:S(2)}, u32[]{:S(2)}) collective-permute-start(f32[1,768]{1,0:T(1,128)S(1)} %broadcast_in_dim.8.refs_13_.refs_14_), channel_id=1, source_target_pairs={{0,3},{1,2},{2,1},{3,0},{4,7},{5,6},{6,5},{7,4},{8,11},{9,10},{10,... | collective-permute-start | bytes 9224 | tf_op jit(solution)/shard_map/ppermute | solution.py:688
  50.5 39.0 %collective-permute-start.12 = (bf16[512,512]{1,0:T(8,128)(2,1)S(1)}, bf16[512,512]{1,0:T(8,128)(2,1)S(1)}, u32[]{:S(2)}, u32[]{:S(2)}) collective-permute-start(bf16[512,512]{1,0:T(8,128)(2,1)S(1)} %copy-done), channel_id=1, source_target_pairs={{0,1},{1,0},{2,3},{3,2},{4,5},{5,4},{6,7},{7,6},{8,9},{9,8},{10,11... | collective-permute-start | bytes 1572872 | tf_op jit(solution)/shard_map/ppermute | solution.py:622
  66.1 23.4 %collective-permute-start.15 = (bf16[512,512]{1,0:T(8,128)(2,1)S(1)}, bf16[512,512]{1,0:T(8,128)(2,1)S(1)}, u32[]{:S(2)}, u32[]{:S(2)}) collective-permute-start(bf16[512,512]{1,0:T(8,128)(2,1)S(1)} %copy-done.1), channel_id=1, source_target_pairs={{0,1},{1,0},{2,3},{3,2},{4,5},{5,4},{6,7},{7,6},{8,9},{9,8},{10,11... | collective-permute-start | bytes 1572872 | tf_op jit(solution)/shard_map/ppermute | solution.py:622
  66.1 11.6 %collective-permute-start.10 = (bf16[512,128]{1,0:T(8,128)(2,1)S(1)}, bf16[512,128]{1,0:T(8,128)(2,1)S(1)}, u32[]{:S(2)}, u32[]{:S(2)}) collective-permute-start(bf16[512,128]{1,0:T(8,128)(2,1)S(1)} %copy-done.2), channel_id=1, source_target_pairs={{0,2},{1,3},{2,0},{3,1},{4,6},{5,7},{6,4},{7,5},{8,10},{9,11},{10,... | collective-permute-start | bytes 393224 | tf_op jit(solution)/shard_map/ppermute | solution.py:616
  66.6 22.9 %collective-permute-start.14 = (bf16[512,512]{1,0:T(8,128)(2,1)S(1)}, bf16[512,512]{1,0:T(8,128)(2,1)S(1)}, u32[]{:S(2)}, u32[]{:S(2)}) collective-permute-start(bf16[512,512]{1,0:T(8,128)(2,1)S(1)} %collective-permute-done.13.refs_7_.refs_8_), channel_id=1, source_target_pairs={{0,1},{1,0},{2,3},{3,2},{4,5},{5,4},{6,7},{7,6},{8,9},{9,8},{10,11... | collective-permute-start | bytes 1572872 | tf_op jit(solution)/shard_map/ppermute | solution.py:622
  66.8 22.8 %collective-permute-start.17 = (bf16[512,512]{1,0:T(8,128)(2,1)S(1)}, bf16[512,512]{1,0:T(8,128)(2,1)S(1)}, u32[]{:S(2)}, u32[]{:S(2)}) collective-permute-start(bf16[512,512]{1,0:T(8,128)(2,1)S(1)} %collective-permute-done.16.refs_11_.refs_12_), channel_id=1, source_target_pairs={{0,1},{1,0},{2,3},{3,2},{4,5},{5,4},{6,7},{7,6},{8,9},{9,8},{10,11... | collective-permute-start | bytes 1572872 | tf_op jit(solution)/shard_map/ppermute | solution.py:622
  77.8 5.8 %collective-permute-start.9 = (bf16[512,128]{1,0:T(8,128)(2,1)S(1)}, bf16[512,128]{1,0:T(8,128)(2,1)S(1)}, u32[]{:S(2)}, u32[]{:S(2)}) collective-permute-start(bf16[512,128]{1,0:T(8,128)(2,1)S(1)} %copy-done.2), channel_id=1, source_target_pairs={{0,1},{1,0},{2,3},{3,2},{4,5},{5,4},{6,7},{7,6},{8,9},{9,8},{10,11... | collective-permute-start | bytes 393224 | tf_op jit(solution)/shard_map/ppermute | solution.py:622
  83.5 6.0 %collective-permute-start.11 = (bf16[512,128]{1,0:T(8,128)(2,1)S(1)}, bf16[512,128]{1,0:T(8,128)(2,1)S(1)}, u32[]{:S(2)}, u32[]{:S(2)}) collective-permute-start(bf16[512,128]{1,0:T(8,128)(2,1)S(1)} %collective-permute-done.10.refs_3_.refs_4_), channel_id=1, source_target_pairs={{0,1},{1,0},{2,3},{3,2},{4,5},{5,4},{6,7},{7,6},{8,9},{9,8},{10,11... | collective-permute-start | bytes 393224 | tf_op jit(solution)/shard_map/ppermute | solution.py:622
  91.9 6.0 %collective-permute-start.27 = (bf16[256,128]{1,0:T(8,128)(2,1)S(1)}, bf16[256,128]{1,0:T(8,128)(2,1)S(1)}, u32[]{:S(2)}, u32[]{:S(2)}) collective-permute-start(bf16[256,128]{1,0:T(8,128)(2,1)S(1)} %get-tuple-element.56), channel_id=1, source_target_pairs={{0,1},{1,2},{2,3},{3,0},{4,5},{5,6},{6,7},{7,4},{8,9},{9,10},{10,1... | collective-permute-start | bytes 196616 | tf_op jit(solution)/shard_map/ppermute | solution.py:590
  92.1 7.2 %collective-permute-start.28 = (bf16[256,128]{1,0:T(8,128)(2,1)S(1)}, bf16[256,128]{1,0:T(8,128)(2,1)S(1)}, u32[]{:S(2)}, u32[]{:S(2)}) collective-permute-start(bf16[256,128]{1,0:T(8,128)(2,1)S(1)} %get-tuple-element.57), channel_id=1, source_target_pairs={{0,2},{1,3},{2,0},{3,1},{4,6},{5,7},{6,4},{7,5},{8,10},{9,11},{10,... | collective-permute-start | bytes 196616 | tf_op jit(solution)/shard_map/ppermute | solution.py:590
  93.7 5.6 %collective-permute-start.29 = (bf16[256,128]{1,0:T(8,128)(2,1)S(1)}, bf16[256,128]{1,0:T(8,128)(2,1)S(1)}, u32[]{:S(2)}, u32[]{:S(2)}) collective-permute-start(bf16[256,128]{1,0:T(8,128)(2,1)S(1)} %get-tuple-element.58), channel_id=1, source_target_pairs={{0,3},{1,0},{2,1},{3,2},{4,7},{5,4},{6,5},{7,6},{8,11},{9,8},{10,9... | collective-permute-start | bytes 196616 | tf_op jit(solution)/shard_map/ppermute | solution.py:590
  97.4 3.8 %collective-permute-start.21 = (bf16[256,128]{1,0:T(8,128)(2,1)S(1)}, bf16[256,128]{1,0:T(8,128)(2,1)S(1)}, u32[]{:S(2)}, u32[]{:S(2)}) collective-permute-start(bf16[256,128]{1,0:T(8,128)(2,1)S(1)} %get-tuple-element.48), channel_id=1, source_target_pairs={{0,1},{1,2},{2,3},{3,0},{4,5},{5,6},{6,7},{7,4},{8,9},{9,10},{10,1... | collective-permute-start | bytes 196616 | tf_op jit(solution)/shard_map/ppermute | solution.py:590
  97.4 5.0 %collective-permute-start.22 = (bf16[256,128]{1,0:T(8,128)(2,1)S(1)}, bf16[256,128]{1,0:T(8,128)(2,1)S(1)}, u32[]{:S(2)}, u32[]{:S(2)}) collective-permute-start(bf16[256,128]{1,0:T(8,128)(2,1)S(1)} %get-tuple-element.49), channel_id=1, source_target_pairs={{0,2},{1,3},{2,0},{3,1},{4,6},{5,7},{6,4},{7,5},{8,10},{9,11},{10,... | collective-permute-start | bytes 196616 | tf_op jit(solution)/shard_map/ppermute | solution.py:590
  97.9 4.5 %collective-permute-start.23 = (bf16[256,128]{1,0:T(8,128)(2,1)S(1)}, bf16[256,128]{1,0:T(8,128)(2,1)S(1)}, u32[]{:S(2)}, u32[]{:S(2)}) collective-permute-start(bf16[256,128]{1,0:T(8,128)(2,1)S(1)} %get-tuple-element.50), channel_id=1, source_target_pairs={{0,3},{1,0},{2,1},{3,2},{4,7},{5,4},{6,5},{7,6},{8,11},{9,8},{10,9... | collective-permute-start | bytes 196616 | tf_op jit(solution)/shard_map/ppermute | solution.py:590
  103.6 12.3 %collective-permute-start.30 = (bf16[512,128]{1,0:T(8,128)(2,1)S(1)}, bf16[512,128]{1,0:T(8,128)(2,1)S(1)}, u32[]{:S(2)}, u32[]{:S(2)}) collective-permute-start(bf16[512,128]{1,0:T(8,128)(2,1)S(1)} %get-tuple-element.60), channel_id=1, source_target_pairs={{0,4},{4,8},{8,12},{12,0},{1,5},{5,9},{9,13},{13,1},{2,6},{6,10},{... | collective-permute-start | bytes 393224 | tf_op jit(solution)/shard_map/ppermute | solution.py:590
  109.8 10.0 %collective-permute-start.31 = (bf16[512,128]{1,0:T(8,128)(2,1)S(1)}, bf16[512,128]{1,0:T(8,128)(2,1)S(1)}, u32[]{:S(2)}, u32[]{:S(2)}) collective-permute-start(bf16[512,128]{1,0:T(8,128)(2,1)S(1)} %get-tuple-element.61), channel_id=1, source_target_pairs={{0,8},{4,12},{8,0},{12,4},{1,9},{5,13},{9,1},{13,5},{2,10},{6,14},... | collective-permute-start | bytes 393224 | tf_op jit(solution)/shard_map/ppermute | solution.py:590
  110.3 9.5 %collective-permute-start.32 = (bf16[512,128]{1,0:T(8,128)(2,1)S(1)}, bf16[512,128]{1,0:T(8,128)(2,1)S(1)}, u32[]{:S(2)}, u32[]{:S(2)}) collective-permute-start(bf16[512,128]{1,0:T(8,128)(2,1)S(1)} %get-tuple-element.62), channel_id=1, source_target_pairs={{0,12},{4,0},{8,4},{12,8},{1,13},{5,1},{9,5},{13,9},{2,14},{6,2},{... | collective-permute-start | bytes 393224 | tf_op jit(solution)/shard_map/ppermute | solution.py:590
  113.3 9.3 %collective-permute-start.24 = (bf16[512,128]{1,0:T(8,128)(2,1)S(1)}, bf16[512,128]{1,0:T(8,128)(2,1)S(1)}, u32[]{:S(2)}, u32[]{:S(2)}) collective-permute-start(bf16[512,128]{1,0:T(8,128)(2,1)S(1)} %get-tuple-element.52), channel_id=1, source_target_pairs={{0,4},{4,8},{8,12},{12,0},{1,5},{5,9},{9,13},{13,1},{2,6},{6,10},{... | collective-permute-start | bytes 393224 | tf_op jit(solution)/shard_map/ppermute | solution.py:590
  113.4 17.5 %collective-permute-start.25 = (bf16[512,128]{1,0:T(8,128)(2,1)S(1)}, bf16[512,128]{1,0:T(8,128)(2,1)S(1)}, u32[]{:S(2)}, u32[]{:S(2)}) collective-permute-start(bf16[512,128]{1,0:T(8,128)(2,1)S(1)} %get-tuple-element.53), channel_id=1, source_target_pairs={{0,8},{4,12},{8,0},{12,4},{1,9},{5,13},{9,1},{13,5},{2,10},{6,14},... | collective-permute-start | bytes 393224 | tf_op jit(solution)/shard_map/ppermute | solution.py:590
  115.9 15.0 %collective-permute-start.26 = (bf16[512,128]{1,0:T(8,128)(2,1)S(1)}, bf16[512,128]{1,0:T(8,128)(2,1)S(1)}, u32[]{:S(2)}, u32[]{:S(2)}) collective-permute-start(bf16[512,128]{1,0:T(8,128)(2,1)S(1)} %get-tuple-element.54), channel_id=1, source_target_pairs={{0,12},{4,0},{8,4},{12,8},{1,13},{5,1},{9,5},{13,9},{2,14},{6,2},{... | collective-permute-start | bytes 393224 | tf_op jit(solution)/shard_map/ppermute | solution.py:590
  (15 other events, 403.3 us)

commit v2 on v1

--- a/solution.py
+++ b/solution.py
@@ -13,6 +13,10 @@
 LANES = 128
 ROW_STEP = 64
 TILE = 512
+FAST_TILE = 256
+AHEAD = 4
+UNROLL = 4
+SAFE_LOG2 = 96.0
 DIRECT = 8
 F32 = jnp.float32
 BF = jnp.bfloat16
@@ -348,7 +352,7 @@
 def project_kernel(blocks, patches, group, params, *refs):
     feats = refs[:blocks]
     weights = refs[blocks : 2 * blocks]
-    keys, values, query, kept, normed = refs[2 * blocks :]
+    keys, values, query, kept, small, normed = refs[2 * blocks :]
     rows = feats[0].shape[0]
     width = blocks * LANES
     queries = query.shape[1] // 2
@@ -377,25 +381,45 @@
             ]
     score_scale = HEAD_DIM ** (-0.5) * math.log2(math.e)
     pair_of = 2 if blocks % 2 == 0 else 1
+    span = pair_of * LANES
+    head_r = lax.broadcasted_iota(I32, (span, span), 0) // HEAD_DIM
+    head_c = lax.broadcasted_iota(I32, (span, span), 1) // HEAD_DIM
+    same_head = (head_r == head_c).astype(BF)
+
+    def largest(found):
+        return jnp.max(jnp.abs(found), axis=0, keepdims=True)
+
+    worst = None
     for b in range(0, blocks, pair_of):
         both = range(b, b + pair_of)
+        key_most, query_most = None, None
         q_weight, k_weight, v_weight = (
             jnp.concatenate([weights[c][t] for c in both], axis=1) for t in range(3)
         )
         for i in range(rows // 256):
             at = pl.ds(i * 256, 256)
-            found = dot(normed[at, :], k_weight).astype(BF)
+            found = dot(normed[at, :], k_weight)
+            most = largest(found)
+            key_most = most if i == 0 else jnp.maximum(key_most, most)
+            found = found.astype(BF)
             turned = dot(v_weight, normed[at, :], (0, 1)).astype(BF)
             for n, c in enumerate(both):
                 keys[c, at, :] = found[:, n * LANES : (n + 1) * LANES]
                 values[c, :, i * 256 : (i + 1) * 256] = turned[n * LANES : (n + 1) * LANES]
         for half in range(2):
             at = pl.ds(starts[half], queries)
-            found = (dot(normed[at, :], q_weight) * score_scale).astype(BF)
+            found = dot(normed[at, :], q_weight) * score_scale
+            most = largest(found)
+            query_most = most if half == 0 else jnp.maximum(query_most, most)
+            found = found.astype(BF)
             for n, c in enumerate(both):
                 query[c, pl.ds(half * queries, queries), :] = found[
                     :, n * LANES : (n + 1) * LANES
                 ]
+        product = jnp.broadcast_to(key_most * query_most, (8, span)).astype(BF)
+        bound = dot(product, same_head)
+        worst = bound if b == 0 else jnp.maximum(worst, bound)
+    small[0] = (jnp.max(worst) * 1.05 < SAFE_LOG2).astype(I32)
 
 
 def project(feats, weights, params, patches, group):
@@ -410,9 +434,10 @@
             jax.ShapeDtypeStruct((blocks, LANES, rows), BF),
             own,
             own,
+            jax.ShapeDtypeStruct((1,), I32),
         ],
         in_specs=[VMEM] * (1 + 2 * blocks),
-        out_specs=[VMEM] * 4,
+        out_specs=[VMEM] * 4 + [SMEM],
         scratch_shapes=[pltpu.VMEM((rows, width), BF)],
         compiler_params=grant(14),
         cost_estimate=pl.CostEstimate(
@@ -422,7 +447,7 @@
     )(params, *feats, *weights)
 
 
-def attend_kernel(low, high, half, tile, keys, values, query, out, even, odd):
+def attend_kernel(low, high, half, tile, small, keys, values, query, out, even, odd):
     rows = keys.shape[1]
     queries = query.shape[1] // 2
     lane = lax.broadcasted_iota(I32, (1, LANES), 1)
@@ -478,16 +503,58 @@
             0, once, lambda _, most: step(2 * i + 1, odd, next_top, following, even), next_top
         )
 
-    lax.fori_loop(0, steps // 2, pair, step(0, None, None, 0, even))
-
-
-def attend(keys, values, query, low, high, half):
+    @pl.when(small[0] == 0)
+    def _():
+        lax.fori_loop(0, steps // 2, pair, step(0, None, None, 0, even))
+
+    fast_tile = min(FAST_TILE, rows)
+    tiles = rows // fast_tile
+
+    def several(i, carry):
+        indexes = [UNROLL * i + u for u in range(UNROLL)]
+        plan = [(u, t) for u in range(UNROLL) for t in range(tiles)]
+        owns = [None] * UNROLL
+
+        def score(u, t):
+            if t == 0:
+                owns[u] = select(indexes[u])
+            part = pl.ds(t * fast_tile, fast_tile)
+            return dot(keys[low + indexes[u] // per_block, part, :], owns[u], (1, 1))
+
+        waiting = [score(*plan[n]) for n in range(min(AHEAD, len(plan)))]
+        summed = [None, None]
+        for n, (u, t) in enumerate(plan):
+            if n + AHEAD < len(plan):
+                waiting.append(score(*plan[n + AHEAD]))
+            raised = jnp.exp2(waiting[n]).astype(BF)
+            b, j = indexes[u] // per_block, indexes[u] % per_block
+            for m in range(2):
+                at = pl.ds(pl.multiple_of((2 * j + m) * HEAD_DIM, HEAD_DIM), HEAD_DIM)
+                lhs = jnp.concatenate(
+                    [
+                        values[low + b, at, t * fast_tile : (t + 1) * fast_tile],
+                        jnp.ones((HEAD_DIM, fast_tile), BF),
+                    ],
+                    axis=0,
+                )
+                more = dot(lhs, raised[:, m * queries : (m + 1) * queries])
+                summed[m] = more if t == 0 else summed[m] + more
+                if t == tiles - 1:
+                    out[b, at, :] = (summed[m][:HEAD_DIM] / summed[m][HEAD_DIM:]).astype(BF)
+        return carry
+
+    @pl.when(small[0] != 0)
+    def _():
+        lax.fori_loop(0, steps // UNROLL, several, 0)
+
+
+def attend(small, keys, values, query, low, high, half):
     rows = keys.shape[1]
     queries = query.shape[1] // 2
     return pl.pallas_call(
         functools.partial(attend_kernel, low, high, half, min(TILE, rows)),
         out_shape=jax.ShapeDtypeStruct((high - low, LANES, queries), BF),
-        in_specs=[VMEM] * 3,
+        in_specs=[SMEM] + [VMEM] * 3,
         out_specs=VMEM,
         scratch_shapes=[pltpu.VMEM((rows, 2 * queries), F32)] * 2,
         compiler_params=grant(14),
@@ -497,7 +564,7 @@
             transcendentals=0,
         ),
         name="attend",
-    )(keys, values, query)
+    )(small, keys, values, query)
 
 
 def mlp_kernel(blocks, members, patches, sends, chunk, half, pieces_of, params, kept, *refs):
@@ -709,7 +776,7 @@
         feats = natural(feats)
         qkv_blocks, out_blocks = natural(qkv_found), natural(out_found)
 
-    keys, values, query, kept = project(feats, qkv_blocks, params, patches, group)
+    keys, values, query, kept, small = project(feats, qkv_blocks, params, patches, group)
 
     def columns_back(half, mixed):
         results = mlp(
@@ -723,13 +790,13 @@
             ]
         return [results[0]] + [shift(results[k], "head", members, k) for k in range(1, members)]
 
-    mixed = attend(keys, values, query, 0, blocks, 0)
+    mixed = attend(small, keys, values, query, 0, blocks, 0)
     parts = columns_back(0, [mixed])
     middle = blocks // 2
-    mixed_low = attend(keys, values, query, 0, middle, 1)
+    mixed_low = attend(small, keys, values, query, 0, middle, 1)
     outgoing = spread(pieces, parts, patches, members, shards, cap, 0)
     returned = exchange(outgoing, "pts", shards)
-    mixed_high = attend(keys, values, query, middle, blocks, 1)
+    mixed_high = attend(small, keys, values, query, middle, blocks, 1)
     parts = parts + columns_back(1, [mixed_low, mixed_high])
     outgoing = spread(pieces, parts, patches, members, shards, cap, 1)
     returned = returned + exchange(outgoing, "pts", shards)

time: 136 us -> 139 us (1.022)
  Pallas kernels: 44.7 us -> 47.8 us
    pallas_call x3, Pallas kernels: 21.7 us -> 23.9 us  [attend(): pl.pallas_call(functools.partial(attend_kernel, low, high, half, min(TILE...]
  transfers between devices with their start and end apart: 33 -> 33, of which waited for: 10 -> 10; matrix products, arithmetic and copies ran while one was open for 0% -> 0% of each run, Pallas kernels for 27% -> 29%
where the time goes in v2:
time: 139 us; the launch traced here: 138 us
  waiting for transfers between devices  56.1 us (40%)
  Pallas kernels  47.8 us (34%)
  starting transfers between devices  31.8 us (23%)
    ppermute x15, waiting for transfers between devices, shift(): lax.ppermute(array, axis, [(i, (i + step) % size) for i in range(size)])  34.3 us
    pallas_call x3, Pallas kernels, attend(): pl.pallas_call(functools.partial(attend_kernel, low, high, half, min(TILE...  23.9 us
    ppermute x15, starting transfers between devices, shift(): lax.ppermute(array, axis, [(i, (i + step) % size) for i in range(size)])  22 us
    ppermute x3, waiting for transfers between devices, body(): vectors.append(lax.ppermute(vector, 'head', pairs))  14 us
    pallas_call x1, Pallas kernels, pack(): pl.pallas_call(functools.partial(pack_kernel, shards, cap, rows_here, col...  7.21 us
    ppermute x5, waiting for transfers between devices, group_shift(): return lax.ppermute(array, 'head', pairs)  6.85 us
    ppermute x5, starting transfers between devices, group_shift(): return lax.ppermute(array, 'head', pairs)  5.73 us
    pallas_call x1, Pallas kernels, unpack(): pl.pallas_call(functools.partial(unpack_kernel, shards, cap), out_shape=j...  4.89 us
  transfers between devices with their start and end apart: 33, of which 10 were waited for; matrix products, arithmetic and copies ran while one was open for 0% of the time, Pallas kernels for 29%

profile of v2, /device:TPU:0, one launch (start us, length us, event | category | flops | bytes accessed | tf_op | source)
XLA Modules:
  0.0 138.0 jit_solution(13202600959704126243)
XLA Ops:
  0.1 3.0 %collective-permute-start.7 = (bf16[3,512,128]{2,1,0:T(8,128)(2,1)}, bf16[3,512,128]{2,1,0:T(8,128)(2,1)S(1)}, u32[]{:S(2)}, u32[]{:S(2)}) collective-permute-start(bf16[3,512,128]{2,1,0:T(8,128)(2,1)} %refs_4_.1), channel_id=1, source_target_pairs={{0,2},{1,3},{2,0},{3,1},{4,6},{5,7},{6,4},{7,5},{8,10},{9,11},{10,... | collective-permute-start | bytes 1179656 | tf_op jit(solution)/shard_map/ppermute | solution.py:683
  3.8 7.2 %pack.1 = (bf16[1024,128]{1,0:T(8,128)(2,1)}, bf16[1024,128]{1,0:T(8,128)(2,1)}, bf16[1024,128]{1,0:T(8,128)(2,1)}, bf16[1024,128]{1,0:T(8,128)(2,1)}, s32[1,3072]{1,0:T(1,128)}) custom-call(s32[1]{0:T(128)S(6)} %copy.16.held, s32[1,3068]{1,0:T(1,128)} %bitcast.5, bf16[3068,512]{1,0:T(8,128)(2,1)} %z_feat.1), custom_call_target="tpu_custom_call" | custom-call | tf_op jit(solution)/shard_map/pack/pallas_call | solution.py:147
  11.0 1.1 collective-permute-start
  12.1 1.4 %collective-permute-start.1 = (bf16[1024,128]{1,0:T(8,128)(2,1)}, bf16[1024,128]{1,0:T(8,128)(2,1)S(1)}, u32[]{:S(2)}, u32[]{:S(2)}) collective-permute-start(bf16[1024,128]{1,0:T(8,128)(2,1)} %get-tuple-element.40), channel_id=1, source_target_pairs={{0,8},{4,12},{8,0},{12,4},{1,9},{5,13},{9,1},{13,5},{2,10},{6,14},... | collective-permute-start | bytes 786440 | tf_op jit(solution)/shard_map/ppermute | solution.py:657
  13.5 1.9 %collective-permute-start.2 = (bf16[1024,128]{1,0:T(8,128)(2,1)}, bf16[1024,128]{1,0:T(8,128)(2,1)S(1)}, u32[]{:S(2)}, u32[]{:S(2)}) collective-permute-start(bf16[1024,128]{1,0:T(8,128)(2,1)} %get-tuple-element.41), channel_id=1, source_target_pairs={{0,12},{4,0},{8,4},{12,8},{1,13},{5,1},{9,5},{13,9},{2,14},{6,2},{... | collective-permute-start | bytes 786440 | tf_op jit(solution)/shard_map/ppermute | solution.py:657
  15.7 6.7 %collective-permute-done.refs_1_ = bf16[1024,128]{1,0:T(8,128)(2,1)S(1)} collective-permute-done((bf16[1024,128]{1,0:T(8,128)(2,1)}, bf16[1024,128]{1,0:T(8,128)(2,1)S(1)}, u32[]{:S(2)}, u32[]{:S(2)}) %collective-permute-start) | collective-permute-done | bytes 262176 | tf_op jit(solution)/shard_map/ppermute | solution.py:657
  22.4 10.8 %collective-permute-done.1.refs_2_ = bf16[1024,128]{1,0:T(8,128)(2,1)S(1)} collective-permute-done((bf16[1024,128]{1,0:T(8,128)(2,1)}, bf16[1024,128]{1,0:T(8,128)(2,1)S(1)}, u32[]{:S(2)}, u32[]{:S(2)}) %collective-permute-start.1) | collective-permute-done | bytes 262176 | tf_op jit(solution)/shard_map/ppermute | solution.py:657
  34.1 1.5 %compact.1 = (bf16[1024,128]{1,0:T(8,128)(2,1)S(1)}, bf16[1024,128]{1,0:T(8,128)(2,1)S(1)}) custom-call(s32[2,4]{1,0:T(2,128)S(1)} %convert_reduce_fusion.pieces, bf16[1024,128]{1,0:T(8,128)(2,1)S(1)} %copy-done.3, bf16[1024,128]{1,0:T(8,128)(2,1)S(1)} %collective-permute-done.refs_1_, bf16[1024,128]{1,0:T(8,128)(2,1)S(1)} %collective-permute-done.1.refs_2_, ...), custom_call_target="tpu_custom_call" | custom-call | tf_op jit(solution)/shard_map/compact/pallas_call | solution.py:220
  35.8 2.0 %collective-permute-start.13 = (bf16[512,512]{1,0:T(8,128)(2,1)S(1)}, bf16[512,512]{1,0:T(8,128)(2,1)S(1)}, u32[]{:S(2)}, u32[]{:S(2)}) collective-permute-start(bf16[512,512]{1,0:T(8,128)(2,1)S(1)} %copy-done), channel_id=1, source_target_pairs={{0,2},{1,3},{2,0},{3,1},{4,6},{5,7},{6,4},{7,5},{8,10},{9,11},{10,... | collective-permute-start | bytes 1572872 | tf_op jit(solution)/shard_map/ppermute | solution.py:683
  38.1 6.8 %collective-permute-done.4.refs_2_ = bf16[1024,128]{1,0:T(8,128)(2,1)S(1)} collective-permute-done((bf16[1024,128]{1,0:T(8,128)(2,1)S(1)}, bf16[1024,128]{1,0:T(8,128)(2,1)S(1)}, u32[]{:S(2)}, u32[]{:S(2)}) %collective-permute-start.4) | collective-permute-done | bytes 262176 | tf_op jit(solution)/shard_map/ppermute | solution.py:683
  46.5 1.4 %collective-permute-start.20 = (f32[1,768]{1,0:T(1,128)S(1)}, f32[1,768]{1,0:T(1,128)S(1)}, u32[]{:S(2)}, u32[]{:S(2)}) collective-permute-start(f32[1,768]{1,0:T(1,128)S(1)} %broadcast_in_dim.8.refs_13_.refs_14_), channel_id=1, source_target_pairs={{0,3},{1,2},{2,1},{3,0},{4,7},{5,6},{6,5},{7,4},{8,11},{9,10},{10,... | collective-permute-start | bytes 9224 | tf_op jit(solution)/shard_map/ppermute | solution.py:755
  47.9 3.4 %project.1 = (bf16[4,1024,128]{2,1,0:T(8,128)(2,1)S(1)}, bf16[4,128,1024]{2,1,0:T(8,128)(2,1)S(1)}, bf16[4,512,128]{2,1,0:T(8,128)(2,1)S(1)}, bf16[4,512,128]{2,1,0:T(8,128)(2,1)S(1)}, s32[1]{0:T(128)}) custom-call(f32[4,512]{1,0:T(4,128)S(1)} %pad_maximum_fusion.params, bf16[1024,128]{1,0:T(8,128)(2,1)S(1)} %get-tuple-element.42.refs_0_, ...), custom_call_target="tpu_custom_call" | custom-call | flops 1610612736 | bytes 4194304 | tf_op jit(solution)/shard_map/project/pallas_call | solution.py:430
  52.1 14.0 %collective-permute-done.19.refs_15_.refs_16_ = f32[1,768]{1,0:T(1,128)S(1)} collective-permute-done((f32[1,768]{1,0:T(1,128)S(1)}, f32[1,768]{1,0:T(1,128)S(1)}, u32[]{:S(2)}, u32[]{:S(2)}) %collective-permute-start.19) | collective-permute-done | bytes 3104 | tf_op jit(solution)/shard_map/ppermute | solution.py:755
  67.1 11.3 %attend.3.refs_0_ = bf16[4,128,256]{2,1,0:T(8,128)(2,1)S(1)} custom-call(s32[1]{0:T(128)} %get-tuple-element.45.small, bf16[4,1024,128]{2,1,0:T(8,128)(2,1)S(1)} %get-tuple-element.46.keys, bf16[4,128,1024]{2,1,0:T(8,128)(2,1)S(1)} %get-tuple-element.47.values, bf16[4,512,128]{2,1,0:T(8,128)(2,1)S(1)} %get-tuple-element.48.query), custom_call_target="tpu_custom_call" | custom-call | flops 4294967296 | bytes 2097152 | tf_op jit(solution)/shard_map/attend/pallas_call | solution.py:554
  78.7 6.2 %attend.5.refs_1_ = bf16[2,128,256]{2,1,0:T(8,128)(2,1)S(1)} custom-call(s32[1]{0:T(128)} %get-tuple-element.45.small, bf16[4,1024,128]{2,1,0:T(8,128)(2,1)S(1)} %get-tuple-element.46.keys, bf16[4,128,1024]{2,1,0:T(8,128)(2,1)S(1)} %get-tuple-element.47.values, bf16[4,512,128]{2,1,0:T(8,128)(2,1)S(1)} %get-tuple-element.48.query), custom_call_target="tpu_custom_call" | custom-call | flops 2147483648 | bytes 1048576 | tf_op jit(solution)/shard_map/attend/pallas_call | solution.py:554
  85.3 6.4 %attend.4.refs_0_ = bf16[2,128,256]{2,1,0:T(8,128)(2,1)S(1)} custom-call(s32[1]{0:T(128)} %get-tuple-element.45.small, bf16[4,1024,128]{2,1,0:T(8,128)(2,1)S(1)} %get-tuple-element.46.keys, bf16[4,128,1024]{2,1,0:T(8,128)(2,1)S(1)} %get-tuple-element.47.values, bf16[4,512,128]{2,1,0:T(8,128)(2,1)S(1)} %get-tuple-element.48.query), custom_call_target="tpu_custom_call" | custom-call | flops 2147483648 | bytes 1048576 | tf_op jit(solution)/shard_map/attend/pallas_call | solution.py:554
  91.8 2.3 %mlp.3 = (bf16[256,128]{1,0:T(8,128)(2,1)S(1)}, bf16[256,128]{1,0:T(8,128)(2,1)S(1)}, bf16[256,128]{1,0:T(8,128)(2,1)S(1)}, bf16[256,128]{1,0:T(8,128)(2,1)S(1)}) custom-call(f32[4,512]{1,0:T(4,128)S(1)} %pad_maximum_fusion.params, bf16[4,512,128]{2,1,0:T(8,128)(2,1)S(1)} %get-tuple-element.44.kept, bf16[2,128,256]{2,1,0:T(8,128)(2,1)S(1)} %attend.4.refs_0_, ...), custom_call_target="tpu_custom_call" | custom-call | flops 1073741824 | bytes 4194304 | tf_op jit(solution)/shard_map/mlp/pallas_call | solution.py:634
  94.3 1.6 %collective-permute-start.28 = (bf16[256,128]{1,0:T(8,128)(2,1)S(1)}, bf16[256,128]{1,0:T(8,128)(2,1)S(1)}, u32[]{:S(2)}, u32[]{:S(2)}) collective-permute-start(bf16[256,128]{1,0:T(8,128)(2,1)S(1)} %get-tuple-element.59), channel_id=1, source_target_pairs={{0,2},{1,3},{2,0},{3,1},{4,6},{5,7},{6,4},{7,5},{8,10},{9,11},{10,... | collective-permute-start | bytes 196616 | tf_op jit(solution)/shard_map/ppermute | solution.py:657
  96.0 1.3 collective-permute-start.29
  97.3 2.3 %mlp.2 = (bf16[256,128]{1,0:T(8,128)(2,1)S(1)}, bf16[256,128]{1,0:T(8,128)(2,1)S(1)}, bf16[256,128]{1,0:T(8,128)(2,1)S(1)}, bf16[256,128]{1,0:T(8,128)(2,1)S(1)}) custom-call(f32[4,512]{1,0:T(4,128)S(1)} %pad_maximum_fusion.params, bf16[4,512,128]{2,1,0:T(8,128)(2,1)S(1)} %get-tuple-element.44.kept, bf16[4,128,256]{2,1,0:T(8,128)(2,1)S(1)} %attend.3.refs_0_, ...), custom_call_target="tpu_custom_call" | custom-call | flops 1073741824 | bytes 4194304 | tf_op jit(solution)/shard_map/mlp/pallas_call | solution.py:634
  100.2 1.4 %collective-permute-start.23 = (bf16[256,128]{1,0:T(8,128)(2,1)S(1)}, bf16[256,128]{1,0:T(8,128)(2,1)S(1)}, u32[]{:S(2)}, u32[]{:S(2)}) collective-permute-start(bf16[256,128]{1,0:T(8,128)(2,1)S(1)} %get-tuple-element.52), channel_id=1, source_target_pairs={{0,3},{1,0},{2,1},{3,2},{4,7},{5,4},{6,5},{7,6},{8,11},{9,8},{10,9... | collective-permute-start | bytes 196616 | tf_op jit(solution)/shard_map/ppermute | solution.py:657
  101.6 1.9 %collective-permute-done.21.refs_1_ = bf16[256,128]{1,0:T(8,128)(2,1)S(1)} collective-permute-done((bf16[256,128]{1,0:T(8,128)(2,1)S(1)}, bf16[256,128]{1,0:T(8,128)(2,1)S(1)}, u32[]{:S(2)}, u32[]{:S(2)}) %collective-permute-start.21) | collective-permute-done | bytes 65568 | tf_op jit(solution)/shard_map/ppermute | solution.py:657
  103.4 1.3 collective-permute-done.22.refs_2_
  104.8 1.1 spread.3
  105.9 6.2 %collective-permute-start.30 = (bf16[512,128]{1,0:T(8,128)(2,1)S(1)}, bf16[512,128]{1,0:T(8,128)(2,1)S(1)}, u32[]{:S(2)}, u32[]{:S(2)}) collective-permute-start(bf16[512,128]{1,0:T(8,128)(2,1)S(1)} %get-tuple-element.62), channel_id=1, source_target_pairs={{0,4},{4,8},{8,12},{12,0},{1,5},{5,9},{9,13},{13,1},{2,6},{6,10},{... | collective-permute-start | bytes 393224 | tf_op jit(solution)/shard_map/ppermute | solution.py:657
  112.5 2.0 %collective-permute-start.32 = (bf16[512,128]{1,0:T(8,128)(2,1)S(1)}, bf16[512,128]{1,0:T(8,128)(2,1)S(1)}, u32[]{:S(2)}, u32[]{:S(2)}) collective-permute-start(bf16[512,128]{1,0:T(8,128)(2,1)S(1)} %get-tuple-element.64), channel_id=1, source_target_pairs={{0,12},{4,0},{8,4},{12,8},{1,13},{5,1},{9,5},{13,9},{2,14},{6,2},{... | collective-permute-start | bytes 393224 | tf_op jit(solution)/shard_map/ppermute | solution.py:657
  115.7 2.5 %collective-permute-start.25 = (bf16[512,128]{1,0:T(8,128)(2,1)S(1)}, bf16[512,128]{1,0:T(8,128)(2,1)S(1)}, u32[]{:S(2)}, u32[]{:S(2)}) collective-permute-start(bf16[512,128]{1,0:T(8,128)(2,1)S(1)} %get-tuple-element.55), channel_id=1, source_target_pairs={{0,8},{4,12},{8,0},{12,4},{1,9},{5,13},{9,1},{13,5},{2,10},{6,14},... | collective-permute-start | bytes 393224 | tf_op jit(solution)/shard_map/ppermute | solution.py:657
  118.2 1.3 collective-permute-start.26
  119.5 2.6 %collective-permute-done.31.refs_6_ = bf16[512,128]{1,0:T(8,128)(2,1)S(1)} collective-permute-done((bf16[512,128]{1,0:T(8,128)(2,1)S(1)}, bf16[512,128]{1,0:T(8,128)(2,1)S(1)}, u32[]{:S(2)}, u32[]{:S(2)}) %collective-permute-start.31) | collective-permute-done | bytes 131104 | tf_op jit(solution)/shard_map/ppermute | solution.py:657
  122.0 2.8 %collective-permute-done.24.refs_1_ = bf16[512,128]{1,0:T(8,128)(2,1)S(1)} collective-permute-done((bf16[512,128]{1,0:T(8,128)(2,1)S(1)}, bf16[512,128]{1,0:T(8,128)(2,1)S(1)}, u32[]{:S(2)}, u32[]{:S(2)}) %collective-permute-start.24) | collective-permute-done | bytes 131104 | tf_op jit(solution)/shard_map/ppermute | solution.py:657
  124.9 8.2 %collective-permute-done.25.refs_2_ = bf16[512,128]{1,0:T(8,128)(2,1)S(1)} collective-permute-done((bf16[512,128]{1,0:T(8,128)(2,1)S(1)}, bf16[512,128]{1,0:T(8,128)(2,1)S(1)}, u32[]{:S(2)}, u32[]{:S(2)}) %collective-permute-start.25) | collective-permute-done | bytes 131104 | tf_op jit(solution)/shard_map/ppermute | solution.py:657
  133.1 4.9 %unpack.1 = bf16[3068,128]{1,0:T(8,128)(2,1)} custom-call(s32[1]{0:T(128)S(6)} %copy.16.held, s32[1,3072]{1,0:T(1,128)S(1)} %copy-done.4, bf16[512,128]{1,0:T(8,128)(2,1)S(1)} %get-tuple-element.53.refs_0_, bf16[512,128]{1,0:T(8,128)(2,1)S(1)} %collective-permute-done.24.refs_1_, bf16[512,128]{1,0:T(8,128)(2,1)S(1)} %collective-permute-done.25.refs_2_, ...), custom_call_target="tpu_custom_call" | custom-call | tf_op jit(solution)/shard_map/unpack/pallas_call | solution.py:322
  (79 shorter events, 7.7 us)
Async XLA Ops:
  0.1 35.7 %collective-permute-start.7 = (bf16[3,512,128]{2,1,0:T(8,128)(2,1)}, bf16[3,512,128]{2,1,0:T(8,128)(2,1)S(1)}, u32[]{:S(2)}, u32[]{:S(2)}) collective-permute-start(bf16[3,512,128]{2,1,0:T(8,128)(2,1)} %refs_4_.1), channel_id=1, source_target_pairs={{0,2},{1,3},{2,0},{3,1},{4,6},{5,7},{6,4},{7,5},{8,10},{9,11},{10,... | collective-permute-start | bytes 1179656 | tf_op jit(solution)/shard_map/ppermute | solution.py:683
  3.1 34.8 %collective-permute-start.6 = (bf16[3,512,128]{2,1,0:T(8,128)(2,1)}, bf16[3,512,128]{2,1,0:T(8,128)(2,1)S(1)}, u32[]{:S(2)}, u32[]{:S(2)}) collective-permute-start(bf16[3,512,128]{2,1,0:T(8,128)(2,1)} %refs_4_.1), channel_id=1, source_target_pairs={{0,1},{1,0},{2,3},{3,2},{4,5},{5,4},{6,7},{7,6},{8,9},{9,8},{10,11... | collective-permute-start | bytes 1179656 | tf_op jit(solution)/shard_map/ppermute | solution.py:689
  11.0 11.4 %collective-permute-start = (bf16[1024,128]{1,0:T(8,128)(2,1)}, bf16[1024,128]{1,0:T(8,128)(2,1)S(1)}, u32[]{:S(2)}, u32[]{:S(2)}) collective-permute-start(bf16[1024,128]{1,0:T(8,128)(2,1)} %get-tuple-element.39), channel_id=1, source_target_pairs={{0,4},{4,8},{8,12},{12,0},{1,5},{5,9},{9,13},{13,1},{2,6},{6,10},{... | collective-permute-start | bytes 786440 | tf_op jit(solution)/shard_map/ppermute | solution.py:657
  12.1 21.1 %collective-permute-start.1 = (bf16[1024,128]{1,0:T(8,128)(2,1)}, bf16[1024,128]{1,0:T(8,128)(2,1)S(1)}, u32[]{:S(2)}, u32[]{:S(2)}) collective-permute-start(bf16[1024,128]{1,0:T(8,128)(2,1)} %get-tuple-element.40), channel_id=1, source_target_pairs={{0,8},{4,12},{8,0},{12,4},{1,9},{5,13},{9,1},{13,5},{2,10},{6,14},... | collective-permute-start | bytes 786440 | tf_op jit(solution)/shard_map/ppermute | solution.py:657
  13.5 19.6 %collective-permute-start.2 = (bf16[1024,128]{1,0:T(8,128)(2,1)}, bf16[1024,128]{1,0:T(8,128)(2,1)S(1)}, u32[]{:S(2)}, u32[]{:S(2)}) collective-permute-start(bf16[1024,128]{1,0:T(8,128)(2,1)} %get-tuple-element.41), channel_id=1, source_target_pairs={{0,12},{4,0},{8,4},{12,8},{1,13},{5,1},{9,5},{13,9},{2,14},{6,2},{... | collective-permute-start | bytes 786440 | tf_op jit(solution)/shard_map/ppermute | solution.py:657
  35.7 9.2 %collective-permute-start.4 = (bf16[1024,128]{1,0:T(8,128)(2,1)S(1)}, bf16[1024,128]{1,0:T(8,128)(2,1)S(1)}, u32[]{:S(2)}, u32[]{:S(2)}) collective-permute-start(bf16[1024,128]{1,0:T(8,128)(2,1)S(1)} %get-tuple-element.43), channel_id=1, source_target_pairs={{0,2},{1,3},{2,0},{3,1},{4,6},{5,7},{6,4},{7,5},{8,10},{9,11},{10,... | collective-permute-start | bytes 786440 | tf_op jit(solution)/shard_map/ppermute | solution.py:683
  35.8 10.7 %collective-permute-start.8 = (bf16[3,512,128]{2,1,0:T(8,128)(2,1)S(1)}, bf16[3,512,128]{2,1,0:T(8,128)(2,1)S(1)}, u32[]{:S(2)}, u32[]{:S(2)}) collective-permute-start(bf16[3,512,128]{2,1,0:T(8,128)(2,1)S(1)} %collective-permute-done.7.refs_6_), channel_id=1, source_target_pairs={{0,1},{1,0},{2,3},{3,2},{4,5},{5,4},{6,7},{7,6},{8,9},{9,8},{10,11... | collective-permute-start | bytes 1179656 | tf_op jit(solution)/shard_map/ppermute | solution.py:689
  35.8 30.8 %collective-permute-start.13 = (bf16[512,512]{1,0:T(8,128)(2,1)S(1)}, bf16[512,512]{1,0:T(8,128)(2,1)S(1)}, u32[]{:S(2)}, u32[]{:S(2)}) collective-permute-start(bf16[512,512]{1,0:T(8,128)(2,1)S(1)} %copy-done), channel_id=1, source_target_pairs={{0,2},{1,3},{2,0},{3,1},{4,6},{5,7},{6,4},{7,5},{8,10},{9,11},{10,... | collective-permute-start | bytes 1572872 | tf_op jit(solution)/shard_map/ppermute | solution.py:683
  37.8 28.9 %collective-permute-start.16 = (bf16[512,512]{1,0:T(8,128)(2,1)S(1)}, bf16[512,512]{1,0:T(8,128)(2,1)S(1)}, u32[]{:S(2)}, u32[]{:S(2)}) collective-permute-start(bf16[512,512]{1,0:T(8,128)(2,1)S(1)} %copy-done.1), channel_id=1, source_target_pairs={{0,2},{1,3},{2,0},{3,1},{4,6},{5,7},{6,4},{7,5},{8,10},{9,11},{10,... | collective-permute-start | bytes 1572872 | tf_op jit(solution)/shard_map/ppermute | solution.py:683
  37.9 7.0 %collective-permute-start.3 = (bf16[1024,128]{1,0:T(8,128)(2,1)S(1)}, bf16[1024,128]{1,0:T(8,128)(2,1)S(1)}, u32[]{:S(2)}, u32[]{:S(2)}) collective-permute-start(bf16[1024,128]{1,0:T(8,128)(2,1)S(1)} %get-tuple-element.42.refs_0_), channel_id=1, source_target_pairs={{0,1},{1,0},{2,3},{3,2},{4,5},{5,4},{6,7},{7,6},{8,9},{9,8},{10,11... | collective-permute-start | bytes 786440 | tf_op jit(solution)/shard_map/ppermute | solution.py:689
  45.0 6.4 %collective-permute-start.18 = (f32[1,768]{1,0:T(1,128)S(1)}, f32[1,768]{1,0:T(1,128)S(1)}, u32[]{:S(2)}, u32[]{:S(2)}) collective-permute-start(f32[1,768]{1,0:T(1,128)S(1)} %broadcast_in_dim.8.refs_13_.refs_14_), channel_id=1, source_target_pairs={{0,1},{1,0},{2,3},{3,2},{4,5},{5,4},{6,7},{7,6},{8,9},{9,8},{10,11... | collective-permute-start | bytes 9224 | tf_op jit(solution)/shard_map/ppermute | solution.py:755
  46.4 19.7 %collective-permute-start.19 = (f32[1,768]{1,0:T(1,128)S(1)}, f32[1,768]{1,0:T(1,128)S(1)}, u32[]{:S(2)}, u32[]{:S(2)}) collective-permute-start(f32[1,768]{1,0:T(1,128)S(1)} %broadcast_in_dim.8.refs_13_.refs_14_), channel_id=1, source_target_pairs={{0,2},{1,3},{2,0},{3,1},{4,6},{5,7},{6,4},{7,5},{8,10},{9,11},{10,... | collective-permute-start | bytes 9224 | tf_op jit(solution)/shard_map/ppermute | solution.py:755
  46.5 19.6 %collective-permute-start.20 = (f32[1,768]{1,0:T(1,128)S(1)}, f32[1,768]{1,0:T(1,128)S(1)}, u32[]{:S(2)}, u32[]{:S(2)}) collective-permute-start(f32[1,768]{1,0:T(1,128)S(1)} %broadcast_in_dim.8.refs_13_.refs_14_), channel_id=1, source_target_pairs={{0,3},{1,2},{2,1},{3,0},{4,7},{5,6},{6,5},{7,4},{8,11},{9,10},{10,... | collective-permute-start | bytes 9224 | tf_op jit(solution)/shard_map/ppermute | solution.py:755
  51.4 40.4 %collective-permute-start.12 = (bf16[512,512]{1,0:T(8,128)(2,1)S(1)}, bf16[512,512]{1,0:T(8,128)(2,1)S(1)}, u32[]{:S(2)}, u32[]{:S(2)}) collective-permute-start(bf16[512,512]{1,0:T(8,128)(2,1)S(1)} %copy-done), channel_id=1, source_target_pairs={{0,1},{1,0},{2,3},{3,2},{4,5},{5,4},{6,7},{7,6},{8,9},{9,8},{10,11... | collective-permute-start | bytes 1572872 | tf_op jit(solution)/shard_map/ppermute | solution.py:689
  66.1 25.7 %collective-permute-start.15 = (bf16[512,512]{1,0:T(8,128)(2,1)S(1)}, bf16[512,512]{1,0:T(8,128)(2,1)S(1)}, u32[]{:S(2)}, u32[]{:S(2)}) collective-permute-start(bf16[512,512]{1,0:T(8,128)(2,1)S(1)} %copy-done.1), channel_id=1, source_target_pairs={{0,1},{1,0},{2,3},{3,2},{4,5},{5,4},{6,7},{7,6},{8,9},{9,8},{10,11... | collective-permute-start | bytes 1572872 | tf_op jit(solution)/shard_map/ppermute | solution.py:689
  66.1 12.3 %collective-permute-start.10 = (bf16[512,128]{1,0:T(8,128)(2,1)S(1)}, bf16[512,128]{1,0:T(8,128)(2,1)S(1)}, u32[]{:S(2)}, u32[]{:S(2)}) collective-permute-start(bf16[512,128]{1,0:T(8,128)(2,1)S(1)} %copy-done.2), channel_id=1, source_target_pairs={{0,2},{1,3},{2,0},{3,1},{4,6},{5,7},{6,4},{7,5},{8,10},{9,11},{10,... | collective-permute-start | bytes 393224 | tf_op jit(solution)/shard_map/ppermute | solution.py:683
  66.6 25.2 %collective-permute-start.14 = (bf16[512,512]{1,0:T(8,128)(2,1)S(1)}, bf16[512,512]{1,0:T(8,128)(2,1)S(1)}, u32[]{:S(2)}, u32[]{:S(2)}) collective-permute-start(bf16[512,512]{1,0:T(8,128)(2,1)S(1)} %collective-permute-done.13.refs_7_.refs_8_), channel_id=1, source_target_pairs={{0,1},{1,0},{2,3},{3,2},{4,5},{5,4},{6,7},{7,6},{8,9},{9,8},{10,11... | collective-permute-start | bytes 1572872 | tf_op jit(solution)/shard_map/ppermute | solution.py:689
  66.8 25.0 %collective-permute-start.17 = (bf16[512,512]{1,0:T(8,128)(2,1)S(1)}, bf16[512,512]{1,0:T(8,128)(2,1)S(1)}, u32[]{:S(2)}, u32[]{:S(2)}) collective-permute-start(bf16[512,512]{1,0:T(8,128)(2,1)S(1)} %collective-permute-done.16.refs_11_.refs_12_), channel_id=1, source_target_pairs={{0,1},{1,0},{2,3},{3,2},{4,5},{5,4},{6,7},{7,6},{8,9},{9,8},{10,11... | collective-permute-start | bytes 1572872 | tf_op jit(solution)/shard_map/ppermute | solution.py:689
  78.5 6.5 %collective-permute-start.9 = (bf16[512,128]{1,0:T(8,128)(2,1)S(1)}, bf16[512,128]{1,0:T(8,128)(2,1)S(1)}, u32[]{:S(2)}, u32[]{:S(2)}) collective-permute-start(bf16[512,128]{1,0:T(8,128)(2,1)S(1)} %copy-done.2), channel_id=1, source_target_pairs={{0,1},{1,0},{2,3},{3,2},{4,5},{5,4},{6,7},{7,6},{8,9},{9,8},{10,11... | collective-permute-start | bytes 393224 | tf_op jit(solution)/shard_map/ppermute | solution.py:689
  84.9 6.8 %collective-permute-start.11 = (bf16[512,128]{1,0:T(8,128)(2,1)S(1)}, bf16[512,128]{1,0:T(8,128)(2,1)S(1)}, u32[]{:S(2)}, u32[]{:S(2)}) collective-permute-start(bf16[512,128]{1,0:T(8,128)(2,1)S(1)} %collective-permute-done.10.refs_3_.refs_4_), channel_id=1, source_target_pairs={{0,1},{1,0},{2,3},{3,2},{4,5},{5,4},{6,7},{7,6},{8,9},{9,8},{10,11... | collective-permute-start | bytes 393224 | tf_op jit(solution)/shard_map/ppermute | solution.py:689
  94.1 6.0 %collective-permute-start.27 = (bf16[256,128]{1,0:T(8,128)(2,1)S(1)}, bf16[256,128]{1,0:T(8,128)(2,1)S(1)}, u32[]{:S(2)}, u32[]{:S(2)}) collective-permute-start(bf16[256,128]{1,0:T(8,128)(2,1)S(1)} %get-tuple-element.58), channel_id=1, source_target_pairs={{0,1},{1,2},{2,3},{3,0},{4,5},{5,6},{6,7},{7,4},{8,9},{9,10},{10,1... | collective-permute-start | bytes 196616 | tf_op jit(solution)/shard_map/ppermute | solution.py:657
  94.3 7.2 %collective-permute-start.28 = (bf16[256,128]{1,0:T(8,128)(2,1)S(1)}, bf16[256,128]{1,0:T(8,128)(2,1)S(1)}, u32[]{:S(2)}, u32[]{:S(2)}) collective-permute-start(bf16[256,128]{1,0:T(8,128)(2,1)S(1)} %get-tuple-element.59), channel_id=1, source_target_pairs={{0,2},{1,3},{2,0},{3,1},{4,6},{5,7},{6,4},{7,5},{8,10},{9,11},{10,... | collective-permute-start | bytes 196616 | tf_op jit(solution)/shard_map/ppermute | solution.py:657
  96.0 5.6 %collective-permute-start.29 = (bf16[256,128]{1,0:T(8,128)(2,1)S(1)}, bf16[256,128]{1,0:T(8,128)(2,1)S(1)}, u32[]{:S(2)}, u32[]{:S(2)}) collective-permute-start(bf16[256,128]{1,0:T(8,128)(2,1)S(1)} %get-tuple-element.60), channel_id=1, source_target_pairs={{0,3},{1,0},{2,1},{3,2},{4,7},{5,4},{6,5},{7,6},{8,11},{9,8},{10,9... | collective-permute-start | bytes 196616 | tf_op jit(solution)/shard_map/ppermute | solution.py:657
  99.7 3.8 %collective-permute-start.21 = (bf16[256,128]{1,0:T(8,128)(2,1)S(1)}, bf16[256,128]{1,0:T(8,128)(2,1)S(1)}, u32[]{:S(2)}, u32[]{:S(2)}) collective-permute-start(bf16[256,128]{1,0:T(8,128)(2,1)S(1)} %get-tuple-element.50), channel_id=1, source_target_pairs={{0,1},{1,2},{2,3},{3,0},{4,5},{5,6},{6,7},{7,4},{8,9},{9,10},{10,1... | collective-permute-start | bytes 196616 | tf_op jit(solution)/shard_map/ppermute | solution.py:657
  99.7 5.0 %collective-permute-start.22 = (bf16[256,128]{1,0:T(8,128)(2,1)S(1)}, bf16[256,128]{1,0:T(8,128)(2,1)S(1)}, u32[]{:S(2)}, u32[]{:S(2)}) collective-permute-start(bf16[256,128]{1,0:T(8,128)(2,1)S(1)} %get-tuple-element.51), channel_id=1, source_target_pairs={{0,2},{1,3},{2,0},{3,1},{4,6},{5,7},{6,4},{7,5},{8,10},{9,11},{10,... | collective-permute-start | bytes 196616 | tf_op jit(solution)/shard_map/ppermute | solution.py:657
  100.2 4.6 %collective-permute-start.23 = (bf16[256,128]{1,0:T(8,128)(2,1)S(1)}, bf16[256,128]{1,0:T(8,128)(2,1)S(1)}, u32[]{:S(2)}, u32[]{:S(2)}) collective-permute-start(bf16[256,128]{1,0:T(8,128)(2,1)S(1)} %get-tuple-element.52), channel_id=1, source_target_pairs={{0,3},{1,0},{2,1},{3,2},{4,7},{5,4},{6,5},{7,6},{8,11},{9,8},{10,9... | collective-permute-start | bytes 196616 | tf_op jit(solution)/shard_map/ppermute | solution.py:657
  105.9 12.3 %collective-permute-start.30 = (bf16[512,128]{1,0:T(8,128)(2,1)S(1)}, bf16[512,128]{1,0:T(8,128)(2,1)S(1)}, u32[]{:S(2)}, u32[]{:S(2)}) collective-permute-start(bf16[512,128]{1,0:T(8,128)(2,1)S(1)} %get-tuple-element.62), channel_id=1, source_target_pairs={{0,4},{4,8},{8,12},{12,0},{1,5},{5,9},{9,13},{13,1},{2,6},{6,10},{... | collective-permute-start | bytes 393224 | tf_op jit(solution)/shard_map/ppermute | solution.py:657
  112.1 9.9 %collective-permute-start.31 = (bf16[512,128]{1,0:T(8,128)(2,1)S(1)}, bf16[512,128]{1,0:T(8,128)(2,1)S(1)}, u32[]{:S(2)}, u32[]{:S(2)}) collective-permute-start(bf16[512,128]{1,0:T(8,128)(2,1)S(1)} %get-tuple-element.63), channel_id=1, source_target_pairs={{0,8},{4,12},{8,0},{12,4},{1,9},{5,13},{9,1},{13,5},{2,10},{6,14},... | collective-permute-start | bytes 393224 | tf_op jit(solution)/shard_map/ppermute | solution.py:657
  112.5 9.5 %collective-permute-start.32 = (bf16[512,128]{1,0:T(8,128)(2,1)S(1)}, bf16[512,128]{1,0:T(8,128)(2,1)S(1)}, u32[]{:S(2)}, u32[]{:S(2)}) collective-permute-start(bf16[512,128]{1,0:T(8,128)(2,1)S(1)} %get-tuple-element.64), channel_id=1, source_target_pairs={{0,12},{4,0},{8,4},{12,8},{1,13},{5,1},{9,5},{13,9},{2,14},{6,2},{... | collective-permute-start | bytes 393224 | tf_op jit(solution)/shard_map/ppermute | solution.py:657
  115.6 9.3 %collective-permute-start.24 = (bf16[512,128]{1,0:T(8,128)(2,1)S(1)}, bf16[512,128]{1,0:T(8,128)(2,1)S(1)}, u32[]{:S(2)}, u32[]{:S(2)}) collective-permute-start(bf16[512,128]{1,0:T(8,128)(2,1)S(1)} %get-tuple-element.54), channel_id=1, source_target_pairs={{0,4},{4,8},{8,12},{12,0},{1,5},{5,9},{9,13},{13,1},{2,6},{6,10},{... | collective-permute-start | bytes 393224 | tf_op jit(solution)/shard_map/ppermute | solution.py:657
  115.7 17.4 %collective-permute-start.25 = (bf16[512,128]{1,0:T(8,128)(2,1)S(1)}, bf16[512,128]{1,0:T(8,128)(2,1)S(1)}, u32[]{:S(2)}, u32[]{:S(2)}) collective-permute-start(bf16[512,128]{1,0:T(8,128)(2,1)S(1)} %get-tuple-element.55), channel_id=1, source_target_pairs={{0,8},{4,12},{8,0},{12,4},{1,9},{5,13},{9,1},{13,5},{2,10},{6,14},... | collective-permute-start | bytes 393224 | tf_op jit(solution)/shard_map/ppermute | solution.py:657
  118.2 15.0 %collective-permute-start.26 = (bf16[512,128]{1,0:T(8,128)(2,1)S(1)}, bf16[512,128]{1,0:T(8,128)(2,1)S(1)}, u32[]{:S(2)}, u32[]{:S(2)}) collective-permute-start(bf16[512,128]{1,0:T(8,128)(2,1)S(1)} %get-tuple-element.56), channel_id=1, source_target_pairs={{0,12},{4,0},{8,4},{12,8},{1,13},{5,1},{9,5},{13,9},{2,14},{6,2},{... | collective-permute-start | bytes 393224 | tf_op jit(solution)/shard_map/ppermute | solution.py:657
  (15 other events, 403.4 us)

commit v3 on v2

--- a/solution.py
+++ b/solution.py
@@ -11,7 +11,7 @@
 PATCH = 1024
 HEAD_DIM = 16
 LANES = 128
-ROW_STEP = 64
+ROW_STEP = 128
 TILE = 512
 FAST_TILE = 256
 AHEAD = 4
@@ -128,13 +128,15 @@
         ].astype(F32)
     to_smem.wait()
 
+    stride = slots // ROW_STEP
+
     def place_rows(i, carry):
-        base = pl.multiple_of(i * ROW_STEP, ROW_STEP)
         for k in range(ROW_STEP):
-            packed[pl.ds(place_smem[0, base + k], 1), :] = wide[pl.ds(base + k, 1), :]
+            target = place_smem.at[:, pl.ds(k * stride, stride)][0, i]
+            packed[pl.ds(target, 1), :] = wide.at[pl.ds(k * stride, stride)][pl.ds(i, 1), :]
         return carry
 
-    lax.fori_loop(0, (count + ROW_STEP - 1) // ROW_STEP, place_rows, 0)
+    lax.fori_loop(0, stride, place_rows, 0)
     for k in range(shards):
         at = pl.multiple_of(lax.rem(here + k, shards) * cap, cap)
         convert_rows(packed, at, sends[k], 0, cap)
@@ -161,6 +163,21 @@
         ],
         name="pack",
     )(held, rank, z_feat)
+
+
+def keep_kernel(block, out):
+    out[...] = block[...]
+
+
+def keep(block):
+    return pl.pallas_call(
+        keep_kernel,
+        out_shape=jax.ShapeDtypeStruct(block.shape, block.dtype),
+        in_specs=[VMEM],
+        out_specs=VMEM,
+        compiler_params=grant(2),
+        name="keep",
+    )(block)
 
 
 def move_segment(source, source_at, target, target_at, length):
@@ -290,13 +307,15 @@
             at = lax.rem(here - k + shards, shards) * cap + half * size
             convert_rows(blocks[half * shards + k], 0, wide, pl.multiple_of(at, size), size)
 
+    stride = picked.shape[0] // ROW_STEP
+
     def pick_rows(i, carry):
-        base = pl.multiple_of(i * ROW_STEP, ROW_STEP)
         for k in range(ROW_STEP):
-            picked[pl.ds(base + k, 1), :] = wide[pl.ds(place[0, base + k], 1), :]
+            source = place.at[:, pl.ds(k * stride, stride)][0, i]
+            picked.at[pl.ds(k * stride, stride)][pl.ds(i, 1), :] = wide[pl.ds(source, 1), :]
         return carry
 
-    lax.fori_loop(0, (count + ROW_STEP - 1) // ROW_STEP, pick_rows, 0)
+    lax.fori_loop(0, stride, pick_rows, 0)
 
     def masked(at, rows):
         slot = at + lax.broadcasted_iota(I32, (rows, width), 0)
@@ -767,6 +786,7 @@
     params = jnp.stack([ln1_gain, ln1_bias, ln2_gain, ln2_bias])
     pieces, params = lax.optimization_barrier((pieces, params))
     arrived = exchange(sends, "pts", shards)
+    arrived[0] = keep(arrived[0])
     patch_blocks = compact(pieces, arrived, patches, group)
     feats = gather_members(patch_blocks, patches, group)
 

time: 139 us -> 137 us (0.986)
  Pallas kernels: 47.8 us -> 46.1 us
  starting transfers between devices: 31.8 us -> 33.4 us
  waiting for transfers between devices: 56.1 us -> 54.7 us
    ppermute x15, waiting for transfers between devices: 34.3 us -> 32.9 us  [shift(): lax.ppermute(array, axis, [(i, (i + step) % size) for i in range(size)])]
  transfers between devices with their start and end apart: 33 -> 33, of which waited for: 10 -> 10; matrix products, arithmetic and copies ran while one was open for 0% -> 0% of each run, Pallas kernels for 29% -> 28%
where the time goes in v3:
time: 137 us; the launch traced here: 136 us
  waiting for transfers between devices  54.7 us (40%)
  Pallas kernels  46.1 us (34%)
  starting transfers between devices  33.4 us (24%)
    ppermute x15, waiting for transfers between devices, shift(): lax.ppermute(array, axis, [(i, (i + step) % size) for i in range(size)])  32.9 us
    pallas_call x3, Pallas kernels, attend(): pl.pallas_call(functools.partial(attend_kernel, low, high, half, min(TILE...  23.9 us
    ppermute x15, starting transfers between devices, shift(): lax.ppermute(array, axis, [(i, (i + step) % size) for i in range(size)])  23.2 us
    ppermute x3, waiting for transfers between devices, body(): vectors.append(lax.ppermute(vector, 'head', pairs))  14.4 us
    ppermute x5, waiting for transfers between devices, group_shift(): return lax.ppermute(array, 'head', pairs)  6.54 us
    ppermute x5, starting transfers between devices, group_shift(): return lax.ppermute(array, 'head', pairs)  6.34 us
    pallas_call x1, Pallas kernels, pack(): pl.pallas_call(functools.partial(pack_kernel, shards, cap, rows_here, col...  6.33 us
    pallas_call x2, Pallas kernels, mlp(): pl.pallas_call(functools.partial(mlp_kernel, blocks, members, patches, se...  4.67 us
  transfers between devices with their start and end apart: 33, of which 10 were waited for; matrix products, arithmetic and copies ran while one was open for 0% of the time, Pallas kernels for 28%

profile of v3, /device:TPU:0, one launch (start us, length us, event | category | flops | bytes accessed | tf_op | source)
XLA Modules:
  0.0 136.4 jit_solution(15266348383006988007)
XLA Ops:
  0.1 3.0 %collective-permute-start.7 = (bf16[3,512,128]{2,1,0:T(8,128)(2,1)}, bf16[3,512,128]{2,1,0:T(8,128)(2,1)S(1)}, u32[]{:S(2)}, u32[]{:S(2)}) collective-permute-start(bf16[3,512,128]{2,1,0:T(8,128)(2,1)} %refs_4_.1), channel_id=1, source_target_pairs={{0,2},{1,3},{2,0},{3,1},{4,6},{5,7},{6,4},{7,5},{8,10},{9,11},{10,... | collective-permute-start | bytes 1179656 | tf_op jit(solution)/shard_map/ppermute | solution.py:702
  3.8 6.3 %pack.1 = (bf16[1024,128]{1,0:T(8,128)(2,1)}, bf16[1024,128]{1,0:T(8,128)(2,1)}, bf16[1024,128]{1,0:T(8,128)(2,1)}, bf16[1024,128]{1,0:T(8,128)(2,1)}, s32[1,3072]{1,0:T(1,128)}) custom-call(s32[1]{0:T(128)S(6)} %copy.16.held, s32[1,3068]{1,0:T(1,128)} %bitcast.5, bf16[3068,512]{1,0:T(8,128)(2,1)} %z_feat.1), custom_call_target="tpu_custom_call" | custom-call | tf_op jit(solution)/shard_map/pack/pallas_call | solution.py:149
  10.1 1.6 %collective-permute-start = (bf16[1024,128]{1,0:T(8,128)(2,1)}, bf16[1024,128]{1,0:T(8,128)(2,1)S(1)}, u32[]{:S(2)}, u32[]{:S(2)}) collective-permute-start(bf16[1024,128]{1,0:T(8,128)(2,1)} %get-tuple-element.39), channel_id=1, source_target_pairs={{0,4},{4,8},{8,12},{12,0},{1,5},{5,9},{9,13},{13,1},{2,6},{6,10},{... | collective-permute-start | bytes 786440 | tf_op jit(solution)/shard_map/ppermute | solution.py:676
  11.7 2.6 %collective-permute-start.1 = (bf16[1024,128]{1,0:T(8,128)(2,1)}, bf16[1024,128]{1,0:T(8,128)(2,1)S(1)}, u32[]{:S(2)}, u32[]{:S(2)}) collective-permute-start(bf16[1024,128]{1,0:T(8,128)(2,1)} %get-tuple-element.40), channel_id=1, source_target_pairs={{0,8},{4,12},{8,0},{12,4},{1,9},{5,13},{9,1},{13,5},{2,10},{6,14},... | collective-permute-start | bytes 786440 | tf_op jit(solution)/shard_map/ppermute | solution.py:676
  14.3 1.3 collective-permute-start.2
  16.9 4.6 %collective-permute-done.refs_1_ = bf16[1024,128]{1,0:T(8,128)(2,1)S(1)} collective-permute-done((bf16[1024,128]{1,0:T(8,128)(2,1)}, bf16[1024,128]{1,0:T(8,128)(2,1)S(1)}, u32[]{:S(2)}, u32[]{:S(2)}) %collective-permute-start) | collective-permute-done | bytes 262176 | tf_op jit(solution)/shard_map/ppermute | solution.py:676
  21.5 10.8 %collective-permute-done.1.refs_2_ = bf16[1024,128]{1,0:T(8,128)(2,1)S(1)} collective-permute-done((bf16[1024,128]{1,0:T(8,128)(2,1)}, bf16[1024,128]{1,0:T(8,128)(2,1)S(1)}, u32[]{:S(2)}, u32[]{:S(2)}) %collective-permute-start.1) | collective-permute-done | bytes 262176 | tf_op jit(solution)/shard_map/ppermute | solution.py:676
  32.3 1.5 %compact.1 = (bf16[1024,128]{1,0:T(8,128)(2,1)S(1)}, bf16[1024,128]{1,0:T(8,128)(2,1)S(1)}) custom-call(s32[2,4]{1,0:T(2,128)S(1)} %convert_reduce_fusion.pieces, bf16[1024,128]{1,0:T(8,128)(2,1)S(1)} %keep.1.refs_0_, bf16[1024,128]{1,0:T(8,128)(2,1)S(1)} %collective-permute-done.refs_1_, bf16[1024,128]{1,0:T(8,128)(2,1)S(1)} %collective-permute-done.1.refs_2_, ...), custom_call_target="tpu_custom_call" | custom-call | tf_op jit(solution)/shard_map/compact/pallas_call | solution.py:237
  34.5 1.6 %collective-permute-start.13 = (bf16[512,512]{1,0:T(8,128)(2,1)S(1)}, bf16[512,512]{1,0:T(8,128)(2,1)S(1)}, u32[]{:S(2)}, u32[]{:S(2)}) collective-permute-start(bf16[512,512]{1,0:T(8,128)(2,1)S(1)} %copy-done), channel_id=1, source_target_pairs={{0,2},{1,3},{2,0},{3,1},{4,6},{5,7},{6,4},{7,5},{8,10},{9,11},{10,... | collective-permute-start | bytes 1572872 | tf_op jit(solution)/shard_map/ppermute | solution.py:702
  36.6 6.5 %collective-permute-done.4.refs_2_ = bf16[1024,128]{1,0:T(8,128)(2,1)S(1)} collective-permute-done((bf16[1024,128]{1,0:T(8,128)(2,1)S(1)}, bf16[1024,128]{1,0:T(8,128)(2,1)S(1)}, u32[]{:S(2)}, u32[]{:S(2)}) %collective-permute-start.4) | collective-permute-done | bytes 262176 | tf_op jit(solution)/shard_map/ppermute | solution.py:702
  46.1 3.5 %project.1 = (bf16[4,1024,128]{2,1,0:T(8,128)(2,1)S(1)}, bf16[4,128,1024]{2,1,0:T(8,128)(2,1)S(1)}, bf16[4,512,128]{2,1,0:T(8,128)(2,1)S(1)}, bf16[4,512,128]{2,1,0:T(8,128)(2,1)S(1)}, s32[1]{0:T(128)}) custom-call(f32[4,512]{1,0:T(4,128)S(1)} %pad_maximum_fusion.params, bf16[1024,128]{1,0:T(8,128)(2,1)S(1)} %get-tuple-element.42.refs_0_, ...), custom_call_target="tpu_custom_call" | custom-call | flops 1610612736 | bytes 4194304 | tf_op jit(solution)/shard_map/project/pallas_call | solution.py:449
  50.3 14.4 %collective-permute-done.19.refs_15_.refs_16_ = f32[1,768]{1,0:T(1,128)S(1)} collective-permute-done((f32[1,768]{1,0:T(1,128)S(1)}, f32[1,768]{1,0:T(1,128)S(1)}, u32[]{:S(2)}, u32[]{:S(2)}) %collective-permute-start.19) | collective-permute-done | bytes 3104 | tf_op jit(solution)/shard_map/ppermute | solution.py:774
  65.8 11.3 %attend.3.refs_0_ = bf16[4,128,256]{2,1,0:T(8,128)(2,1)S(1)} custom-call(s32[1]{0:T(128)} %get-tuple-element.45.small, bf16[4,1024,128]{2,1,0:T(8,128)(2,1)S(1)} %get-tuple-element.46.keys, bf16[4,128,1024]{2,1,0:T(8,128)(2,1)S(1)} %get-tuple-element.47.values, bf16[4,512,128]{2,1,0:T(8,128)(2,1)S(1)} %get-tuple-element.48.query), custom_call_target="tpu_custom_call" | custom-call | flops 4294967296 | bytes 2097152 | tf_op jit(solution)/shard_map/attend/pallas_call | solution.py:573
  77.4 6.2 %attend.5.refs_1_ = bf16[2,128,256]{2,1,0:T(8,128)(2,1)S(1)} custom-call(s32[1]{0:T(128)} %get-tuple-element.45.small, bf16[4,1024,128]{2,1,0:T(8,128)(2,1)S(1)} %get-tuple-element.46.keys, bf16[4,128,1024]{2,1,0:T(8,128)(2,1)S(1)} %get-tuple-element.47.values, bf16[4,512,128]{2,1,0:T(8,128)(2,1)S(1)} %get-tuple-element.48.query), custom_call_target="tpu_custom_call" | custom-call | flops 2147483648 | bytes 1048576 | tf_op jit(solution)/shard_map/attend/pallas_call | solution.py:573
  84.0 6.4 %attend.4.refs_0_ = bf16[2,128,256]{2,1,0:T(8,128)(2,1)S(1)} custom-call(s32[1]{0:T(128)} %get-tuple-element.45.small, bf16[4,1024,128]{2,1,0:T(8,128)(2,1)S(1)} %get-tuple-element.46.keys, bf16[4,128,1024]{2,1,0:T(8,128)(2,1)S(1)} %get-tuple-element.47.values, bf16[4,512,128]{2,1,0:T(8,128)(2,1)S(1)} %get-tuple-element.48.query), custom_call_target="tpu_custom_call" | custom-call | flops 2147483648 | bytes 1048576 | tf_op jit(solution)/shard_map/attend/pallas_call | solution.py:573
  90.5 2.4 %mlp.3 = (bf16[256,128]{1,0:T(8,128)(2,1)S(1)}, bf16[256,128]{1,0:T(8,128)(2,1)S(1)}, bf16[256,128]{1,0:T(8,128)(2,1)S(1)}, bf16[256,128]{1,0:T(8,128)(2,1)S(1)}) custom-call(f32[4,512]{1,0:T(4,128)S(1)} %pad_maximum_fusion.params, bf16[4,512,128]{2,1,0:T(8,128)(2,1)S(1)} %get-tuple-element.44.kept, bf16[2,128,256]{2,1,0:T(8,128)(2,1)S(1)} %attend.4.refs_0_, ...), custom_call_target="tpu_custom_call" | custom-call | flops 1073741824 | bytes 4194304 | tf_op jit(solution)/shard_map/mlp/pallas_call | solution.py:653
  93.0 1.5 %collective-permute-start.28 = (bf16[256,128]{1,0:T(8,128)(2,1)S(1)}, bf16[256,128]{1,0:T(8,128)(2,1)S(1)}, u32[]{:S(2)}, u32[]{:S(2)}) collective-permute-start(bf16[256,128]{1,0:T(8,128)(2,1)S(1)} %get-tuple-element.59), channel_id=1, source_target_pairs={{0,2},{1,3},{2,0},{3,1},{4,6},{5,7},{6,4},{7,5},{8,10},{9,11},{10,... | collective-permute-start | bytes 196616 | tf_op jit(solution)/shard_map/ppermute | solution.py:676
  94.5 1.3 collective-permute-start.29
  95.8 2.3 %mlp.2 = (bf16[256,128]{1,0:T(8,128)(2,1)S(1)}, bf16[256,128]{1,0:T(8,128)(2,1)S(1)}, bf16[256,128]{1,0:T(8,128)(2,1)S(1)}, bf16[256,128]{1,0:T(8,128)(2,1)S(1)}) custom-call(f32[4,512]{1,0:T(4,128)S(1)} %pad_maximum_fusion.params, bf16[4,512,128]{2,1,0:T(8,128)(2,1)S(1)} %get-tuple-element.44.kept, bf16[4,128,256]{2,1,0:T(8,128)(2,1)S(1)} %attend.3.refs_0_, ...), custom_call_target="tpu_custom_call" | custom-call | flops 1073741824 | bytes 4194304 | tf_op jit(solution)/shard_map/mlp/pallas_call | solution.py:653
  98.8 1.4 %collective-permute-start.23 = (bf16[256,128]{1,0:T(8,128)(2,1)S(1)}, bf16[256,128]{1,0:T(8,128)(2,1)S(1)}, u32[]{:S(2)}, u32[]{:S(2)}) collective-permute-start(bf16[256,128]{1,0:T(8,128)(2,1)S(1)} %get-tuple-element.52), channel_id=1, source_target_pairs={{0,3},{1,0},{2,1},{3,2},{4,7},{5,4},{6,5},{7,6},{8,11},{9,8},{10,9... | collective-permute-start | bytes 196616 | tf_op jit(solution)/shard_map/ppermute | solution.py:676
  100.2 1.7 %collective-permute-done.21.refs_1_ = bf16[256,128]{1,0:T(8,128)(2,1)S(1)} collective-permute-done((bf16[256,128]{1,0:T(8,128)(2,1)S(1)}, bf16[256,128]{1,0:T(8,128)(2,1)S(1)}, u32[]{:S(2)}, u32[]{:S(2)}) %collective-permute-start.21) | collective-permute-done | bytes 65568 | tf_op jit(solution)/shard_map/ppermute | solution.py:676
  101.9 1.3 collective-permute-done.22.refs_2_
  103.2 1.1 spread.3
  104.4 6.2 %collective-permute-start.30 = (bf16[512,128]{1,0:T(8,128)(2,1)S(1)}, bf16[512,128]{1,0:T(8,128)(2,1)S(1)}, u32[]{:S(2)}, u32[]{:S(2)}) collective-permute-start(bf16[512,128]{1,0:T(8,128)(2,1)S(1)} %get-tuple-element.62), channel_id=1, source_target_pairs={{0,4},{4,8},{8,12},{12,0},{1,5},{5,9},{9,13},{13,1},{2,6},{6,10},{... | collective-permute-start | bytes 393224 | tf_op jit(solution)/shard_map/ppermute | solution.py:676
  110.6 1.2 collective-permute-start.31
  111.8 1.2 collective-permute-start.32
  114.9 1.7 %collective-permute-start.25 = (bf16[512,128]{1,0:T(8,128)(2,1)S(1)}, bf16[512,128]{1,0:T(8,128)(2,1)S(1)}, u32[]{:S(2)}, u32[]{:S(2)}) collective-permute-start(bf16[512,128]{1,0:T(8,128)(2,1)S(1)} %get-tuple-element.55), channel_id=1, source_target_pairs={{0,8},{4,12},{8,0},{12,4},{1,9},{5,13},{9,1},{13,5},{2,10},{6,14},... | collective-permute-start | bytes 393224 | tf_op jit(solution)/shard_map/ppermute | solution.py:676
  116.6 1.3 collective-permute-start.26
  118.0 3.3 %collective-permute-done.31.refs_6_ = bf16[512,128]{1,0:T(8,128)(2,1)S(1)} collective-permute-done((bf16[512,128]{1,0:T(8,128)(2,1)S(1)}, bf16[512,128]{1,0:T(8,128)(2,1)S(1)}, u32[]{:S(2)}, u32[]{:S(2)}) %collective-permute-start.31) | collective-permute-done | bytes 131104 | tf_op jit(solution)/shard_map/ppermute | solution.py:676
  121.3 2.8 %collective-permute-done.24.refs_1_ = bf16[512,128]{1,0:T(8,128)(2,1)S(1)} collective-permute-done((bf16[512,128]{1,0:T(8,128)(2,1)S(1)}, bf16[512,128]{1,0:T(8,128)(2,1)S(1)}, u32[]{:S(2)}, u32[]{:S(2)}) %collective-permute-start.24) | collective-permute-done | bytes 131104 | tf_op jit(solution)/shard_map/ppermute | solution.py:676
  124.2 8.3 %collective-permute-done.25.refs_2_ = bf16[512,128]{1,0:T(8,128)(2,1)S(1)} collective-permute-done((bf16[512,128]{1,0:T(8,128)(2,1)S(1)}, bf16[512,128]{1,0:T(8,128)(2,1)S(1)}, u32[]{:S(2)}, u32[]{:S(2)}) %collective-permute-start.25) | collective-permute-done | bytes 131104 | tf_op jit(solution)/shard_map/ppermute | solution.py:676
  132.4 4.0 %unpack.1 = bf16[3068,128]{1,0:T(8,128)(2,1)} custom-call(s32[1]{0:T(128)S(6)} %copy.16.held, s32[1,3072]{1,0:T(1,128)S(1)} %copy-done.4, bf16[512,128]{1,0:T(8,128)(2,1)S(1)} %get-tuple-element.53.refs_0_, bf16[512,128]{1,0:T(8,128)(2,1)S(1)} %collective-permute-done.24.refs_1_, bf16[512,128]{1,0:T(8,128)(2,1)S(1)} %collective-permute-done.25.refs_2_, ...), custom_call_target="tpu_custom_call" | custom-call | tf_op jit(solution)/shard_map/unpack/pallas_call | solution.py:341
  (80 shorter events, 10.6 us)
Async XLA Ops:
  0.1 34.4 %collective-permute-start.7 = (bf16[3,512,128]{2,1,0:T(8,128)(2,1)}, bf16[3,512,128]{2,1,0:T(8,128)(2,1)S(1)}, u32[]{:S(2)}, u32[]{:S(2)}) collective-permute-start(bf16[3,512,128]{2,1,0:T(8,128)(2,1)} %refs_4_.1), channel_id=1, source_target_pairs={{0,2},{1,3},{2,0},{3,1},{4,6},{5,7},{6,4},{7,5},{8,10},{9,11},{10,... | collective-permute-start | bytes 1179656 | tf_op jit(solution)/shard_map/ppermute | solution.py:702
  3.1 33.4 %collective-permute-start.6 = (bf16[3,512,128]{2,1,0:T(8,128)(2,1)}, bf16[3,512,128]{2,1,0:T(8,128)(2,1)S(1)}, u32[]{:S(2)}, u32[]{:S(2)}) collective-permute-start(bf16[3,512,128]{2,1,0:T(8,128)(2,1)} %refs_4_.1), channel_id=1, source_target_pairs={{0,1},{1,0},{2,3},{3,2},{4,5},{5,4},{6,7},{7,6},{8,9},{9,8},{10,11... | collective-permute-start | bytes 1179656 | tf_op jit(solution)/shard_map/ppermute | solution.py:708
  10.1 11.4 %collective-permute-start = (bf16[1024,128]{1,0:T(8,128)(2,1)}, bf16[1024,128]{1,0:T(8,128)(2,1)S(1)}, u32[]{:S(2)}, u32[]{:S(2)}) collective-permute-start(bf16[1024,128]{1,0:T(8,128)(2,1)} %get-tuple-element.39), channel_id=1, source_target_pairs={{0,4},{4,8},{8,12},{12,0},{1,5},{5,9},{9,13},{13,1},{2,6},{6,10},{... | collective-permute-start | bytes 786440 | tf_op jit(solution)/shard_map/ppermute | solution.py:676
  11.7 20.6 %collective-permute-start.1 = (bf16[1024,128]{1,0:T(8,128)(2,1)}, bf16[1024,128]{1,0:T(8,128)(2,1)S(1)}, u32[]{:S(2)}, u32[]{:S(2)}) collective-permute-start(bf16[1024,128]{1,0:T(8,128)(2,1)} %get-tuple-element.40), channel_id=1, source_target_pairs={{0,8},{4,12},{8,0},{12,4},{1,9},{5,13},{9,1},{13,5},{2,10},{6,14},... | collective-permute-start | bytes 786440 | tf_op jit(solution)/shard_map/ppermute | solution.py:676
  14.3 18.0 %collective-permute-start.2 = (bf16[1024,128]{1,0:T(8,128)(2,1)}, bf16[1024,128]{1,0:T(8,128)(2,1)S(1)}, u32[]{:S(2)}, u32[]{:S(2)}) collective-permute-start(bf16[1024,128]{1,0:T(8,128)(2,1)} %get-tuple-element.41), channel_id=1, source_target_pairs={{0,12},{4,0},{8,4},{12,8},{1,13},{5,1},{9,5},{13,9},{2,14},{6,2},{... | collective-permute-start | bytes 786440 | tf_op jit(solution)/shard_map/ppermute | solution.py:676
  33.9 9.2 %collective-permute-start.4 = (bf16[1024,128]{1,0:T(8,128)(2,1)S(1)}, bf16[1024,128]{1,0:T(8,128)(2,1)S(1)}, u32[]{:S(2)}, u32[]{:S(2)}) collective-permute-start(bf16[1024,128]{1,0:T(8,128)(2,1)S(1)} %get-tuple-element.43), channel_id=1, source_target_pairs={{0,2},{1,3},{2,0},{3,1},{4,6},{5,7},{6,4},{7,5},{8,10},{9,11},{10,... | collective-permute-start | bytes 786440 | tf_op jit(solution)/shard_map/ppermute | solution.py:702
  34.5 10.7 %collective-permute-start.8 = (bf16[3,512,128]{2,1,0:T(8,128)(2,1)S(1)}, bf16[3,512,128]{2,1,0:T(8,128)(2,1)S(1)}, u32[]{:S(2)}, u32[]{:S(2)}) collective-permute-start(bf16[3,512,128]{2,1,0:T(8,128)(2,1)S(1)} %collective-permute-done.7.refs_6_), channel_id=1, source_target_pairs={{0,1},{1,0},{2,3},{3,2},{4,5},{5,4},{6,7},{7,6},{8,9},{9,8},{10,11... | collective-permute-start | bytes 1179656 | tf_op jit(solution)/shard_map/ppermute | solution.py:708
  34.5 30.8 %collective-permute-start.13 = (bf16[512,512]{1,0:T(8,128)(2,1)S(1)}, bf16[512,512]{1,0:T(8,128)(2,1)S(1)}, u32[]{:S(2)}, u32[]{:S(2)}) collective-permute-start(bf16[512,512]{1,0:T(8,128)(2,1)S(1)} %copy-done), channel_id=1, source_target_pairs={{0,2},{1,3},{2,0},{3,1},{4,6},{5,7},{6,4},{7,5},{8,10},{9,11},{10,... | collective-permute-start | bytes 1572872 | tf_op jit(solution)/shard_map/ppermute | solution.py:702
  36.0 29.4 %collective-permute-start.16 = (bf16[512,512]{1,0:T(8,128)(2,1)S(1)}, bf16[512,512]{1,0:T(8,128)(2,1)S(1)}, u32[]{:S(2)}, u32[]{:S(2)}) collective-permute-start(bf16[512,512]{1,0:T(8,128)(2,1)S(1)} %copy-done.1), channel_id=1, source_target_pairs={{0,2},{1,3},{2,0},{3,1},{4,6},{5,7},{6,4},{7,5},{8,10},{9,11},{10,... | collective-permute-start | bytes 1572872 | tf_op jit(solution)/shard_map/ppermute | solution.py:702
  36.6 6.6 %collective-permute-start.3 = (bf16[1024,128]{1,0:T(8,128)(2,1)S(1)}, bf16[1024,128]{1,0:T(8,128)(2,1)S(1)}, u32[]{:S(2)}, u32[]{:S(2)}) collective-permute-start(bf16[1024,128]{1,0:T(8,128)(2,1)S(1)} %get-tuple-element.42.refs_0_), channel_id=1, source_target_pairs={{0,1},{1,0},{2,3},{3,2},{4,5},{5,4},{6,7},{7,6},{8,9},{9,8},{10,11... | collective-permute-start | bytes 786440 | tf_op jit(solution)/shard_map/ppermute | solution.py:708
  43.2 6.4 %collective-permute-start.18 = (f32[1,768]{1,0:T(1,128)S(1)}, f32[1,768]{1,0:T(1,128)S(1)}, u32[]{:S(2)}, u32[]{:S(2)}) collective-permute-start(f32[1,768]{1,0:T(1,128)S(1)} %broadcast_in_dim.8.refs_13_.refs_14_), channel_id=1, source_target_pairs={{0,1},{1,0},{2,3},{3,2},{4,5},{5,4},{6,7},{7,6},{8,9},{9,8},{10,11... | collective-permute-start | bytes 9224 | tf_op jit(solution)/shard_map/ppermute | solution.py:774
  44.6 20.0 %collective-permute-start.19 = (f32[1,768]{1,0:T(1,128)S(1)}, f32[1,768]{1,0:T(1,128)S(1)}, u32[]{:S(2)}, u32[]{:S(2)}) collective-permute-start(f32[1,768]{1,0:T(1,128)S(1)} %broadcast_in_dim.8.refs_13_.refs_14_), channel_id=1, source_target_pairs={{0,2},{1,3},{2,0},{3,1},{4,6},{5,7},{6,4},{7,5},{8,10},{9,11},{10,... | collective-permute-start | bytes 9224 | tf_op jit(solution)/shard_map/ppermute | solution.py:774
  45.2 19.5 %collective-permute-start.20 = (f32[1,768]{1,0:T(1,128)S(1)}, f32[1,768]{1,0:T(1,128)S(1)}, u32[]{:S(2)}, u32[]{:S(2)}) collective-permute-start(f32[1,768]{1,0:T(1,128)S(1)} %broadcast_in_dim.8.refs_13_.refs_14_), channel_id=1, source_target_pairs={{0,3},{1,2},{2,1},{3,0},{4,7},{5,6},{6,5},{7,4},{8,11},{9,10},{10,... | collective-permute-start | bytes 9224 | tf_op jit(solution)/shard_map/ppermute | solution.py:774
  49.6 40.8 %collective-permute-start.12 = (bf16[512,512]{1,0:T(8,128)(2,1)S(1)}, bf16[512,512]{1,0:T(8,128)(2,1)S(1)}, u32[]{:S(2)}, u32[]{:S(2)}) collective-permute-start(bf16[512,512]{1,0:T(8,128)(2,1)S(1)} %copy-done), channel_id=1, source_target_pairs={{0,1},{1,0},{2,3},{3,2},{4,5},{5,4},{6,7},{7,6},{8,9},{9,8},{10,11... | collective-permute-start | bytes 1572872 | tf_op jit(solution)/shard_map/ppermute | solution.py:708
  64.7 25.8 %collective-permute-start.15 = (bf16[512,512]{1,0:T(8,128)(2,1)S(1)}, bf16[512,512]{1,0:T(8,128)(2,1)S(1)}, u32[]{:S(2)}, u32[]{:S(2)}) collective-permute-start(bf16[512,512]{1,0:T(8,128)(2,1)S(1)} %copy-done.1), channel_id=1, source_target_pairs={{0,1},{1,0},{2,3},{3,2},{4,5},{5,4},{6,7},{7,6},{8,9},{9,8},{10,11... | collective-permute-start | bytes 1572872 | tf_op jit(solution)/shard_map/ppermute | solution.py:708
  64.7 12.5 %collective-permute-start.10 = (bf16[512,128]{1,0:T(8,128)(2,1)S(1)}, bf16[512,128]{1,0:T(8,128)(2,1)S(1)}, u32[]{:S(2)}, u32[]{:S(2)}) collective-permute-start(bf16[512,128]{1,0:T(8,128)(2,1)S(1)} %copy-done.2), channel_id=1, source_target_pairs={{0,2},{1,3},{2,0},{3,1},{4,6},{5,7},{6,4},{7,5},{8,10},{9,11},{10,... | collective-permute-start | bytes 393224 | tf_op jit(solution)/shard_map/ppermute | solution.py:702
  65.3 25.2 %collective-permute-start.14 = (bf16[512,512]{1,0:T(8,128)(2,1)S(1)}, bf16[512,512]{1,0:T(8,128)(2,1)S(1)}, u32[]{:S(2)}, u32[]{:S(2)}) collective-permute-start(bf16[512,512]{1,0:T(8,128)(2,1)S(1)} %collective-permute-done.13.refs_7_.refs_8_), channel_id=1, source_target_pairs={{0,1},{1,0},{2,3},{3,2},{4,5},{5,4},{6,7},{7,6},{8,9},{9,8},{10,11... | collective-permute-start | bytes 1572872 | tf_op jit(solution)/shard_map/ppermute | solution.py:708
  65.5 25.0 %collective-permute-start.17 = (bf16[512,512]{1,0:T(8,128)(2,1)S(1)}, bf16[512,512]{1,0:T(8,128)(2,1)S(1)}, u32[]{:S(2)}, u32[]{:S(2)}) collective-permute-start(bf16[512,512]{1,0:T(8,128)(2,1)S(1)} %collective-permute-done.16.refs_11_.refs_12_), channel_id=1, source_target_pairs={{0,1},{1,0},{2,3},{3,2},{4,5},{5,4},{6,7},{7,6},{8,9},{9,8},{10,11... | collective-permute-start | bytes 1572872 | tf_op jit(solution)/shard_map/ppermute | solution.py:708
  77.2 6.4 %collective-permute-start.9 = (bf16[512,128]{1,0:T(8,128)(2,1)S(1)}, bf16[512,128]{1,0:T(8,128)(2,1)S(1)}, u32[]{:S(2)}, u32[]{:S(2)}) collective-permute-start(bf16[512,128]{1,0:T(8,128)(2,1)S(1)} %copy-done.2), channel_id=1, source_target_pairs={{0,1},{1,0},{2,3},{3,2},{4,5},{5,4},{6,7},{7,6},{8,9},{9,8},{10,11... | collective-permute-start | bytes 393224 | tf_op jit(solution)/shard_map/ppermute | solution.py:708
  83.6 6.8 %collective-permute-start.11 = (bf16[512,128]{1,0:T(8,128)(2,1)S(1)}, bf16[512,128]{1,0:T(8,128)(2,1)S(1)}, u32[]{:S(2)}, u32[]{:S(2)}) collective-permute-start(bf16[512,128]{1,0:T(8,128)(2,1)S(1)} %collective-permute-done.10.refs_3_.refs_4_), channel_id=1, source_target_pairs={{0,1},{1,0},{2,3},{3,2},{4,5},{5,4},{6,7},{7,6},{8,9},{9,8},{10,11... | collective-permute-start | bytes 393224 | tf_op jit(solution)/shard_map/ppermute | solution.py:708
  92.8 6.0 %collective-permute-start.27 = (bf16[256,128]{1,0:T(8,128)(2,1)S(1)}, bf16[256,128]{1,0:T(8,128)(2,1)S(1)}, u32[]{:S(2)}, u32[]{:S(2)}) collective-permute-start(bf16[256,128]{1,0:T(8,128)(2,1)S(1)} %get-tuple-element.58), channel_id=1, source_target_pairs={{0,1},{1,2},{2,3},{3,0},{4,5},{5,6},{6,7},{7,4},{8,9},{9,10},{10,1... | collective-permute-start | bytes 196616 | tf_op jit(solution)/shard_map/ppermute | solution.py:676
  93.0 7.2 %collective-permute-start.28 = (bf16[256,128]{1,0:T(8,128)(2,1)S(1)}, bf16[256,128]{1,0:T(8,128)(2,1)S(1)}, u32[]{:S(2)}, u32[]{:S(2)}) collective-permute-start(bf16[256,128]{1,0:T(8,128)(2,1)S(1)} %get-tuple-element.59), channel_id=1, source_target_pairs={{0,2},{1,3},{2,0},{3,1},{4,6},{5,7},{6,4},{7,5},{8,10},{9,11},{10,... | collective-permute-start | bytes 196616 | tf_op jit(solution)/shard_map/ppermute | solution.py:676
  94.5 5.7 %collective-permute-start.29 = (bf16[256,128]{1,0:T(8,128)(2,1)S(1)}, bf16[256,128]{1,0:T(8,128)(2,1)S(1)}, u32[]{:S(2)}, u32[]{:S(2)}) collective-permute-start(bf16[256,128]{1,0:T(8,128)(2,1)S(1)} %get-tuple-element.60), channel_id=1, source_target_pairs={{0,3},{1,0},{2,1},{3,2},{4,7},{5,4},{6,5},{7,6},{8,11},{9,8},{10,9... | collective-permute-start | bytes 196616 | tf_op jit(solution)/shard_map/ppermute | solution.py:676
  98.1 3.8 %collective-permute-start.21 = (bf16[256,128]{1,0:T(8,128)(2,1)S(1)}, bf16[256,128]{1,0:T(8,128)(2,1)S(1)}, u32[]{:S(2)}, u32[]{:S(2)}) collective-permute-start(bf16[256,128]{1,0:T(8,128)(2,1)S(1)} %get-tuple-element.50), channel_id=1, source_target_pairs={{0,1},{1,2},{2,3},{3,0},{4,5},{5,6},{6,7},{7,4},{8,9},{9,10},{10,1... | collective-permute-start | bytes 196616 | tf_op jit(solution)/shard_map/ppermute | solution.py:676
  98.2 5.0 %collective-permute-start.22 = (bf16[256,128]{1,0:T(8,128)(2,1)S(1)}, bf16[256,128]{1,0:T(8,128)(2,1)S(1)}, u32[]{:S(2)}, u32[]{:S(2)}) collective-permute-start(bf16[256,128]{1,0:T(8,128)(2,1)S(1)} %get-tuple-element.51), channel_id=1, source_target_pairs={{0,2},{1,3},{2,0},{3,1},{4,6},{5,7},{6,4},{7,5},{8,10},{9,11},{10,... | collective-permute-start | bytes 196616 | tf_op jit(solution)/shard_map/ppermute | solution.py:676
  98.8 4.4 %collective-permute-start.23 = (bf16[256,128]{1,0:T(8,128)(2,1)S(1)}, bf16[256,128]{1,0:T(8,128)(2,1)S(1)}, u32[]{:S(2)}, u32[]{:S(2)}) collective-permute-start(bf16[256,128]{1,0:T(8,128)(2,1)S(1)} %get-tuple-element.52), channel_id=1, source_target_pairs={{0,3},{1,0},{2,1},{3,2},{4,7},{5,4},{6,5},{7,6},{8,11},{9,8},{10,9... | collective-permute-start | bytes 196616 | tf_op jit(solution)/shard_map/ppermute | solution.py:676
  104.4 12.3 %collective-permute-start.30 = (bf16[512,128]{1,0:T(8,128)(2,1)S(1)}, bf16[512,128]{1,0:T(8,128)(2,1)S(1)}, u32[]{:S(2)}, u32[]{:S(2)}) collective-permute-start(bf16[512,128]{1,0:T(8,128)(2,1)S(1)} %get-tuple-element.62), channel_id=1, source_target_pairs={{0,4},{4,8},{8,12},{12,0},{1,5},{5,9},{9,13},{13,1},{2,6},{6,10},{... | collective-permute-start | bytes 393224 | tf_op jit(solution)/shard_map/ppermute | solution.py:676
  110.6 10.7 %collective-permute-start.31 = (bf16[512,128]{1,0:T(8,128)(2,1)S(1)}, bf16[512,128]{1,0:T(8,128)(2,1)S(1)}, u32[]{:S(2)}, u32[]{:S(2)}) collective-permute-start(bf16[512,128]{1,0:T(8,128)(2,1)S(1)} %get-tuple-element.63), channel_id=1, source_target_pairs={{0,8},{4,12},{8,0},{12,4},{1,9},{5,13},{9,1},{13,5},{2,10},{6,14},... | collective-permute-start | bytes 393224 | tf_op jit(solution)/shard_map/ppermute | solution.py:676
  111.8 9.5 %collective-permute-start.32 = (bf16[512,128]{1,0:T(8,128)(2,1)S(1)}, bf16[512,128]{1,0:T(8,128)(2,1)S(1)}, u32[]{:S(2)}, u32[]{:S(2)}) collective-permute-start(bf16[512,128]{1,0:T(8,128)(2,1)S(1)} %get-tuple-element.64), channel_id=1, source_target_pairs={{0,12},{4,0},{8,4},{12,8},{1,13},{5,1},{9,5},{13,9},{2,14},{6,2},{... | collective-permute-start | bytes 393224 | tf_op jit(solution)/shard_map/ppermute | solution.py:676
  114.1 10.1 %collective-permute-start.24 = (bf16[512,128]{1,0:T(8,128)(2,1)S(1)}, bf16[512,128]{1,0:T(8,128)(2,1)S(1)}, u32[]{:S(2)}, u32[]{:S(2)}) collective-permute-start(bf16[512,128]{1,0:T(8,128)(2,1)S(1)} %get-tuple-element.54), channel_id=1, source_target_pairs={{0,4},{4,8},{8,12},{12,0},{1,5},{5,9},{9,13},{13,1},{2,6},{6,10},{... | collective-permute-start | bytes 393224 | tf_op jit(solution)/shard_map/ppermute | solution.py:676
  114.9 17.5 %collective-permute-start.25 = (bf16[512,128]{1,0:T(8,128)(2,1)S(1)}, bf16[512,128]{1,0:T(8,128)(2,1)S(1)}, u32[]{:S(2)}, u32[]{:S(2)}) collective-permute-start(bf16[512,128]{1,0:T(8,128)(2,1)S(1)} %get-tuple-element.55), channel_id=1, source_target_pairs={{0,8},{4,12},{8,0},{12,4},{1,9},{5,13},{9,1},{13,5},{2,10},{6,14},... | collective-permute-start | bytes 393224 | tf_op jit(solution)/shard_map/ppermute | solution.py:676
  116.6 15.8 %collective-permute-start.26 = (bf16[512,128]{1,0:T(8,128)(2,1)S(1)}, bf16[512,128]{1,0:T(8,128)(2,1)S(1)}, u32[]{:S(2)}, u32[]{:S(2)}) collective-permute-start(bf16[512,128]{1,0:T(8,128)(2,1)S(1)} %get-tuple-element.56), channel_id=1, source_target_pairs={{0,12},{4,0},{8,4},{12,8},{1,13},{5,1},{9,5},{13,9},{2,14},{6,2},{... | collective-permute-start | bytes 393224 | tf_op jit(solution)/shard_map/ppermute | solution.py:676
  (15 other events, 395.5 us)

commit v4 on v3

--- a/solution.py
+++ b/solution.py
@@ -408,37 +408,38 @@
     def largest(found):
         return jnp.max(jnp.abs(found), axis=0, keepdims=True)
 
+    def pair_weight(b, kind):
+        return jnp.concatenate([weights[c][kind] for c in range(b, b + pair_of)], axis=1)
+
     worst = None
     for b in range(0, blocks, pair_of):
-        both = range(b, b + pair_of)
         key_most, query_most = None, None
-        q_weight, k_weight, v_weight = (
-            jnp.concatenate([weights[c][t] for c in both], axis=1) for t in range(3)
-        )
+        k_weight, q_weight = pair_weight(b, 1), pair_weight(b, 0)
+        for half in range(2):
+            at = pl.ds(starts[half], queries)
+            found = dot(normed[at, :], q_weight) * score_scale
+            most = largest(found)
+            query_most = most if half == 0 else jnp.maximum(query_most, most)
+            for n in range(pair_of):
+                query[b + n, pl.ds(half * queries, queries), :] = found[
+                    :, n * LANES : (n + 1) * LANES
+                ].astype(BF)
         for i in range(rows // 256):
             at = pl.ds(i * 256, 256)
             found = dot(normed[at, :], k_weight)
             most = largest(found)
             key_most = most if i == 0 else jnp.maximum(key_most, most)
-            found = found.astype(BF)
-            turned = dot(v_weight, normed[at, :], (0, 1)).astype(BF)
-            for n, c in enumerate(both):
-                keys[c, at, :] = found[:, n * LANES : (n + 1) * LANES]
-                values[c, :, i * 256 : (i + 1) * 256] = turned[n * LANES : (n + 1) * LANES]
-        for half in range(2):
-            at = pl.ds(starts[half], queries)
-            found = dot(normed[at, :], q_weight) * score_scale
-            most = largest(found)
-            query_most = most if half == 0 else jnp.maximum(query_most, most)
-            found = found.astype(BF)
-            for n, c in enumerate(both):
-                query[c, pl.ds(half * queries, queries), :] = found[
-                    :, n * LANES : (n + 1) * LANES
-                ]
+            for n in range(pair_of):
+                keys[b + n, at, :] = found[:, n * LANES : (n + 1) * LANES].astype(BF)
         product = jnp.broadcast_to(key_most * query_most, (8, span)).astype(BF)
         bound = dot(product, same_head)
         worst = bound if b == 0 else jnp.maximum(worst, bound)
-    small[0] = (jnp.max(worst) * 1.05 < SAFE_LOG2).astype(I32)
+    is_small = (jnp.max(worst) * 1.05 < SAFE_LOG2).astype(I32)
+    for b in range(0, blocks, pair_of):
+        turned = dot(pair_weight(b, 2), normed[...], (0, 1))
+        for n in range(pair_of):
+            values[b + n] = turned[n * LANES : (n + 1) * LANES].astype(BF)
+    small[0] = is_small
 
 
 def project(feats, weights, params, patches, group):

time: 137 us -> 137 us (level)
  no operation moved by 1% of the time
where the time goes in v4:
time: 137 us; the launch traced here: 136 us
  waiting for transfers between devices  55.3 us (40%)
  Pallas kernels  45.5 us (33%)
  starting transfers between devices  33.4 us (24%)
    ppermute x15, waiting for transfers between devices, shift(): lax.ppermute(array, axis, [(i, (i + step) % size) for i in range(size)])  32.9 us
    pallas_call x3, Pallas kernels, attend(): pl.pallas_call(functools.partial(attend_kernel, low, high, half, min(TILE...  23.9 us
    ppermute x15, starting transfers between devices, shift(): lax.ppermute(array, axis, [(i, (i + step) % size) for i in range(size)])  23.2 us
    ppermute x3, waiting for transfers between devices, body(): vectors.append(lax.ppermute(vector, 'head', pairs))  14.9 us
    ppermute x5, waiting for transfers between devices, group_shift(): return lax.ppermute(array, 'head', pairs)  6.54 us
    ppermute x5, starting transfers between devices, group_shift(): return lax.ppermute(array, 'head', pairs)  6.34 us
    pallas_call x1, Pallas kernels, pack(): pl.pallas_call(functools.partial(pack_kernel, shards, cap, rows_here, col...  6.33 us
    pallas_call x2, Pallas kernels, mlp(): pl.pallas_call(functools.partial(mlp_kernel, blocks, members, patches, se...  4.67 us
  transfers between devices with their start and end apart: 33, of which 10 were waited for; matrix products, arithmetic and copies ran while one was open for 0% of the time, Pallas kernels for 28%

profile of v4, /device:TPU:0, one launch (start us, length us, event | category | flops | bytes accessed | tf_op | source)
XLA Modules:
  0.0 136.4 jit_solution(5790696691994028190)
XLA Ops:
  0.1 3.0 %collective-permute-start.7 = (bf16[3,512,128]{2,1,0:T(8,128)(2,1)}, bf16[3,512,128]{2,1,0:T(8,128)(2,1)S(1)}, u32[]{:S(2)}, u32[]{:S(2)}) collective-permute-start(bf16[3,512,128]{2,1,0:T(8,128)(2,1)} %refs_4_.1), channel_id=1, source_target_pairs={{0,2},{1,3},{2,0},{3,1},{4,6},{5,7},{6,4},{7,5},{8,10},{9,11},{10,... | collective-permute-start | bytes 1179656 | tf_op jit(solution)/shard_map/ppermute | solution.py:703
  3.8 6.3 %pack.1 = (bf16[1024,128]{1,0:T(8,128)(2,1)}, bf16[1024,128]{1,0:T(8,128)(2,1)}, bf16[1024,128]{1,0:T(8,128)(2,1)}, bf16[1024,128]{1,0:T(8,128)(2,1)}, s32[1,3072]{1,0:T(1,128)}) custom-call(s32[1]{0:T(128)S(6)} %copy.16.held, s32[1,3068]{1,0:T(1,128)} %bitcast.5, bf16[3068,512]{1,0:T(8,128)(2,1)} %z_feat.1), custom_call_target="tpu_custom_call" | custom-call | tf_op jit(solution)/shard_map/pack/pallas_call | solution.py:149
  10.1 1.6 %collective-permute-start = (bf16[1024,128]{1,0:T(8,128)(2,1)}, bf16[1024,128]{1,0:T(8,128)(2,1)S(1)}, u32[]{:S(2)}, u32[]{:S(2)}) collective-permute-start(bf16[1024,128]{1,0:T(8,128)(2,1)} %get-tuple-element.39), channel_id=1, source_target_pairs={{0,4},{4,8},{8,12},{12,0},{1,5},{5,9},{9,13},{13,1},{2,6},{6,10},{... | collective-permute-start | bytes 786440 | tf_op jit(solution)/shard_map/ppermute | solution.py:677
  11.7 2.6 %collective-permute-start.1 = (bf16[1024,128]{1,0:T(8,128)(2,1)}, bf16[1024,128]{1,0:T(8,128)(2,1)S(1)}, u32[]{:S(2)}, u32[]{:S(2)}) collective-permute-start(bf16[1024,128]{1,0:T(8,128)(2,1)} %get-tuple-element.40), channel_id=1, source_target_pairs={{0,8},{4,12},{8,0},{12,4},{1,9},{5,13},{9,1},{13,5},{2,10},{6,14},... | collective-permute-start | bytes 786440 | tf_op jit(solution)/shard_map/ppermute | solution.py:677
  14.3 1.3 collective-permute-start.2
  16.9 4.6 %collective-permute-done.refs_1_ = bf16[1024,128]{1,0:T(8,128)(2,1)S(1)} collective-permute-done((bf16[1024,128]{1,0:T(8,128)(2,1)}, bf16[1024,128]{1,0:T(8,128)(2,1)S(1)}, u32[]{:S(2)}, u32[]{:S(2)}) %collective-permute-start) | collective-permute-done | bytes 262176 | tf_op jit(solution)/shard_map/ppermute | solution.py:677
  21.5 10.8 %collective-permute-done.1.refs_2_ = bf16[1024,128]{1,0:T(8,128)(2,1)S(1)} collective-permute-done((bf16[1024,128]{1,0:T(8,128)(2,1)}, bf16[1024,128]{1,0:T(8,128)(2,1)S(1)}, u32[]{:S(2)}, u32[]{:S(2)}) %collective-permute-start.1) | collective-permute-done | bytes 262176 | tf_op jit(solution)/shard_map/ppermute | solution.py:677
  32.3 1.5 %compact.1 = (bf16[1024,128]{1,0:T(8,128)(2,1)S(1)}, bf16[1024,128]{1,0:T(8,128)(2,1)S(1)}) custom-call(s32[2,4]{1,0:T(2,128)S(1)} %convert_reduce_fusion.pieces, bf16[1024,128]{1,0:T(8,128)(2,1)S(1)} %keep.1.refs_0_, bf16[1024,128]{1,0:T(8,128)(2,1)S(1)} %collective-permute-done.refs_1_, bf16[1024,128]{1,0:T(8,128)(2,1)S(1)} %collective-permute-done.1.refs_2_, ...), custom_call_target="tpu_custom_call" | custom-call | tf_op jit(solution)/shard_map/compact/pallas_call | solution.py:237
  34.5 1.6 %collective-permute-start.13 = (bf16[512,512]{1,0:T(8,128)(2,1)S(1)}, bf16[512,512]{1,0:T(8,128)(2,1)S(1)}, u32[]{:S(2)}, u32[]{:S(2)}) collective-permute-start(bf16[512,512]{1,0:T(8,128)(2,1)S(1)} %copy-done), channel_id=1, source_target_pairs={{0,2},{1,3},{2,0},{3,1},{4,6},{5,7},{6,4},{7,5},{8,10},{9,11},{10,... | collective-permute-start | bytes 1572872 | tf_op jit(solution)/shard_map/ppermute | solution.py:703
  36.6 6.5 %collective-permute-done.4.refs_2_ = bf16[1024,128]{1,0:T(8,128)(2,1)S(1)} collective-permute-done((bf16[1024,128]{1,0:T(8,128)(2,1)S(1)}, bf16[1024,128]{1,0:T(8,128)(2,1)S(1)}, u32[]{:S(2)}, u32[]{:S(2)}) %collective-permute-start.4) | collective-permute-done | bytes 262176 | tf_op jit(solution)/shard_map/ppermute | solution.py:703
  46.1 2.9 %project.1 = (bf16[4,1024,128]{2,1,0:T(8,128)(2,1)S(1)}, bf16[4,128,1024]{2,1,0:T(8,128)(2,1)S(1)}, bf16[4,512,128]{2,1,0:T(8,128)(2,1)S(1)}, bf16[4,512,128]{2,1,0:T(8,128)(2,1)S(1)}, s32[1]{0:T(128)}) custom-call(f32[4,512]{1,0:T(4,128)S(1)} %pad_maximum_fusion.params, bf16[1024,128]{1,0:T(8,128)(2,1)S(1)} %get-tuple-element.42.refs_0_, ...), custom_call_target="tpu_custom_call" | custom-call | flops 1610612736 | bytes 4194304 | tf_op jit(solution)/shard_map/project/pallas_call | solution.py:450
  49.8 14.9 %collective-permute-done.19.refs_15_.refs_16_ = f32[1,768]{1,0:T(1,128)S(1)} collective-permute-done((f32[1,768]{1,0:T(1,128)S(1)}, f32[1,768]{1,0:T(1,128)S(1)}, u32[]{:S(2)}, u32[]{:S(2)}) %collective-permute-start.19) | collective-permute-done | bytes 3104 | tf_op jit(solution)/shard_map/ppermute | solution.py:775
  65.8 11.3 %attend.3.refs_0_ = bf16[4,128,256]{2,1,0:T(8,128)(2,1)S(1)} custom-call(s32[1]{0:T(128)} %get-tuple-element.45.small, bf16[4,1024,128]{2,1,0:T(8,128)(2,1)S(1)} %get-tuple-element.46.keys, bf16[4,128,1024]{2,1,0:T(8,128)(2,1)S(1)} %get-tuple-element.47.values, bf16[4,512,128]{2,1,0:T(8,128)(2,1)S(1)} %get-tuple-element.48.query), custom_call_target="tpu_custom_call" | custom-call | flops 4294967296 | bytes 2097152 | tf_op jit(solution)/shard_map/attend/pallas_call | solution.py:574
  77.4 6.2 %attend.5.refs_1_ = bf16[2,128,256]{2,1,0:T(8,128)(2,1)S(1)} custom-call(s32[1]{0:T(128)} %get-tuple-element.45.small, bf16[4,1024,128]{2,1,0:T(8,128)(2,1)S(1)} %get-tuple-element.46.keys, bf16[4,128,1024]{2,1,0:T(8,128)(2,1)S(1)} %get-tuple-element.47.values, bf16[4,512,128]{2,1,0:T(8,128)(2,1)S(1)} %get-tuple-element.48.query), custom_call_target="tpu_custom_call" | custom-call | flops 2147483648 | bytes 1048576 | tf_op jit(solution)/shard_map/attend/pallas_call | solution.py:574
  84.0 6.4 %attend.4.refs_0_ = bf16[2,128,256]{2,1,0:T(8,128)(2,1)S(1)} custom-call(s32[1]{0:T(128)} %get-tuple-element.45.small, bf16[4,1024,128]{2,1,0:T(8,128)(2,1)S(1)} %get-tuple-element.46.keys, bf16[4,128,1024]{2,1,0:T(8,128)(2,1)S(1)} %get-tuple-element.47.values, bf16[4,512,128]{2,1,0:T(8,128)(2,1)S(1)} %get-tuple-element.48.query), custom_call_target="tpu_custom_call" | custom-call | flops 2147483648 | bytes 1048576 | tf_op jit(solution)/shard_map/attend/pallas_call | solution.py:574
  90.5 2.4 %mlp.3 = (bf16[256,128]{1,0:T(8,128)(2,1)S(1)}, bf16[256,128]{1,0:T(8,128)(2,1)S(1)}, bf16[256,128]{1,0:T(8,128)(2,1)S(1)}, bf16[256,128]{1,0:T(8,128)(2,1)S(1)}) custom-call(f32[4,512]{1,0:T(4,128)S(1)} %pad_maximum_fusion.params, bf16[4,512,128]{2,1,0:T(8,128)(2,1)S(1)} %get-tuple-element.44.kept, bf16[2,128,256]{2,1,0:T(8,128)(2,1)S(1)} %attend.4.refs_0_, ...), custom_call_target="tpu_custom_call" | custom-call | flops 1073741824 | bytes 4194304 | tf_op jit(solution)/shard_map/mlp/pallas_call | solution.py:654
  93.0 1.5 %collective-permute-start.28 = (bf16[256,128]{1,0:T(8,128)(2,1)S(1)}, bf16[256,128]{1,0:T(8,128)(2,1)S(1)}, u32[]{:S(2)}, u32[]{:S(2)}) collective-permute-start(bf16[256,128]{1,0:T(8,128)(2,1)S(1)} %get-tuple-element.59), channel_id=1, source_target_pairs={{0,2},{1,3},{2,0},{3,1},{4,6},{5,7},{6,4},{7,5},{8,10},{9,11},{10,... | collective-permute-start | bytes 196616 | tf_op jit(solution)/shard_map/ppermute | solution.py:677
  94.5 1.3 collective-permute-start.29
  95.8 2.3 %mlp.2 = (bf16[256,128]{1,0:T(8,128)(2,1)S(1)}, bf16[256,128]{1,0:T(8,128)(2,1)S(1)}, bf16[256,128]{1,0:T(8,128)(2,1)S(1)}, bf16[256,128]{1,0:T(8,128)(2,1)S(1)}) custom-call(f32[4,512]{1,0:T(4,128)S(1)} %pad_maximum_fusion.params, bf16[4,512,128]{2,1,0:T(8,128)(2,1)S(1)} %get-tuple-element.44.kept, bf16[4,128,256]{2,1,0:T(8,128)(2,1)S(1)} %attend.3.refs_0_, ...), custom_call_target="tpu_custom_call" | custom-call | flops 1073741824 | bytes 4194304 | tf_op jit(solution)/shard_map/mlp/pallas_call | solution.py:654
  98.8 1.4 %collective-permute-start.23 = (bf16[256,128]{1,0:T(8,128)(2,1)S(1)}, bf16[256,128]{1,0:T(8,128)(2,1)S(1)}, u32[]{:S(2)}, u32[]{:S(2)}) collective-permute-start(bf16[256,128]{1,0:T(8,128)(2,1)S(1)} %get-tuple-element.52), channel_id=1, source_target_pairs={{0,3},{1,0},{2,1},{3,2},{4,7},{5,4},{6,5},{7,6},{8,11},{9,8},{10,9... | collective-permute-start | bytes 196616 | tf_op jit(solution)/shard_map/ppermute | solution.py:677
  100.2 1.7 %collective-permute-done.21.refs_1_ = bf16[256,128]{1,0:T(8,128)(2,1)S(1)} collective-permute-done((bf16[256,128]{1,0:T(8,128)(2,1)S(1)}, bf16[256,128]{1,0:T(8,128)(2,1)S(1)}, u32[]{:S(2)}, u32[]{:S(2)}) %collective-permute-start.21) | collective-permute-done | bytes 65568 | tf_op jit(solution)/shard_map/ppermute | solution.py:677
  101.9 1.3 collective-permute-done.22.refs_2_
  103.2 1.1 spread.3
  104.4 6.2 %collective-permute-start.30 = (bf16[512,128]{1,0:T(8,128)(2,1)S(1)}, bf16[512,128]{1,0:T(8,128)(2,1)S(1)}, u32[]{:S(2)}, u32[]{:S(2)}) collective-permute-start(bf16[512,128]{1,0:T(8,128)(2,1)S(1)} %get-tuple-element.62), channel_id=1, source_target_pairs={{0,4},{4,8},{8,12},{12,0},{1,5},{5,9},{9,13},{13,1},{2,6},{6,10},{... | collective-permute-start | bytes 393224 | tf_op jit(solution)/shard_map/ppermute | solution.py:677
  110.6 1.2 collective-permute-start.31
  111.8 1.2 collective-permute-start.32
  114.9 1.7 %collective-permute-start.25 = (bf16[512,128]{1,0:T(8,128)(2,1)S(1)}, bf16[512,128]{1,0:T(8,128)(2,1)S(1)}, u32[]{:S(2)}, u32[]{:S(2)}) collective-permute-start(bf16[512,128]{1,0:T(8,128)(2,1)S(1)} %get-tuple-element.55), channel_id=1, source_target_pairs={{0,8},{4,12},{8,0},{12,4},{1,9},{5,13},{9,1},{13,5},{2,10},{6,14},... | collective-permute-start | bytes 393224 | tf_op jit(solution)/shard_map/ppermute | solution.py:677
  116.6 1.3 collective-permute-start.26
  118.0 3.3 %collective-permute-done.31.refs_6_ = bf16[512,128]{1,0:T(8,128)(2,1)S(1)} collective-permute-done((bf16[512,128]{1,0:T(8,128)(2,1)S(1)}, bf16[512,128]{1,0:T(8,128)(2,1)S(1)}, u32[]{:S(2)}, u32[]{:S(2)}) %collective-permute-start.31) | collective-permute-done | bytes 131104 | tf_op jit(solution)/shard_map/ppermute | solution.py:677
  121.3 2.8 %collective-permute-done.24.refs_1_ = bf16[512,128]{1,0:T(8,128)(2,1)S(1)} collective-permute-done((bf16[512,128]{1,0:T(8,128)(2,1)S(1)}, bf16[512,128]{1,0:T(8,128)(2,1)S(1)}, u32[]{:S(2)}, u32[]{:S(2)}) %collective-permute-start.24) | collective-permute-done | bytes 131104 | tf_op jit(solution)/shard_map/ppermute | solution.py:677
  124.2 8.3 %collective-permute-done.25.refs_2_ = bf16[512,128]{1,0:T(8,128)(2,1)S(1)} collective-permute-done((bf16[512,128]{1,0:T(8,128)(2,1)S(1)}, bf16[512,128]{1,0:T(8,128)(2,1)S(1)}, u32[]{:S(2)}, u32[]{:S(2)}) %collective-permute-start.25) | collective-permute-done | bytes 131104 | tf_op jit(solution)/shard_map/ppermute | solution.py:677
  132.4 4.0 %unpack.1 = bf16[3068,128]{1,0:T(8,128)(2,1)} custom-call(s32[1]{0:T(128)S(6)} %copy.16.held, s32[1,3072]{1,0:T(1,128)S(1)} %copy-done.4, bf16[512,128]{1,0:T(8,128)(2,1)S(1)} %get-tuple-element.53.refs_0_, bf16[512,128]{1,0:T(8,128)(2,1)S(1)} %collective-permute-done.24.refs_1_, bf16[512,128]{1,0:T(8,128)(2,1)S(1)} %collective-permute-done.25.refs_2_, ...), custom_call_target="tpu_custom_call" | custom-call | tf_op jit(solution)/shard_map/unpack/pallas_call | solution.py:341
  (80 shorter events, 10.6 us)
Async XLA Ops:
  0.1 34.4 %collective-permute-start.7 = (bf16[3,512,128]{2,1,0:T(8,128)(2,1)}, bf16[3,512,128]{2,1,0:T(8,128)(2,1)S(1)}, u32[]{:S(2)}, u32[]{:S(2)}) collective-permute-start(bf16[3,512,128]{2,1,0:T(8,128)(2,1)} %refs_4_.1), channel_id=1, source_target_pairs={{0,2},{1,3},{2,0},{3,1},{4,6},{5,7},{6,4},{7,5},{8,10},{9,11},{10,... | collective-permute-start | bytes 1179656 | tf_op jit(solution)/shard_map/ppermute | solution.py:703
  3.1 33.4 %collective-permute-start.6 = (bf16[3,512,128]{2,1,0:T(8,128)(2,1)}, bf16[3,512,128]{2,1,0:T(8,128)(2,1)S(1)}, u32[]{:S(2)}, u32[]{:S(2)}) collective-permute-start(bf16[3,512,128]{2,1,0:T(8,128)(2,1)} %refs_4_.1), channel_id=1, source_target_pairs={{0,1},{1,0},{2,3},{3,2},{4,5},{5,4},{6,7},{7,6},{8,9},{9,8},{10,11... | collective-permute-start | bytes 1179656 | tf_op jit(solution)/shard_map/ppermute | solution.py:709
  10.1 11.4 %collective-permute-start = (bf16[1024,128]{1,0:T(8,128)(2,1)}, bf16[1024,128]{1,0:T(8,128)(2,1)S(1)}, u32[]{:S(2)}, u32[]{:S(2)}) collective-permute-start(bf16[1024,128]{1,0:T(8,128)(2,1)} %get-tuple-element.39), channel_id=1, source_target_pairs={{0,4},{4,8},{8,12},{12,0},{1,5},{5,9},{9,13},{13,1},{2,6},{6,10},{... | collective-permute-start | bytes 786440 | tf_op jit(solution)/shard_map/ppermute | solution.py:677
  11.7 20.6 %collective-permute-start.1 = (bf16[1024,128]{1,0:T(8,128)(2,1)}, bf16[1024,128]{1,0:T(8,128)(2,1)S(1)}, u32[]{:S(2)}, u32[]{:S(2)}) collective-permute-start(bf16[1024,128]{1,0:T(8,128)(2,1)} %get-tuple-element.40), channel_id=1, source_target_pairs={{0,8},{4,12},{8,0},{12,4},{1,9},{5,13},{9,1},{13,5},{2,10},{6,14},... | collective-permute-start | bytes 786440 | tf_op jit(solution)/shard_map/ppermute | solution.py:677
  14.3 18.0 %collective-permute-start.2 = (bf16[1024,128]{1,0:T(8,128)(2,1)}, bf16[1024,128]{1,0:T(8,128)(2,1)S(1)}, u32[]{:S(2)}, u32[]{:S(2)}) collective-permute-start(bf16[1024,128]{1,0:T(8,128)(2,1)} %get-tuple-element.41), channel_id=1, source_target_pairs={{0,12},{4,0},{8,4},{12,8},{1,13},{5,1},{9,5},{13,9},{2,14},{6,2},{... | collective-permute-start | bytes 786440 | tf_op jit(solution)/shard_map/ppermute | solution.py:677
  33.9 9.2 %collective-permute-start.4 = (bf16[1024,128]{1,0:T(8,128)(2,1)S(1)}, bf16[1024,128]{1,0:T(8,128)(2,1)S(1)}, u32[]{:S(2)}, u32[]{:S(2)}) collective-permute-start(bf16[1024,128]{1,0:T(8,128)(2,1)S(1)} %get-tuple-element.43), channel_id=1, source_target_pairs={{0,2},{1,3},{2,0},{3,1},{4,6},{5,7},{6,4},{7,5},{8,10},{9,11},{10,... | collective-permute-start | bytes 786440 | tf_op jit(solution)/shard_map/ppermute | solution.py:703
  34.5 10.7 %collective-permute-start.8 = (bf16[3,512,128]{2,1,0:T(8,128)(2,1)S(1)}, bf16[3,512,128]{2,1,0:T(8,128)(2,1)S(1)}, u32[]{:S(2)}, u32[]{:S(2)}) collective-permute-start(bf16[3,512,128]{2,1,0:T(8,128)(2,1)S(1)} %collective-permute-done.7.refs_6_), channel_id=1, source_target_pairs={{0,1},{1,0},{2,3},{3,2},{4,5},{5,4},{6,7},{7,6},{8,9},{9,8},{10,11... | collective-permute-start | bytes 1179656 | tf_op jit(solution)/shard_map/ppermute | solution.py:709
  34.5 30.8 %collective-permute-start.13 = (bf16[512,512]{1,0:T(8,128)(2,1)S(1)}, bf16[512,512]{1,0:T(8,128)(2,1)S(1)}, u32[]{:S(2)}, u32[]{:S(2)}) collective-permute-start(bf16[512,512]{1,0:T(8,128)(2,1)S(1)} %copy-done), channel_id=1, source_target_pairs={{0,2},{1,3},{2,0},{3,1},{4,6},{5,7},{6,4},{7,5},{8,10},{9,11},{10,... | collective-permute-start | bytes 1572872 | tf_op jit(solution)/shard_map/ppermute | solution.py:703
  36.0 29.4 %collective-permute-start.16 = (bf16[512,512]{1,0:T(8,128)(2,1)S(1)}, bf16[512,512]{1,0:T(8,128)(2,1)S(1)}, u32[]{:S(2)}, u32[]{:S(2)}) collective-permute-start(bf16[512,512]{1,0:T(8,128)(2,1)S(1)} %copy-done.1), channel_id=1, source_target_pairs={{0,2},{1,3},{2,0},{3,1},{4,6},{5,7},{6,4},{7,5},{8,10},{9,11},{10,... | collective-permute-start | bytes 1572872 | tf_op jit(solution)/shard_map/ppermute | solution.py:703
  36.6 6.6 %collective-permute-start.3 = (bf16[1024,128]{1,0:T(8,128)(2,1)S(1)}, bf16[1024,128]{1,0:T(8,128)(2,1)S(1)}, u32[]{:S(2)}, u32[]{:S(2)}) collective-permute-start(bf16[1024,128]{1,0:T(8,128)(2,1)S(1)} %get-tuple-element.42.refs_0_), channel_id=1, source_target_pairs={{0,1},{1,0},{2,3},{3,2},{4,5},{5,4},{6,7},{7,6},{8,9},{9,8},{10,11... | collective-permute-start | bytes 786440 | tf_op jit(solution)/shard_map/ppermute | solution.py:709
  43.2 5.9 %collective-permute-start.18 = (f32[1,768]{1,0:T(1,128)S(1)}, f32[1,768]{1,0:T(1,128)S(1)}, u32[]{:S(2)}, u32[]{:S(2)}) collective-permute-start(f32[1,768]{1,0:T(1,128)S(1)} %broadcast_in_dim.8.refs_13_.refs_14_), channel_id=1, source_target_pairs={{0,1},{1,0},{2,3},{3,2},{4,5},{5,4},{6,7},{7,6},{8,9},{9,8},{10,11... | collective-permute-start | bytes 9224 | tf_op jit(solution)/shard_map/ppermute | solution.py:775
  44.6 20.0 %collective-permute-start.19 = (f32[1,768]{1,0:T(1,128)S(1)}, f32[1,768]{1,0:T(1,128)S(1)}, u32[]{:S(2)}, u32[]{:S(2)}) collective-permute-start(f32[1,768]{1,0:T(1,128)S(1)} %broadcast_in_dim.8.refs_13_.refs_14_), channel_id=1, source_target_pairs={{0,2},{1,3},{2,0},{3,1},{4,6},{5,7},{6,4},{7,5},{8,10},{9,11},{10,... | collective-permute-start | bytes 9224 | tf_op jit(solution)/shard_map/ppermute | solution.py:775
  45.2 19.5 %collective-permute-start.20 = (f32[1,768]{1,0:T(1,128)S(1)}, f32[1,768]{1,0:T(1,128)S(1)}, u32[]{:S(2)}, u32[]{:S(2)}) collective-permute-start(f32[1,768]{1,0:T(1,128)S(1)} %broadcast_in_dim.8.refs_13_.refs_14_), channel_id=1, source_target_pairs={{0,3},{1,2},{2,1},{3,0},{4,7},{5,6},{6,5},{7,4},{8,11},{9,10},{10,... | collective-permute-start | bytes 9224 | tf_op jit(solution)/shard_map/ppermute | solution.py:775
  49.0 41.4 %collective-permute-start.12 = (bf16[512,512]{1,0:T(8,128)(2,1)S(1)}, bf16[512,512]{1,0:T(8,128)(2,1)S(1)}, u32[]{:S(2)}, u32[]{:S(2)}) collective-permute-start(bf16[512,512]{1,0:T(8,128)(2,1)S(1)} %copy-done), channel_id=1, source_target_pairs={{0,1},{1,0},{2,3},{3,2},{4,5},{5,4},{6,7},{7,6},{8,9},{9,8},{10,11... | collective-permute-start | bytes 1572872 | tf_op jit(solution)/shard_map/ppermute | solution.py:709
  64.7 25.8 %collective-permute-start.15 = (bf16[512,512]{1,0:T(8,128)(2,1)S(1)}, bf16[512,512]{1,0:T(8,128)(2,1)S(1)}, u32[]{:S(2)}, u32[]{:S(2)}) collective-permute-start(bf16[512,512]{1,0:T(8,128)(2,1)S(1)} %copy-done.1), channel_id=1, source_target_pairs={{0,1},{1,0},{2,3},{3,2},{4,5},{5,4},{6,7},{7,6},{8,9},{9,8},{10,11... | collective-permute-start | bytes 1572872 | tf_op jit(solution)/shard_map/ppermute | solution.py:709
  64.7 12.5 %collective-permute-start.10 = (bf16[512,128]{1,0:T(8,128)(2,1)S(1)}, bf16[512,128]{1,0:T(8,128)(2,1)S(1)}, u32[]{:S(2)}, u32[]{:S(2)}) collective-permute-start(bf16[512,128]{1,0:T(8,128)(2,1)S(1)} %copy-done.2), channel_id=1, source_target_pairs={{0,2},{1,3},{2,0},{3,1},{4,6},{5,7},{6,4},{7,5},{8,10},{9,11},{10,... | collective-permute-start | bytes 393224 | tf_op jit(solution)/shard_map/ppermute | solution.py:703
  65.3 25.2 %collective-permute-start.14 = (bf16[512,512]{1,0:T(8,128)(2,1)S(1)}, bf16[512,512]{1,0:T(8,128)(2,1)S(1)}, u32[]{:S(2)}, u32[]{:S(2)}) collective-permute-start(bf16[512,512]{1,0:T(8,128)(2,1)S(1)} %collective-permute-done.13.refs_7_.refs_8_), channel_id=1, source_target_pairs={{0,1},{1,0},{2,3},{3,2},{4,5},{5,4},{6,7},{7,6},{8,9},{9,8},{10,11... | collective-permute-start | bytes 1572872 | tf_op jit(solution)/shard_map/ppermute | solution.py:709
  65.5 25.0 %collective-permute-start.17 = (bf16[512,512]{1,0:T(8,128)(2,1)S(1)}, bf16[512,512]{1,0:T(8,128)(2,1)S(1)}, u32[]{:S(2)}, u32[]{:S(2)}) collective-permute-start(bf16[512,512]{1,0:T(8,128)(2,1)S(1)} %collective-permute-done.16.refs_11_.refs_12_), channel_id=1, source_target_pairs={{0,1},{1,0},{2,3},{3,2},{4,5},{5,4},{6,7},{7,6},{8,9},{9,8},{10,11... | collective-permute-start | bytes 1572872 | tf_op jit(solution)/shard_map/ppermute | solution.py:709
  77.2 6.4 %collective-permute-start.9 = (bf16[512,128]{1,0:T(8,128)(2,1)S(1)}, bf16[512,128]{1,0:T(8,128)(2,1)S(1)}, u32[]{:S(2)}, u32[]{:S(2)}) collective-permute-start(bf16[512,128]{1,0:T(8,128)(2,1)S(1)} %copy-done.2), channel_id=1, source_target_pairs={{0,1},{1,0},{2,3},{3,2},{4,5},{5,4},{6,7},{7,6},{8,9},{9,8},{10,11... | collective-permute-start | bytes 393224 | tf_op jit(solution)/shard_map/ppermute | solution.py:709
  83.6 6.8 %collective-permute-start.11 = (bf16[512,128]{1,0:T(8,128)(2,1)S(1)}, bf16[512,128]{1,0:T(8,128)(2,1)S(1)}, u32[]{:S(2)}, u32[]{:S(2)}) collective-permute-start(bf16[512,128]{1,0:T(8,128)(2,1)S(1)} %collective-permute-done.10.refs_3_.refs_4_), channel_id=1, source_target_pairs={{0,1},{1,0},{2,3},{3,2},{4,5},{5,4},{6,7},{7,6},{8,9},{9,8},{10,11... | collective-permute-start | bytes 393224 | tf_op jit(solution)/shard_map/ppermute | solution.py:709
  92.8 6.0 %collective-permute-start.27 = (bf16[256,128]{1,0:T(8,128)(2,1)S(1)}, bf16[256,128]{1,0:T(8,128)(2,1)S(1)}, u32[]{:S(2)}, u32[]{:S(2)}) collective-permute-start(bf16[256,128]{1,0:T(8,128)(2,1)S(1)} %get-tuple-element.58), channel_id=1, source_target_pairs={{0,1},{1,2},{2,3},{3,0},{4,5},{5,6},{6,7},{7,4},{8,9},{9,10},{10,1... | collective-permute-start | bytes 196616 | tf_op jit(solution)/shard_map/ppermute | solution.py:677
  93.0 7.2 %collective-permute-start.28 = (bf16[256,128]{1,0:T(8,128)(2,1)S(1)}, bf16[256,128]{1,0:T(8,128)(2,1)S(1)}, u32[]{:S(2)}, u32[]{:S(2)}) collective-permute-start(bf16[256,128]{1,0:T(8,128)(2,1)S(1)} %get-tuple-element.59), channel_id=1, source_target_pairs={{0,2},{1,3},{2,0},{3,1},{4,6},{5,7},{6,4},{7,5},{8,10},{9,11},{10,... | collective-permute-start | bytes 196616 | tf_op jit(solution)/shard_map/ppermute | solution.py:677
  94.5 5.7 %collective-permute-start.29 = (bf16[256,128]{1,0:T(8,128)(2,1)S(1)}, bf16[256,128]{1,0:T(8,128)(2,1)S(1)}, u32[]{:S(2)}, u32[]{:S(2)}) collective-permute-start(bf16[256,128]{1,0:T(8,128)(2,1)S(1)} %get-tuple-element.60), channel_id=1, source_target_pairs={{0,3},{1,0},{2,1},{3,2},{4,7},{5,4},{6,5},{7,6},{8,11},{9,8},{10,9... | collective-permute-start | bytes 196616 | tf_op jit(solution)/shard_map/ppermute | solution.py:677
  98.1 3.8 %collective-permute-start.21 = (bf16[256,128]{1,0:T(8,128)(2,1)S(1)}, bf16[256,128]{1,0:T(8,128)(2,1)S(1)}, u32[]{:S(2)}, u32[]{:S(2)}) collective-permute-start(bf16[256,128]{1,0:T(8,128)(2,1)S(1)} %get-tuple-element.50), channel_id=1, source_target_pairs={{0,1},{1,2},{2,3},{3,0},{4,5},{5,6},{6,7},{7,4},{8,9},{9,10},{10,1... | collective-permute-start | bytes 196616 | tf_op jit(solution)/shard_map/ppermute | solution.py:677
  98.2 5.0 %collective-permute-start.22 = (bf16[256,128]{1,0:T(8,128)(2,1)S(1)}, bf16[256,128]{1,0:T(8,128)(2,1)S(1)}, u32[]{:S(2)}, u32[]{:S(2)}) collective-permute-start(bf16[256,128]{1,0:T(8,128)(2,1)S(1)} %get-tuple-element.51), channel_id=1, source_target_pairs={{0,2},{1,3},{2,0},{3,1},{4,6},{5,7},{6,4},{7,5},{8,10},{9,11},{10,... | collective-permute-start | bytes 196616 | tf_op jit(solution)/shard_map/ppermute | solution.py:677
  98.8 4.4 %collective-permute-start.23 = (bf16[256,128]{1,0:T(8,128)(2,1)S(1)}, bf16[256,128]{1,0:T(8,128)(2,1)S(1)}, u32[]{:S(2)}, u32[]{:S(2)}) collective-permute-start(bf16[256,128]{1,0:T(8,128)(2,1)S(1)} %get-tuple-element.52), channel_id=1, source_target_pairs={{0,3},{1,0},{2,1},{3,2},{4,7},{5,4},{6,5},{7,6},{8,11},{9,8},{10,9... | collective-permute-start | bytes 196616 | tf_op jit(solution)/shard_map/ppermute | solution.py:677
  104.4 12.3 %collective-permute-start.30 = (bf16[512,128]{1,0:T(8,128)(2,1)S(1)}, bf16[512,128]{1,0:T(8,128)(2,1)S(1)}, u32[]{:S(2)}, u32[]{:S(2)}) collective-permute-start(bf16[512,128]{1,0:T(8,128)(2,1)S(1)} %get-tuple-element.62), channel_id=1, source_target_pairs={{0,4},{4,8},{8,12},{12,0},{1,5},{5,9},{9,13},{13,1},{2,6},{6,10},{... | collective-permute-start | bytes 393224 | tf_op jit(solution)/shard_map/ppermute | solution.py:677
  110.6 10.7 %collective-permute-start.31 = (bf16[512,128]{1,0:T(8,128)(2,1)S(1)}, bf16[512,128]{1,0:T(8,128)(2,1)S(1)}, u32[]{:S(2)}, u32[]{:S(2)}) collective-permute-start(bf16[512,128]{1,0:T(8,128)(2,1)S(1)} %get-tuple-element.63), channel_id=1, source_target_pairs={{0,8},{4,12},{8,0},{12,4},{1,9},{5,13},{9,1},{13,5},{2,10},{6,14},... | collective-permute-start | bytes 393224 | tf_op jit(solution)/shard_map/ppermute | solution.py:677
  111.8 9.5 %collective-permute-start.32 = (bf16[512,128]{1,0:T(8,128)(2,1)S(1)}, bf16[512,128]{1,0:T(8,128)(2,1)S(1)}, u32[]{:S(2)}, u32[]{:S(2)}) collective-permute-start(bf16[512,128]{1,0:T(8,128)(2,1)S(1)} %get-tuple-element.64), channel_id=1, source_target_pairs={{0,12},{4,0},{8,4},{12,8},{1,13},{5,1},{9,5},{13,9},{2,14},{6,2},{... | collective-permute-start | bytes 393224 | tf_op jit(solution)/shard_map/ppermute | solution.py:677
  114.1 10.1 %collective-permute-start.24 = (bf16[512,128]{1,0:T(8,128)(2,1)S(1)}, bf16[512,128]{1,0:T(8,128)(2,1)S(1)}, u32[]{:S(2)}, u32[]{:S(2)}) collective-permute-start(bf16[512,128]{1,0:T(8,128)(2,1)S(1)} %get-tuple-element.54), channel_id=1, source_target_pairs={{0,4},{4,8},{8,12},{12,0},{1,5},{5,9},{9,13},{13,1},{2,6},{6,10},{... | collective-permute-start | bytes 393224 | tf_op jit(solution)/shard_map/ppermute | solution.py:677
  114.9 17.5 %collective-permute-start.25 = (bf16[512,128]{1,0:T(8,128)(2,1)S(1)}, bf16[512,128]{1,0:T(8,128)(2,1)S(1)}, u32[]{:S(2)}, u32[]{:S(2)}) collective-permute-start(bf16[512,128]{1,0:T(8,128)(2,1)S(1)} %get-tuple-element.55), channel_id=1, source_target_pairs={{0,8},{4,12},{8,0},{12,4},{1,9},{5,13},{9,1},{13,5},{2,10},{6,14},... | collective-permute-start | bytes 393224 | tf_op jit(solution)/shard_map/ppermute | solution.py:677
  116.6 15.8 %collective-permute-start.26 = (bf16[512,128]{1,0:T(8,128)(2,1)S(1)}, bf16[512,128]{1,0:T(8,128)(2,1)S(1)}, u32[]{:S(2)}, u32[]{:S(2)}) collective-permute-start(bf16[512,128]{1,0:T(8,128)(2,1)S(1)} %get-tuple-element.56), channel_id=1, source_target_pairs={{0,12},{4,0},{8,4},{12,8},{1,13},{5,1},{9,5},{13,9},{2,14},{6,2},{... | collective-permute-start | bytes 393224 | tf_op jit(solution)/shard_map/ppermute | solution.py:677
  (15 other events, 395.5 us)

commit v5 on v4

--- a/solution.py
+++ b/solution.py
@@ -182,13 +182,13 @@
 
 def move_segment(source, source_at, target, target_at, length):
     def one(i, carry):
-        for k in range(4):
-            target[pl.ds(target_at + i * 32 + k * 8, 8), :] = source[
-                pl.ds(source_at + i * 32 + k * 8, 8), :
+        for k in range(8):
+            target[pl.ds(target_at + i * 64 + k * 8, 8), :] = source[
+                pl.ds(source_at + i * 64 + k * 8, 8), :
             ]
         return carry
 
-    lax.fori_loop(0, (length + 31) // 32, one, 0)
+    lax.fori_loop(0, (length + 63) // 64, one, 0)
 
 
 def segment_table(pieces, patches, shards, cap):

time: 137 us -> 137 us (level)
  no operation moved by 1% of the time
where the time goes in v5:
time: 137 us; the launch traced here: 136 us
  waiting for transfers between devices  55.4 us (40%)
  Pallas kernels  45.1 us (33%)
  starting transfers between devices  33.4 us (24%)
    ppermute x15, waiting for transfers between devices, shift(): lax.ppermute(array, axis, [(i, (i + step) % size) for i in range(size)])  33 us
    pallas_call x3, Pallas kernels, attend(): pl.pallas_call(functools.partial(attend_kernel, low, high, half, min(TILE...  23.9 us
    ppermute x15, starting transfers between devices, shift(): lax.ppermute(array, axis, [(i, (i + step) % size) for i in range(size)])  23.1 us
    ppermute x3, waiting for transfers between devices, body(): vectors.append(lax.ppermute(vector, 'head', pairs))  14.9 us
    ppermute x5, waiting for transfers between devices, group_shift(): return lax.ppermute(array, 'head', pairs)  6.54 us
    ppermute x5, starting transfers between devices, group_shift(): return lax.ppermute(array, 'head', pairs)  6.34 us
    pallas_call x1, Pallas kernels, pack(): pl.pallas_call(functools.partial(pack_kernel, shards, cap, rows_here, col...  6.33 us
    pallas_call x2, Pallas kernels, mlp(): pl.pallas_call(functools.partial(mlp_kernel, blocks, members, patches, se...  4.67 us
  transfers between devices with their start and end apart: 33, of which 10 were waited for; matrix products, arithmetic and copies ran while one was open for 0% of the time, Pallas kernels for 28%

profile of v5, /device:TPU:0, one launch (start us, length us, event | category | flops | bytes accessed | tf_op | source)
XLA Modules:
  0.0 136.2 jit_solution(7167226345324906462)
XLA Ops:
  0.1 3.0 %collective-permute-start.7 = (bf16[3,512,128]{2,1,0:T(8,128)(2,1)}, bf16[3,512,128]{2,1,0:T(8,128)(2,1)S(1)}, u32[]{:S(2)}, u32[]{:S(2)}) collective-permute-start(bf16[3,512,128]{2,1,0:T(8,128)(2,1)} %refs_4_.1), channel_id=1, source_target_pairs={{0,2},{1,3},{2,0},{3,1},{4,6},{5,7},{6,4},{7,5},{8,10},{9,11},{10,... | collective-permute-start | bytes 1179656 | tf_op jit(solution)/shard_map/ppermute | solution.py:703
  3.8 6.3 %pack.1 = (bf16[1024,128]{1,0:T(8,128)(2,1)}, bf16[1024,128]{1,0:T(8,128)(2,1)}, bf16[1024,128]{1,0:T(8,128)(2,1)}, bf16[1024,128]{1,0:T(8,128)(2,1)}, s32[1,3072]{1,0:T(1,128)}) custom-call(s32[1]{0:T(128)S(6)} %copy.16.held, s32[1,3068]{1,0:T(1,128)} %bitcast.5, bf16[3068,512]{1,0:T(8,128)(2,1)} %z_feat.1), custom_call_target="tpu_custom_call" | custom-call | tf_op jit(solution)/shard_map/pack/pallas_call | solution.py:149
  10.1 1.6 %collective-permute-start = (bf16[1024,128]{1,0:T(8,128)(2,1)}, bf16[1024,128]{1,0:T(8,128)(2,1)S(1)}, u32[]{:S(2)}, u32[]{:S(2)}) collective-permute-start(bf16[1024,128]{1,0:T(8,128)(2,1)} %get-tuple-element.39), channel_id=1, source_target_pairs={{0,4},{4,8},{8,12},{12,0},{1,5},{5,9},{9,13},{13,1},{2,6},{6,10},{... | collective-permute-start | bytes 786440 | tf_op jit(solution)/shard_map/ppermute | solution.py:677
  11.7 2.6 %collective-permute-start.1 = (bf16[1024,128]{1,0:T(8,128)(2,1)}, bf16[1024,128]{1,0:T(8,128)(2,1)S(1)}, u32[]{:S(2)}, u32[]{:S(2)}) collective-permute-start(bf16[1024,128]{1,0:T(8,128)(2,1)} %get-tuple-element.40), channel_id=1, source_target_pairs={{0,8},{4,12},{8,0},{12,4},{1,9},{5,13},{9,1},{13,5},{2,10},{6,14},... | collective-permute-start | bytes 786440 | tf_op jit(solution)/shard_map/ppermute | solution.py:677
  14.3 1.3 collective-permute-start.2
  16.9 4.6 %collective-permute-done.refs_1_ = bf16[1024,128]{1,0:T(8,128)(2,1)S(1)} collective-permute-done((bf16[1024,128]{1,0:T(8,128)(2,1)}, bf16[1024,128]{1,0:T(8,128)(2,1)S(1)}, u32[]{:S(2)}, u32[]{:S(2)}) %collective-permute-start) | collective-permute-done | bytes 262176 | tf_op jit(solution)/shard_map/ppermute | solution.py:677
  21.5 10.8 %collective-permute-done.1.refs_2_ = bf16[1024,128]{1,0:T(8,128)(2,1)S(1)} collective-permute-done((bf16[1024,128]{1,0:T(8,128)(2,1)}, bf16[1024,128]{1,0:T(8,128)(2,1)S(1)}, u32[]{:S(2)}, u32[]{:S(2)}) %collective-permute-start.1) | collective-permute-done | bytes 262176 | tf_op jit(solution)/shard_map/ppermute | solution.py:677
  32.3 1.3 compact.1
  34.3 1.6 %collective-permute-start.13 = (bf16[512,512]{1,0:T(8,128)(2,1)S(1)}, bf16[512,512]{1,0:T(8,128)(2,1)S(1)}, u32[]{:S(2)}, u32[]{:S(2)}) collective-permute-start(bf16[512,512]{1,0:T(8,128)(2,1)S(1)} %copy-done), channel_id=1, source_target_pairs={{0,2},{1,3},{2,0},{3,1},{4,6},{5,7},{6,4},{7,5},{8,10},{9,11},{10,... | collective-permute-start | bytes 1572872 | tf_op jit(solution)/shard_map/ppermute | solution.py:703
  36.4 6.5 %collective-permute-done.4.refs_2_ = bf16[1024,128]{1,0:T(8,128)(2,1)S(1)} collective-permute-done((bf16[1024,128]{1,0:T(8,128)(2,1)S(1)}, bf16[1024,128]{1,0:T(8,128)(2,1)S(1)}, u32[]{:S(2)}, u32[]{:S(2)}) %collective-permute-start.4) | collective-permute-done | bytes 262176 | tf_op jit(solution)/shard_map/ppermute | solution.py:703
  45.9 2.9 %project.1 = (bf16[4,1024,128]{2,1,0:T(8,128)(2,1)S(1)}, bf16[4,128,1024]{2,1,0:T(8,128)(2,1)S(1)}, bf16[4,512,128]{2,1,0:T(8,128)(2,1)S(1)}, bf16[4,512,128]{2,1,0:T(8,128)(2,1)S(1)}, s32[1]{0:T(128)}) custom-call(f32[4,512]{1,0:T(4,128)S(1)} %pad_maximum_fusion.params, bf16[1024,128]{1,0:T(8,128)(2,1)S(1)} %get-tuple-element.42.refs_0_, ...), custom_call_target="tpu_custom_call" | custom-call | flops 1610612736 | bytes 4194304 | tf_op jit(solution)/shard_map/project/pallas_call | solution.py:450
  49.6 14.9 %collective-permute-done.19.refs_15_.refs_16_ = f32[1,768]{1,0:T(1,128)S(1)} collective-permute-done((f32[1,768]{1,0:T(1,128)S(1)}, f32[1,768]{1,0:T(1,128)S(1)}, u32[]{:S(2)}, u32[]{:S(2)}) %collective-permute-start.19) | collective-permute-done | bytes 3104 | tf_op jit(solution)/shard_map/ppermute | solution.py:775
  65.6 11.3 %attend.3.refs_0_ = bf16[4,128,256]{2,1,0:T(8,128)(2,1)S(1)} custom-call(s32[1]{0:T(128)} %get-tuple-element.45.small, bf16[4,1024,128]{2,1,0:T(8,128)(2,1)S(1)} %get-tuple-element.46.keys, bf16[4,128,1024]{2,1,0:T(8,128)(2,1)S(1)} %get-tuple-element.47.values, bf16[4,512,128]{2,1,0:T(8,128)(2,1)S(1)} %get-tuple-element.48.query), custom_call_target="tpu_custom_call" | custom-call | flops 4294967296 | bytes 2097152 | tf_op jit(solution)/shard_map/attend/pallas_call | solution.py:574
  77.2 6.2 %attend.5.refs_1_ = bf16[2,128,256]{2,1,0:T(8,128)(2,1)S(1)} custom-call(s32[1]{0:T(128)} %get-tuple-element.45.small, bf16[4,1024,128]{2,1,0:T(8,128)(2,1)S(1)} %get-tuple-element.46.keys, bf16[4,128,1024]{2,1,0:T(8,128)(2,1)S(1)} %get-tuple-element.47.values, bf16[4,512,128]{2,1,0:T(8,128)(2,1)S(1)} %get-tuple-element.48.query), custom_call_target="tpu_custom_call" | custom-call | flops 2147483648 | bytes 1048576 | tf_op jit(solution)/shard_map/attend/pallas_call | solution.py:574
  83.8 6.4 %attend.4.refs_0_ = bf16[2,128,256]{2,1,0:T(8,128)(2,1)S(1)} custom-call(s32[1]{0:T(128)} %get-tuple-element.45.small, bf16[4,1024,128]{2,1,0:T(8,128)(2,1)S(1)} %get-tuple-element.46.keys, bf16[4,128,1024]{2,1,0:T(8,128)(2,1)S(1)} %get-tuple-element.47.values, bf16[4,512,128]{2,1,0:T(8,128)(2,1)S(1)} %get-tuple-element.48.query), custom_call_target="tpu_custom_call" | custom-call | flops 2147483648 | bytes 1048576 | tf_op jit(solution)/shard_map/attend/pallas_call | solution.py:574
  90.3 2.4 %mlp.3 = (bf16[256,128]{1,0:T(8,128)(2,1)S(1)}, bf16[256,128]{1,0:T(8,128)(2,1)S(1)}, bf16[256,128]{1,0:T(8,128)(2,1)S(1)}, bf16[256,128]{1,0:T(8,128)(2,1)S(1)}) custom-call(f32[4,512]{1,0:T(4,128)S(1)} %pad_maximum_fusion.params, bf16[4,512,128]{2,1,0:T(8,128)(2,1)S(1)} %get-tuple-element.44.kept, bf16[2,128,256]{2,1,0:T(8,128)(2,1)S(1)} %attend.4.refs_0_, ...), custom_call_target="tpu_custom_call" | custom-call | flops 1073741824 | bytes 4194304 | tf_op jit(solution)/shard_map/mlp/pallas_call | solution.py:654
  92.8 1.5 %collective-permute-start.28 = (bf16[256,128]{1,0:T(8,128)(2,1)S(1)}, bf16[256,128]{1,0:T(8,128)(2,1)S(1)}, u32[]{:S(2)}, u32[]{:S(2)}) collective-permute-start(bf16[256,128]{1,0:T(8,128)(2,1)S(1)} %get-tuple-element.59), channel_id=1, source_target_pairs={{0,2},{1,3},{2,0},{3,1},{4,6},{5,7},{6,4},{7,5},{8,10},{9,11},{10,... | collective-permute-start | bytes 196616 | tf_op jit(solution)/shard_map/ppermute | solution.py:677
  94.3 1.4 collective-permute-start.29
  95.7 2.3 %mlp.2 = (bf16[256,128]{1,0:T(8,128)(2,1)S(1)}, bf16[256,128]{1,0:T(8,128)(2,1)S(1)}, bf16[256,128]{1,0:T(8,128)(2,1)S(1)}, bf16[256,128]{1,0:T(8,128)(2,1)S(1)}) custom-call(f32[4,512]{1,0:T(4,128)S(1)} %pad_maximum_fusion.params, bf16[4,512,128]{2,1,0:T(8,128)(2,1)S(1)} %get-tuple-element.44.kept, bf16[4,128,256]{2,1,0:T(8,128)(2,1)S(1)} %attend.3.refs_0_, ...), custom_call_target="tpu_custom_call" | custom-call | flops 1073741824 | bytes 4194304 | tf_op jit(solution)/shard_map/mlp/pallas_call | solution.py:654
  98.6 1.4 %collective-permute-start.23 = (bf16[256,128]{1,0:T(8,128)(2,1)S(1)}, bf16[256,128]{1,0:T(8,128)(2,1)S(1)}, u32[]{:S(2)}, u32[]{:S(2)}) collective-permute-start(bf16[256,128]{1,0:T(8,128)(2,1)S(1)} %get-tuple-element.52), channel_id=1, source_target_pairs={{0,3},{1,0},{2,1},{3,2},{4,7},{5,4},{6,5},{7,6},{8,11},{9,8},{10,9... | collective-permute-start | bytes 196616 | tf_op jit(solution)/shard_map/ppermute | solution.py:677
  100.0 1.8 %collective-permute-done.21.refs_1_ = bf16[256,128]{1,0:T(8,128)(2,1)S(1)} collective-permute-done((bf16[256,128]{1,0:T(8,128)(2,1)S(1)}, bf16[256,128]{1,0:T(8,128)(2,1)S(1)}, u32[]{:S(2)}, u32[]{:S(2)}) %collective-permute-start.21) | collective-permute-done | bytes 65568 | tf_op jit(solution)/shard_map/ppermute | solution.py:677
  101.8 1.3 collective-permute-done.22.refs_2_
  103.1 1.0 spread.3
  104.1 6.2 %collective-permute-start.30 = (bf16[512,128]{1,0:T(8,128)(2,1)S(1)}, bf16[512,128]{1,0:T(8,128)(2,1)S(1)}, u32[]{:S(2)}, u32[]{:S(2)}) collective-permute-start(bf16[512,128]{1,0:T(8,128)(2,1)S(1)} %get-tuple-element.62), channel_id=1, source_target_pairs={{0,4},{4,8},{8,12},{12,0},{1,5},{5,9},{9,13},{13,1},{2,6},{6,10},{... | collective-permute-start | bytes 393224 | tf_op jit(solution)/shard_map/ppermute | solution.py:677
  110.3 1.2 collective-permute-start.31
  111.5 1.3 collective-permute-start.32
  114.5 1.7 %collective-permute-start.25 = (bf16[512,128]{1,0:T(8,128)(2,1)S(1)}, bf16[512,128]{1,0:T(8,128)(2,1)S(1)}, u32[]{:S(2)}, u32[]{:S(2)}) collective-permute-start(bf16[512,128]{1,0:T(8,128)(2,1)S(1)} %get-tuple-element.55), channel_id=1, source_target_pairs={{0,8},{4,12},{8,0},{12,4},{1,9},{5,13},{9,1},{13,5},{2,10},{6,14},... | collective-permute-start | bytes 393224 | tf_op jit(solution)/shard_map/ppermute | solution.py:677
  116.3 1.3 collective-permute-start.26
  117.6 3.4 %collective-permute-done.31.refs_6_ = bf16[512,128]{1,0:T(8,128)(2,1)S(1)} collective-permute-done((bf16[512,128]{1,0:T(8,128)(2,1)S(1)}, bf16[512,128]{1,0:T(8,128)(2,1)S(1)}, u32[]{:S(2)}, u32[]{:S(2)}) %collective-permute-start.31) | collective-permute-done | bytes 131104 | tf_op jit(solution)/shard_map/ppermute | solution.py:677
  121.0 2.8 %collective-permute-done.24.refs_1_ = bf16[512,128]{1,0:T(8,128)(2,1)S(1)} collective-permute-done((bf16[512,128]{1,0:T(8,128)(2,1)S(1)}, bf16[512,128]{1,0:T(8,128)(2,1)S(1)}, u32[]{:S(2)}, u32[]{:S(2)}) %collective-permute-start.24) | collective-permute-done | bytes 131104 | tf_op jit(solution)/shard_map/ppermute | solution.py:677
  123.9 8.3 %collective-permute-done.25.refs_2_ = bf16[512,128]{1,0:T(8,128)(2,1)S(1)} collective-permute-done((bf16[512,128]{1,0:T(8,128)(2,1)S(1)}, bf16[512,128]{1,0:T(8,128)(2,1)S(1)}, u32[]{:S(2)}, u32[]{:S(2)}) %collective-permute-start.25) | collective-permute-done | bytes 131104 | tf_op jit(solution)/shard_map/ppermute | solution.py:677
  132.1 4.0 %unpack.1 = bf16[3068,128]{1,0:T(8,128)(2,1)} custom-call(s32[1]{0:T(128)S(6)} %copy.16.held, s32[1,3072]{1,0:T(1,128)S(1)} %copy-done.4, bf16[512,128]{1,0:T(8,128)(2,1)S(1)} %get-tuple-element.53.refs_0_, bf16[512,128]{1,0:T(8,128)(2,1)S(1)} %collective-permute-done.24.refs_1_, bf16[512,128]{1,0:T(8,128)(2,1)S(1)} %collective-permute-done.25.refs_2_, ...), custom_call_target="tpu_custom_call" | custom-call | tf_op jit(solution)/shard_map/unpack/pallas_call | solution.py:341
  (80 shorter events, 10.5 us)
Async XLA Ops:
  0.1 34.2 %collective-permute-start.7 = (bf16[3,512,128]{2,1,0:T(8,128)(2,1)}, bf16[3,512,128]{2,1,0:T(8,128)(2,1)S(1)}, u32[]{:S(2)}, u32[]{:S(2)}) collective-permute-start(bf16[3,512,128]{2,1,0:T(8,128)(2,1)} %refs_4_.1), channel_id=1, source_target_pairs={{0,2},{1,3},{2,0},{3,1},{4,6},{5,7},{6,4},{7,5},{8,10},{9,11},{10,... | collective-permute-start | bytes 1179656 | tf_op jit(solution)/shard_map/ppermute | solution.py:703
  3.1 33.3 %collective-permute-start.6 = (bf16[3,512,128]{2,1,0:T(8,128)(2,1)}, bf16[3,512,128]{2,1,0:T(8,128)(2,1)S(1)}, u32[]{:S(2)}, u32[]{:S(2)}) collective-permute-start(bf16[3,512,128]{2,1,0:T(8,128)(2,1)} %refs_4_.1), channel_id=1, source_target_pairs={{0,1},{1,0},{2,3},{3,2},{4,5},{5,4},{6,7},{7,6},{8,9},{9,8},{10,11... | collective-permute-start | bytes 1179656 | tf_op jit(solution)/shard_map/ppermute | solution.py:709
  10.1 11.4 %collective-permute-start = (bf16[1024,128]{1,0:T(8,128)(2,1)}, bf16[1024,128]{1,0:T(8,128)(2,1)S(1)}, u32[]{:S(2)}, u32[]{:S(2)}) collective-permute-start(bf16[1024,128]{1,0:T(8,128)(2,1)} %get-tuple-element.39), channel_id=1, source_target_pairs={{0,4},{4,8},{8,12},{12,0},{1,5},{5,9},{9,13},{13,1},{2,6},{6,10},{... | collective-permute-start | bytes 786440 | tf_op jit(solution)/shard_map/ppermute | solution.py:677
  11.7 20.6 %collective-permute-start.1 = (bf16[1024,128]{1,0:T(8,128)(2,1)}, bf16[1024,128]{1,0:T(8,128)(2,1)S(1)}, u32[]{:S(2)}, u32[]{:S(2)}) collective-permute-start(bf16[1024,128]{1,0:T(8,128)(2,1)} %get-tuple-element.40), channel_id=1, source_target_pairs={{0,8},{4,12},{8,0},{12,4},{1,9},{5,13},{9,1},{13,5},{2,10},{6,14},... | collective-permute-start | bytes 786440 | tf_op jit(solution)/shard_map/ppermute | solution.py:677
  14.3 18.0 %collective-permute-start.2 = (bf16[1024,128]{1,0:T(8,128)(2,1)}, bf16[1024,128]{1,0:T(8,128)(2,1)S(1)}, u32[]{:S(2)}, u32[]{:S(2)}) collective-permute-start(bf16[1024,128]{1,0:T(8,128)(2,1)} %get-tuple-element.41), channel_id=1, source_target_pairs={{0,12},{4,0},{8,4},{12,8},{1,13},{5,1},{9,5},{13,9},{2,14},{6,2},{... | collective-permute-start | bytes 786440 | tf_op jit(solution)/shard_map/ppermute | solution.py:677
  33.7 9.2 %collective-permute-start.4 = (bf16[1024,128]{1,0:T(8,128)(2,1)S(1)}, bf16[1024,128]{1,0:T(8,128)(2,1)S(1)}, u32[]{:S(2)}, u32[]{:S(2)}) collective-permute-start(bf16[1024,128]{1,0:T(8,128)(2,1)S(1)} %get-tuple-element.43), channel_id=1, source_target_pairs={{0,2},{1,3},{2,0},{3,1},{4,6},{5,7},{6,4},{7,5},{8,10},{9,11},{10,... | collective-permute-start | bytes 786440 | tf_op jit(solution)/shard_map/ppermute | solution.py:703
  34.3 10.7 %collective-permute-start.8 = (bf16[3,512,128]{2,1,0:T(8,128)(2,1)S(1)}, bf16[3,512,128]{2,1,0:T(8,128)(2,1)S(1)}, u32[]{:S(2)}, u32[]{:S(2)}) collective-permute-start(bf16[3,512,128]{2,1,0:T(8,128)(2,1)S(1)} %collective-permute-done.7.refs_6_), channel_id=1, source_target_pairs={{0,1},{1,0},{2,3},{3,2},{4,5},{5,4},{6,7},{7,6},{8,9},{9,8},{10,11... | collective-permute-start | bytes 1179656 | tf_op jit(solution)/shard_map/ppermute | solution.py:709
  34.3 30.8 %collective-permute-start.13 = (bf16[512,512]{1,0:T(8,128)(2,1)S(1)}, bf16[512,512]{1,0:T(8,128)(2,1)S(1)}, u32[]{:S(2)}, u32[]{:S(2)}) collective-permute-start(bf16[512,512]{1,0:T(8,128)(2,1)S(1)} %copy-done), channel_id=1, source_target_pairs={{0,2},{1,3},{2,0},{3,1},{4,6},{5,7},{6,4},{7,5},{8,10},{9,11},{10,... | collective-permute-start | bytes 1572872 | tf_op jit(solution)/shard_map/ppermute | solution.py:703
  35.8 29.4 %collective-permute-start.16 = (bf16[512,512]{1,0:T(8,128)(2,1)S(1)}, bf16[512,512]{1,0:T(8,128)(2,1)S(1)}, u32[]{:S(2)}, u32[]{:S(2)}) collective-permute-start(bf16[512,512]{1,0:T(8,128)(2,1)S(1)} %copy-done.1), channel_id=1, source_target_pairs={{0,2},{1,3},{2,0},{3,1},{4,6},{5,7},{6,4},{7,5},{8,10},{9,11},{10,... | collective-permute-start | bytes 1572872 | tf_op jit(solution)/shard_map/ppermute | solution.py:703
  36.4 6.6 %collective-permute-start.3 = (bf16[1024,128]{1,0:T(8,128)(2,1)S(1)}, bf16[1024,128]{1,0:T(8,128)(2,1)S(1)}, u32[]{:S(2)}, u32[]{:S(2)}) collective-permute-start(bf16[1024,128]{1,0:T(8,128)(2,1)S(1)} %get-tuple-element.42.refs_0_), channel_id=1, source_target_pairs={{0,1},{1,0},{2,3},{3,2},{4,5},{5,4},{6,7},{7,6},{8,9},{9,8},{10,11... | collective-permute-start | bytes 786440 | tf_op jit(solution)/shard_map/ppermute | solution.py:709
  43.0 5.9 %collective-permute-start.18 = (f32[1,768]{1,0:T(1,128)S(1)}, f32[1,768]{1,0:T(1,128)S(1)}, u32[]{:S(2)}, u32[]{:S(2)}) collective-permute-start(f32[1,768]{1,0:T(1,128)S(1)} %broadcast_in_dim.8.refs_13_.refs_14_), channel_id=1, source_target_pairs={{0,1},{1,0},{2,3},{3,2},{4,5},{5,4},{6,7},{7,6},{8,9},{9,8},{10,11... | collective-permute-start | bytes 9224 | tf_op jit(solution)/shard_map/ppermute | solution.py:775
  44.4 20.0 %collective-permute-start.19 = (f32[1,768]{1,0:T(1,128)S(1)}, f32[1,768]{1,0:T(1,128)S(1)}, u32[]{:S(2)}, u32[]{:S(2)}) collective-permute-start(f32[1,768]{1,0:T(1,128)S(1)} %broadcast_in_dim.8.refs_13_.refs_14_), channel_id=1, source_target_pairs={{0,2},{1,3},{2,0},{3,1},{4,6},{5,7},{6,4},{7,5},{8,10},{9,11},{10,... | collective-permute-start | bytes 9224 | tf_op jit(solution)/shard_map/ppermute | solution.py:775
  45.0 19.5 %collective-permute-start.20 = (f32[1,768]{1,0:T(1,128)S(1)}, f32[1,768]{1,0:T(1,128)S(1)}, u32[]{:S(2)}, u32[]{:S(2)}) collective-permute-start(f32[1,768]{1,0:T(1,128)S(1)} %broadcast_in_dim.8.refs_13_.refs_14_), channel_id=1, source_target_pairs={{0,3},{1,2},{2,1},{3,0},{4,7},{5,6},{6,5},{7,4},{8,11},{9,10},{10,... | collective-permute-start | bytes 9224 | tf_op jit(solution)/shard_map/ppermute | solution.py:775
  48.9 41.4 %collective-permute-start.12 = (bf16[512,512]{1,0:T(8,128)(2,1)S(1)}, bf16[512,512]{1,0:T(8,128)(2,1)S(1)}, u32[]{:S(2)}, u32[]{:S(2)}) collective-permute-start(bf16[512,512]{1,0:T(8,128)(2,1)S(1)} %copy-done), channel_id=1, source_target_pairs={{0,1},{1,0},{2,3},{3,2},{4,5},{5,4},{6,7},{7,6},{8,9},{9,8},{10,11... | collective-permute-start | bytes 1572872 | tf_op jit(solution)/shard_map/ppermute | solution.py:709
  64.5 25.7 %collective-permute-start.15 = (bf16[512,512]{1,0:T(8,128)(2,1)S(1)}, bf16[512,512]{1,0:T(8,128)(2,1)S(1)}, u32[]{:S(2)}, u32[]{:S(2)}) collective-permute-start(bf16[512,512]{1,0:T(8,128)(2,1)S(1)} %copy-done.1), channel_id=1, source_target_pairs={{0,1},{1,0},{2,3},{3,2},{4,5},{5,4},{6,7},{7,6},{8,9},{9,8},{10,11... | collective-permute-start | bytes 1572872 | tf_op jit(solution)/shard_map/ppermute | solution.py:709
  64.5 12.4 %collective-permute-start.10 = (bf16[512,128]{1,0:T(8,128)(2,1)S(1)}, bf16[512,128]{1,0:T(8,128)(2,1)S(1)}, u32[]{:S(2)}, u32[]{:S(2)}) collective-permute-start(bf16[512,128]{1,0:T(8,128)(2,1)S(1)} %copy-done.2), channel_id=1, source_target_pairs={{0,2},{1,3},{2,0},{3,1},{4,6},{5,7},{6,4},{7,5},{8,10},{9,11},{10,... | collective-permute-start | bytes 393224 | tf_op jit(solution)/shard_map/ppermute | solution.py:703
  65.1 25.1 %collective-permute-start.14 = (bf16[512,512]{1,0:T(8,128)(2,1)S(1)}, bf16[512,512]{1,0:T(8,128)(2,1)S(1)}, u32[]{:S(2)}, u32[]{:S(2)}) collective-permute-start(bf16[512,512]{1,0:T(8,128)(2,1)S(1)} %collective-permute-done.13.refs_7_.refs_8_), channel_id=1, source_target_pairs={{0,1},{1,0},{2,3},{3,2},{4,5},{5,4},{6,7},{7,6},{8,9},{9,8},{10,11... | collective-permute-start | bytes 1572872 | tf_op jit(solution)/shard_map/ppermute | solution.py:709
  65.3 25.0 %collective-permute-start.17 = (bf16[512,512]{1,0:T(8,128)(2,1)S(1)}, bf16[512,512]{1,0:T(8,128)(2,1)S(1)}, u32[]{:S(2)}, u32[]{:S(2)}) collective-permute-start(bf16[512,512]{1,0:T(8,128)(2,1)S(1)} %collective-permute-done.16.refs_11_.refs_12_), channel_id=1, source_target_pairs={{0,1},{1,0},{2,3},{3,2},{4,5},{5,4},{6,7},{7,6},{8,9},{9,8},{10,11... | collective-permute-start | bytes 1572872 | tf_op jit(solution)/shard_map/ppermute | solution.py:709
  76.9 6.4 %collective-permute-start.9 = (bf16[512,128]{1,0:T(8,128)(2,1)S(1)}, bf16[512,128]{1,0:T(8,128)(2,1)S(1)}, u32[]{:S(2)}, u32[]{:S(2)}) collective-permute-start(bf16[512,128]{1,0:T(8,128)(2,1)S(1)} %copy-done.2), channel_id=1, source_target_pairs={{0,1},{1,0},{2,3},{3,2},{4,5},{5,4},{6,7},{7,6},{8,9},{9,8},{10,11... | collective-permute-start | bytes 393224 | tf_op jit(solution)/shard_map/ppermute | solution.py:709
  83.4 6.8 %collective-permute-start.11 = (bf16[512,128]{1,0:T(8,128)(2,1)S(1)}, bf16[512,128]{1,0:T(8,128)(2,1)S(1)}, u32[]{:S(2)}, u32[]{:S(2)}) collective-permute-start(bf16[512,128]{1,0:T(8,128)(2,1)S(1)} %collective-permute-done.10.refs_3_.refs_4_), channel_id=1, source_target_pairs={{0,1},{1,0},{2,3},{3,2},{4,5},{5,4},{6,7},{7,6},{8,9},{9,8},{10,11... | collective-permute-start | bytes 393224 | tf_op jit(solution)/shard_map/ppermute | solution.py:709
  92.6 6.0 %collective-permute-start.27 = (bf16[256,128]{1,0:T(8,128)(2,1)S(1)}, bf16[256,128]{1,0:T(8,128)(2,1)S(1)}, u32[]{:S(2)}, u32[]{:S(2)}) collective-permute-start(bf16[256,128]{1,0:T(8,128)(2,1)S(1)} %get-tuple-element.58), channel_id=1, source_target_pairs={{0,1},{1,2},{2,3},{3,0},{4,5},{5,6},{6,7},{7,4},{8,9},{9,10},{10,1... | collective-permute-start | bytes 196616 | tf_op jit(solution)/shard_map/ppermute | solution.py:677
  92.8 7.2 %collective-permute-start.28 = (bf16[256,128]{1,0:T(8,128)(2,1)S(1)}, bf16[256,128]{1,0:T(8,128)(2,1)S(1)}, u32[]{:S(2)}, u32[]{:S(2)}) collective-permute-start(bf16[256,128]{1,0:T(8,128)(2,1)S(1)} %get-tuple-element.59), channel_id=1, source_target_pairs={{0,2},{1,3},{2,0},{3,1},{4,6},{5,7},{6,4},{7,5},{8,10},{9,11},{10,... | collective-permute-start | bytes 196616 | tf_op jit(solution)/shard_map/ppermute | solution.py:677
  94.3 5.7 %collective-permute-start.29 = (bf16[256,128]{1,0:T(8,128)(2,1)S(1)}, bf16[256,128]{1,0:T(8,128)(2,1)S(1)}, u32[]{:S(2)}, u32[]{:S(2)}) collective-permute-start(bf16[256,128]{1,0:T(8,128)(2,1)S(1)} %get-tuple-element.60), channel_id=1, source_target_pairs={{0,3},{1,0},{2,1},{3,2},{4,7},{5,4},{6,5},{7,6},{8,11},{9,8},{10,9... | collective-permute-start | bytes 196616 | tf_op jit(solution)/shard_map/ppermute | solution.py:677
  98.0 3.8 %collective-permute-start.21 = (bf16[256,128]{1,0:T(8,128)(2,1)S(1)}, bf16[256,128]{1,0:T(8,128)(2,1)S(1)}, u32[]{:S(2)}, u32[]{:S(2)}) collective-permute-start(bf16[256,128]{1,0:T(8,128)(2,1)S(1)} %get-tuple-element.50), channel_id=1, source_target_pairs={{0,1},{1,2},{2,3},{3,0},{4,5},{5,6},{6,7},{7,4},{8,9},{9,10},{10,1... | collective-permute-start | bytes 196616 | tf_op jit(solution)/shard_map/ppermute | solution.py:677
  98.1 5.0 %collective-permute-start.22 = (bf16[256,128]{1,0:T(8,128)(2,1)S(1)}, bf16[256,128]{1,0:T(8,128)(2,1)S(1)}, u32[]{:S(2)}, u32[]{:S(2)}) collective-permute-start(bf16[256,128]{1,0:T(8,128)(2,1)S(1)} %get-tuple-element.51), channel_id=1, source_target_pairs={{0,2},{1,3},{2,0},{3,1},{4,6},{5,7},{6,4},{7,5},{8,10},{9,11},{10,... | collective-permute-start | bytes 196616 | tf_op jit(solution)/shard_map/ppermute | solution.py:677
  98.6 4.5 %collective-permute-start.23 = (bf16[256,128]{1,0:T(8,128)(2,1)S(1)}, bf16[256,128]{1,0:T(8,128)(2,1)S(1)}, u32[]{:S(2)}, u32[]{:S(2)}) collective-permute-start(bf16[256,128]{1,0:T(8,128)(2,1)S(1)} %get-tuple-element.52), channel_id=1, source_target_pairs={{0,3},{1,0},{2,1},{3,2},{4,7},{5,4},{6,5},{7,6},{8,11},{9,8},{10,9... | collective-permute-start | bytes 196616 | tf_op jit(solution)/shard_map/ppermute | solution.py:677
  104.1 12.1 %collective-permute-start.30 = (bf16[512,128]{1,0:T(8,128)(2,1)S(1)}, bf16[512,128]{1,0:T(8,128)(2,1)S(1)}, u32[]{:S(2)}, u32[]{:S(2)}) collective-permute-start(bf16[512,128]{1,0:T(8,128)(2,1)S(1)} %get-tuple-element.62), channel_id=1, source_target_pairs={{0,4},{4,8},{8,12},{12,0},{1,5},{5,9},{9,13},{13,1},{2,6},{6,10},{... | collective-permute-start | bytes 393224 | tf_op jit(solution)/shard_map/ppermute | solution.py:677
  110.3 10.7 %collective-permute-start.31 = (bf16[512,128]{1,0:T(8,128)(2,1)S(1)}, bf16[512,128]{1,0:T(8,128)(2,1)S(1)}, u32[]{:S(2)}, u32[]{:S(2)}) collective-permute-start(bf16[512,128]{1,0:T(8,128)(2,1)S(1)} %get-tuple-element.63), channel_id=1, source_target_pairs={{0,8},{4,12},{8,0},{12,4},{1,9},{5,13},{9,1},{13,5},{2,10},{6,14},... | collective-permute-start | bytes 393224 | tf_op jit(solution)/shard_map/ppermute | solution.py:677
  111.5 9.5 %collective-permute-start.32 = (bf16[512,128]{1,0:T(8,128)(2,1)S(1)}, bf16[512,128]{1,0:T(8,128)(2,1)S(1)}, u32[]{:S(2)}, u32[]{:S(2)}) collective-permute-start(bf16[512,128]{1,0:T(8,128)(2,1)S(1)} %get-tuple-element.64), channel_id=1, source_target_pairs={{0,12},{4,0},{8,4},{12,8},{1,13},{5,1},{9,5},{13,9},{2,14},{6,2},{... | collective-permute-start | bytes 393224 | tf_op jit(solution)/shard_map/ppermute | solution.py:677
  113.7 10.1 %collective-permute-start.24 = (bf16[512,128]{1,0:T(8,128)(2,1)S(1)}, bf16[512,128]{1,0:T(8,128)(2,1)S(1)}, u32[]{:S(2)}, u32[]{:S(2)}) collective-permute-start(bf16[512,128]{1,0:T(8,128)(2,1)S(1)} %get-tuple-element.54), channel_id=1, source_target_pairs={{0,4},{4,8},{8,12},{12,0},{1,5},{5,9},{9,13},{13,1},{2,6},{6,10},{... | collective-permute-start | bytes 393224 | tf_op jit(solution)/shard_map/ppermute | solution.py:677
  114.5 17.6 %collective-permute-start.25 = (bf16[512,128]{1,0:T(8,128)(2,1)S(1)}, bf16[512,128]{1,0:T(8,128)(2,1)S(1)}, u32[]{:S(2)}, u32[]{:S(2)}) collective-permute-start(bf16[512,128]{1,0:T(8,128)(2,1)S(1)} %get-tuple-element.55), channel_id=1, source_target_pairs={{0,8},{4,12},{8,0},{12,4},{1,9},{5,13},{9,1},{13,5},{2,10},{6,14},... | collective-permute-start | bytes 393224 | tf_op jit(solution)/shard_map/ppermute | solution.py:677
  116.3 15.9 %collective-permute-start.26 = (bf16[512,128]{1,0:T(8,128)(2,1)S(1)}, bf16[512,128]{1,0:T(8,128)(2,1)S(1)}, u32[]{:S(2)}, u32[]{:S(2)}) collective-permute-start(bf16[512,128]{1,0:T(8,128)(2,1)S(1)} %get-tuple-element.56), channel_id=1, source_target_pairs={{0,12},{4,0},{8,4},{12,8},{1,13},{5,1},{9,5},{13,9},{2,14},{6,2},{... | collective-permute-start | bytes 393224 | tf_op jit(solution)/shard_map/ppermute | solution.py:677
  (15 other events, 394.3 us)
